TPU v7x, 32 devices: a whole 2x2x4 slice. The times are simulated.
32 devices in a mesh: px: 8 (over z, y), py: 4 (over x, core).
Axes of the slice: x: 2, y: 2, z: 4, core: 2. Of those that a mesh axis runs over, the one named last changes fastest.
Arguments:
- right_side: float32 [4, 5, 5, 5, 16, 8, 128], P(None, None, None, None, 'px', 'py'), may hold values from -6 to 6
- first_guess: float32 [4, 5, 5, 5, 16, 8, 128], P(None, None, None, None, 'px', 'py'), may hold values from -6 to 6
- coefficient: float32 [16, 8, 128], P('px', 'py'), may hold values from 0.2 to 2
- modal_basis: float32 [5, 5], replicated, may hold values from -1 to 1, as said below
- modal_values: float32 [5], replicated, may hold values from 0.5 to 4
- patch_inverse: float32 [256, 256], replicated, may hold values from -0.018 to 0.018
- patch_elements: int32 [16384, 8], P(('px', 'py')), may hold values from 0 to 16383, as said below
- patch_mask: int32 [16384, 8], P(('px', 'py')), may hold values from 0 to 1, as said below
Outputs:
- solution: float32 [4, 5, 5, 5, 16, 8, 128], P(None, None, None, None, 'px', 'py')
Inputs may be any that keep to these rules, and one draw needn't show every extreme that they name: `modal_basis`: an orthogonal matrix. `patch_elements`: element number e = (x 8 + y) * 128 + z. Row r belongs to block b = r // 512 with bx = b // 4 and by = b % 4; every slot of the row, live or padded, names an element with bx * 2 - 1 <= x <= bx * 2 + 2 and by * 2 - 1 <= y <= by * 2 + 2. The live slots of a row name distinct elements that share one mesh vertex. `patch_mask`: padded slots belong to patches of vertices on the boundary of the grid.
All inputs are finite; a program needn't handle non-finite values.
Results may differ from a plain program's by a relative error of at most 0.0001.
Values sent between devices are 32-bit elements; how exact they have to be, the bound alone decides.
No kernel may reach another device: no remote copies, remote signals or barrier semaphores. Data moves between devices by JAX's collectives and lax.ppermute only.
A program may use at most 64 MiB of HBM per device.

v0:
```python
import functools
import math

import jax
import jax.numpy as jnp
from jax import lax
from jax.experimental import pallas as pl
from jax.experimental.pallas import tpu as pltpu
from jax.sharding import PartitionSpec as P

MASS_SHIFT = 1.0
FACE_PENALTY = 0.5
DAMPING = 0.8
KEPT = 1.0 - DAMPING
ROOT = math.sqrt(3.0 / 7.0)
POINTS = (-1.0, -ROOT, 0.0, ROOT, 1.0)
TABLE = tuple(((1.0 - t) / 2.0, (1.0 + t) / 2.0) for t in POINTS)
NODES = len(POINTS)
FACE = NODES * NODES
CUBE = NODES * NODES * NODES
TOP = NODES - 1
SUB, LANES = 8, 128
F32 = jnp.float32


def node(i, j, k):
    return (i * NODES + j) * NODES + k


def sublane_bits():
    sub = lax.broadcasted_iota(jnp.int32, (SUB, LANES), 0)
    return (sub & 2) == 0, (sub & 1) == 0


def lane_ids():
    return lax.broadcasted_iota(jnp.int32, (SUB, LANES), 1)


def down(v, by):
    return pltpu.roll(v, SUB - by, 0)


def up(v, by):
    return pltpu.roll(v, by, 0)


def combine(weights, values):
    total = None
    for w, v in zip(weights, values):
        if isinstance(w, float) and w == 0.0:
            continue
        term = v if isinstance(w, float) and w == 1.0 else v * w
        total = term if total is None else total + term
    return total


def column(c):
    return [TABLE[i][c] for i in range(NODES)]


def restrict_face(vals):
    rows = [[combine(column(c), vals[j * NODES : (j + 1) * NODES]) for c in (0, 1)] for j in range(NODES)]
    return [combine(column(b), [rows[j][c] for j in range(NODES)]) for b in (0, 1) for c in (0, 1)]


def prolong_face(coarse):
    half = [[combine(TABLE[j], [coarse[c], coarse[2 + c]]) for c in (0, 1)] for j in range(NODES)]
    return [combine(TABLE[k], half[j]) for j in range(NODES) for k in range(NODES)]


def is_even(idx_ref, which):
    return (jnp.full((SUB, LANES), idx_ref[which], jnp.int32) & 1) == 0


def pack_lo(first, v0, v1, by):
    return jnp.where(first, v0, up(v1, by))


def pack_hi(first, v0, v1, by):
    return jnp.where(first, down(v0, by), v1)


def outer_pair(first, plus, minus, by):
    return (
        jnp.where(first, minus, up(plus, by)),
        jnp.where(first, down(minus, by), plus),
    )


def couple(u, i, j, k, ex=None, ey=None):
    even_x, even_y = sublane_bits()
    lane = lane_ids()
    terms = []
    if i == TOP:
        terms.append(jnp.where(even_x, down(u(node(0, j, k)), 2), 0.0 if ex is None else ex(j * NODES + k)))
    if i == 0:
        terms.append(jnp.where(even_x, 0.0 if ex is None else ex(j * NODES + k), up(u(node(TOP, j, k)), 2)))
    if j == TOP:
        terms.append(jnp.where(even_y, down(u(node(i, 0, k)), 1), 0.0 if ey is None else ey(i * NODES + k)))
    if j == 0:
        terms.append(jnp.where(even_y, 0.0 if ey is None else ey(i * NODES + k), up(u(node(i, TOP, k)), 1)))
    if k == TOP:
        terms.append(jnp.where(lane < LANES - 1, pltpu.roll(u(node(i, j, 0)), LANES - 1, 1), 0.0))
    if k == 0:
        terms.append(jnp.where(lane > 0, pltpu.roll(u(node(i, j, TOP)), 1, 1), 0.0))
    return combine([1.0] * len(terms), terms) if terms else None


def smooth(load_plane, finish, basis, invd, work):
    fwd = [[basis[i, a] for i in range(NODES)] for a in range(NODES)]
    bwd = [[basis[i, a] for a in range(NODES)] for i in range(NODES)]

    def plane(vals, mats):
        mid = [[combine(m, vals[j * NODES : (j + 1) * NODES]) for m in mats] for j in range(NODES)]
        return [[combine(m, [mid[j][c] for j in range(NODES)]) for c in range(NODES)] for m in mats]

    for i in range(NODES):
        out = plane(load_plane(i), fwd)
        for b in range(NODES):
            for c in range(NODES):
                work[node(i, b, c)] = out[b][c]
    for b in range(NODES):
        for c in range(NODES):
            vals = [work[node(i, b, c)] for i in range(NODES)]
            modal = [combine(fwd[a], vals) * invd[order_of(a, b, c)] for a in range(NODES)]
            for i in range(NODES):
                work[node(i, b, c)] = combine(bwd[i], modal)
    for i in range(NODES):
        out = plane([work[node(i, 0, 0) + n] for n in range(FACE)], bwd)
        finish(i, [out[j][k] for j in range(NODES) for k in range(NODES)])


TRIPLES = [(a, b, c) for a in range(NODES) for b in range(a, NODES) for c in range(b, NODES)]


def order_of(a, b, c):
    return TRIPLES.index(tuple(sorted((a, b, c))))


def x_face(u, side):
    return [u(node(side, j, k)) for j in range(NODES) for k in range(NODES)]


def y_face(u, side):
    return [u(node(i, side, k)) for i in range(NODES) for k in range(NODES)]


def z_face(u, side):
    return [u(node(i, j, side)) for i in range(NODES) for j in range(NODES)]


def inner_restricted(rx, ry, rz, ex, ey):
    even_x, even_y = sublane_bits()
    lane = lane_ids()
    out = []
    for a in (0, 1):
        for b in (0, 1):
            for c in (0, 1):
                n = b * 2 + c
                xo = 0.0 if ex is None else ex[n]
                tx = jnp.where(even_x, down(rx[0][n], 2), xo) if a else jnp.where(even_x, xo, up(rx[1][n], 2))
                n = a * 2 + c
                yo = 0.0 if ey is None else ey[n]
                ty = jnp.where(even_y, down(ry[0][n], 1), yo) if b else jnp.where(even_y, yo, up(ry[1][n], 1))
                n = a * 2 + b
                if c:
                    tz = jnp.where(lane < LANES - 1, pltpu.roll(rz[0][n], LANES - 1, 1), 0.0)
                else:
                    tz = jnp.where(lane > 0, pltpu.roll(rz[1][n], 1, 1), 0.0)
                out.append(tx + ty + tz)
    return out


def swap_store(even, lo, hi, out0, out1, at):
    out0[at] = jnp.where(even, hi, lo)
    out1[at] = jnp.where(even, lo, hi)


def take_in(hbm, vmem, sems):
    copies = []
    for f in range(hbm.shape[0]):
        half = SUB // 2
        dst = vmem.at[f // 2, :, pl.ds(half * (f % 2), half), :]
        copies.append(pltpu.make_async_copy(hbm.at[f], dst, sems.at[f]))
    for c in copies:
        c.start()
    return copies


def faces_kernel(idx, u_hbm, u, mx0, mx1, my0, my1, sems):
    for c in take_in(u_hbm, u, sems):
        c.wait()
    even_x, even_y = sublane_bits()
    par_x, par_y = is_even(idx, 0), is_even(idx, 1)
    for p in range(NODES):
        for q in range(NODES):
            n = p * NODES + q
            lo, hi = node(0, p, q), node(TOP, p, q)
            swap_store(
                par_x,
                pack_lo(even_x, u[0, lo], u[1, lo], 2),
                pack_hi(even_x, u[0, hi], u[1, hi], 2),
                mx0, mx1, n,
            )
            lo, hi = node(p, 0, q), node(p, TOP, q)
            swap_store(
                par_y,
                pack_lo(even_y, u[0, lo], u[1, lo], 1),
                pack_hi(even_y, u[0, hi], u[1, hi], 1),
                my0, my1, n,
            )


def local_kernel(basis, lam, u, coef, rhs_hbm, rhs, w, crd, invd, sems):
    copies = take_in(rhs_hbm, rhs, sems)
    scale = coef[...]
    for t, (a, b, c) in enumerate(TRIPLES):
        invd[t] = 1.0 / (scale * (lam[a] + lam[b] + lam[c]) + MASS_SHIFT)
    wide = []
    for c in (0, 1):
        modal = [
            lam[m] * combine([1.0] * NODES, [basis[i, m] * TABLE[i][c] for i in range(NODES)])
            for m in range(NODES)
        ]
        wide.append([combine([1.0] * NODES, [basis[i, m] * modal[m] for m in range(NODES)]) for i in range(NODES)])
    for cp in copies:
        cp.wait()

    def pair(g, carry):
        def val(n):
            return u[g, n]

        plain, stiff = [], []
        for i in range(NODES):
            t, s, r = [], [], []
            for j in range(NODES):
                here = [u[g, node(i, j, k)] for k in range(NODES)]
                right = [rhs[g, node(i, j, k)] for k in range(NODES)]
                for k in range(NODES):
                    extra = couple(val, i, j, k)
                    w[g, node(i, j, k)] = right[k] if extra is None else right[k] + FACE_PENALTY * extra
                t.append([combine(column(c), here) for c in (0, 1)])
                s.append([combine(wide[c], here) for c in (0, 1)])
                r.append([combine(column(c), [x - y for x, y in zip(right, here)]) for c in (0, 1)])
            both, one, rest = [], [], []
            for b in (0, 1):
                for c in (0, 1):
                    tc = [t[j][c] for j in range(NODES)]
                    one.append(combine(column(b), tc))
                    both.append(combine(wide[b], tc) + combine(column(b), [s[j][c] for j in range(NODES)]))
                    rest.append(combine(column(b), [r[j][c] for j in range(NODES)]))
            plain.append(rest)
            stiff.append((one, both))
        rx = [restrict_face(x_face(val, s)) for s in (0, TOP)]
        ry = [restrict_face(y_face(val, s)) for s in (0, TOP)]
        rz = [restrict_face(z_face(val, s)) for s in (0, TOP)]
        inner = inner_restricted(rx, ry, rz, None, None)
        for a in (0, 1):
            for n in range(4):
                k_part = combine(wide[a], [stiff[i][0][n] for i in range(NODES)])
                k_part = k_part + combine(column(a), [stiff[i][1][n] for i in range(NODES)])
                r_part = combine(column(a), [plain[i][n] for i in range(NODES)])
                crd[g, a * 4 + n] = KEPT * (r_part - scale * k_part) - DAMPING * FACE_PENALTY * inner[a * 4 + n]
        return carry

    lax.fori_loop(0, 2, pair, 0)


def combine_outer(idx, which, first, r0, r1, rows, base, by, out):
    even = is_even(idx, which)
    for n in range(rows):
        a, b = r0[base + n], r1[base + n]
        plus, minus = jnp.where(even, a, b), jnp.where(even, b, a)
        out[0, n], out[1, n] = outer_pair(first, plus, minus, by)


def first_kernel(idx, basis, fx0, fx1, fy0, fy1, u, w, crd, invd, u1, c0, xpk, yf, yface, mx0, mx1, ex, ey, work):
    even_x, even_y = sublane_bits()
    combine_outer(idx, 0, even_x, fx0, fx1, FACE, 0, 2, ex)
    combine_outer(idx, 1, even_y, fy0, fy1, FACE, 0, 1, ey)

    def pair(g, carry):
        def load(i):
            vals = []
            for j in range(NODES):
                for k in range(NODES):
                    v = w[g, node(i, j, k)]
                    if i == TOP:
                        v = v + jnp.where(even_x, 0.0, FACE_PENALTY * ex[g, j * NODES + k])
                    if i == 0:
                        v = v + jnp.where(even_x, FACE_PENALTY * ex[g, j * NODES + k], 0.0)
                    if j == TOP:
                        v = v + jnp.where(even_y, 0.0, FACE_PENALTY * ey[g, i * NODES + k])
                    if j == 0:
                        v = v + jnp.where(even_y, FACE_PENALTY * ey[g, i * NODES + k], 0.0)
                    vals.append(v)
            return vals

        def finish(i, vals):
            for n in range(FACE):
                at = node(i, 0, 0) + n
                u1[g, at] = KEPT * u[g, at] + DAMPING * vals[n]

        smooth(load, finish, basis, invd, work)

        def val(n):
            return u1[g, n]

        rx = [restrict_face(x_face(val, s)) for s in (0, TOP)]
        ry = [restrict_face(y_face(val, s)) for s in (0, TOP)]
        rz = [restrict_face(z_face(val, s)) for s in (0, TOP)]
        back = -DAMPING
        ox = [back * v for v in restrict_face([ex[g, n] for n in range(FACE)])]
        oy = [back * v for v in restrict_face([ey[g, n] for n in range(FACE)])]
        both = inner_restricted(rx, ry, rz, ox, oy)
        for n in range(8):
            c0[g, n] = crd[g, n] + FACE_PENALTY * both[n]
        for n in range(4):
            work[g * 8 + n] = rx[0][n]
            work[g * 8 + 4 + n] = rx[1][n]
            yf[g, n] = jnp.where(even_y, ry[0][n], ry[1][n])
        return carry

    def pair_keep(g, carry):
        carry = pair(g, carry)
        for n in range(8):
            ex[g, n] = work[g * 8 + n]
        return carry

    lax.fori_loop(0, 2, pair_keep, 0)
    par_x = is_even(idx, 0)
    for n in range(8):
        swap_store(
            par_x, pack_lo(even_x, c0[0, n], c0[1, n], 2), pack_hi(even_x, c0[0, n], c0[1, n], 2), mx0, mx1, n
        )
    for n in range(4):
        lo = pack_lo(even_x, ex[0, n], ex[1, n], 2)
        hi = pack_hi(even_x, ex[0, 4 + n], ex[1, 4 + n], 2)
        xpk[0, n], xpk[1, n] = lo, hi
        swap_store(par_x, lo, hi, mx0, mx1, 8 + n)
        swap_store(
            par_x, pack_lo(even_x, yf[0, n], yf[1, n], 2), pack_hi(even_x, yf[0, n], yf[1, n], 2), mx0, mx1, 12 + n
        )
    for p in range(NODES):
        for q in range(NODES):
            n = p * NODES + q
            lo, hi = node(0, p, q), node(TOP, p, q)
            swap_store(
                par_x,
                pack_lo(even_x, u1[0, lo], u1[1, lo], 2),
                pack_hi(even_x, u1[0, hi], u1[1, hi], 2),
                mx0, mx1, 16 + n,
            )
            lo, hi = node(p, 0, q), node(p, TOP, q)
            yface[0, n] = pack_lo(even_y, u1[0, lo], u1[1, lo], 1)
            yface[1, n] = pack_hi(even_y, u1[0, hi], u1[1, hi], 1)


def middle_kernel(idx, rx0, rx1, c0, xpk, yf, yface, c1, ring, pyf, ypk, my0, my1):
    even_x, even_y = sublane_bits()
    par_x, par_y = is_even(idx, 0), is_even(idx, 1)

    def received(n):
        a, b = rx0[n], rx1[n]
        return jnp.where(par_x, a, b), jnp.where(par_x, b, a)

    for n in range(4):
        plus, minus = received(8 + n)
        o0, o1 = outer_pair(even_x, plus, minus, 2)
        for g, o in ((0, o0), (1, o1)):
            c1[g, 4 + n] = c0[g, 4 + n] + jnp.where(even_x, 0.0, FACE_PENALTY * o)
            c1[g, n] = c0[g, n] + jnp.where(even_x, FACE_PENALTY * o, 0.0)
        for a in (0, 1):
            plus, minus = received(a * 4 + n)
            ring[0, a * 4 + n] = plus if a else plus + FACE_PENALTY * xpk[1, n]
            ring[1, a * 4 + n] = minus + FACE_PENALTY * xpk[0, n] if a else minus
        pyf[0, n], pyf[1, n] = received(12 + n)
    for n in range(8):
        swap_store(
            par_y, pack_lo(even_y, c1[0, n], c1[1, n], 1), pack_hi(even_y, c1[0, n], c1[1, n], 1), my0, my1, n
        )
        swap_store(
            par_y,
            pack_lo(even_y, ring[1, n], ring[0, n], 1),
            pack_hi(even_y, ring[1, n], ring[0, n], 1),
            my0, my1, 8 + n,
        )
    for n in range(4):
        for part, (v0, v1) in enumerate(((yf[0, n], yf[1, n]), (pyf[1, n], pyf[0, n]))):
            lo, hi = pack_lo(even_y, v0, v1, 1), pack_hi(even_y, v0, v1, 1)
            ypk[part, 0, n], ypk[part, 1, n] = lo, hi
            swap_store(par_y, lo, hi, my0, my1, 16 + part * 4 + n)
    for n in range(FACE):
        swap_store(par_y, yface[0, n], yface[1, n], my0, my1, 24 + n)


def block_of(x, y, f):
    g, f2 = f // 2, f % 2
    inner_x, inner_y = x in (1, 2), y in (1, 2)
    if inner_x and inner_y:
        return f * 4 + (x - 1) * 2 + (y - 1)
    if inner_y:
        return (16 if x == 3 else 24) + f2 * 4 + g * 2 + (y - 1)
    if inner_x:
        return (32 if y == 3 else 40) + f2 * 4 + (x - 1) * 2 + g
    return (48 if y == 3 else 56) + f2 * 4 + g * 2 + (1 if x == 3 else 0)


def quotient(v, by):
    if by & (by - 1) == 0:
        return lax.shift_right_logical(v, by.bit_length() - 1)
    return lax.div(v, by)


def patch_kernel(
    rows_all, spans, idx, ry0, ry1, c1, ring, ypk, elements, mask, inverse, v, v0, v1, table, gath, answer, e_hi, e_lo
):
    even_x, even_y = sublane_bits()
    par_y = is_even(idx, 1)

    def received(n):
        a, b = ry0[n], ry1[n]
        return jnp.where(par_y, a, b), jnp.where(par_y, b, a)

    def put(source, n, value):
        table[pl.ds(source * 64 + n, 8, stride=8), :] = value

    for a in (0, 1):
        for c in (0, 1):
            f = a * 2 + c
            plus, minus = received(16 + f)
            own = outer_pair(even_y, plus, minus, 1)
            plus, minus = received(20 + f)
            out_minus, out_plus = outer_pair(even_y, plus, minus, 1)
            for b in (0, 1):
                n = a * 4 + b * 2 + c
                for g in (0, 1):
                    o = FACE_PENALTY * own[g]
                    put(g, n, c1[g, n] + (jnp.where(even_y, 0.0, o) if b else jnp.where(even_y, o, 0.0)))
                for side, o in ((0, out_plus), (1, out_minus)):
                    o = FACE_PENALTY * o
                    put(2 + side, n, ring[side, n] + (jnp.where(even_y, 0.0, o) if b else jnp.where(even_y, o, 0.0)))
                for part in (0, 1):
                    plus, minus = received(part * 8 + n)
                    if b:
                        minus = minus + FACE_PENALTY * ypk[part, 0, f]
                    else:
                        plus = plus + FACE_PENALTY * ypk[part, 1, f]
                    put(4 + part * 2, n, plus)
                    put(5 + part * 2, n, minus)

    span_x, span_y, layers = spans
    groups, width = elements.shape[1] // LANES, inverse.shape[0]

    def codes(rg):
        at = pl.ds(pl.multiple_of(rg * LANES, LANES), LANES)
        e = elements[:, at]
        live = mask[:, at] > 0
        column_of = quotient(e, layers)
        z = e - column_of * layers
        x = quotient(column_of, rows_all)
        y = column_of - x * rows_all - (idx[1] * span_y - 1)
        x = x - (idx[0] * span_x - 1)
        least = jnp.min(jnp.where(live, z, layers - 1), axis=0, keepdims=True)
        code = (z - least) * 16 + x * 4 + y
        return at, jnp.where(live, code, -1), jnp.where(live, 1.0, 0.0), least

    def gather(rg, carry):
        at, code, alive, least = codes(rg)
        z0 = jnp.broadcast_to(least, (SUB, LANES))
        z1 = jnp.minimum(z0 + 1, layers - 1)
        for f in range(4):
            picks = []
            for z in (z0, z1):
                for x in range(4):
                    for y in range(4):
                        block = table[pl.ds(block_of(x, y, f) * 8, 8), :]
                        picks.append(jnp.take_along_axis(block, z, axis=1, mode="promise_in_bounds"))
            for s in range(8):
                cs = jnp.broadcast_to(code[s : s + 1], (SUB, LANES))
                level = picks
                bit = 1
                while len(level) > 1:
                    odd = (cs & bit) != 0
                    level = [jnp.where(odd, level[2 * m + 1], level[2 * m]) for m in range(len(level) // 2)]
                    bit *= 2
                on = jnp.broadcast_to(alive[s : s + 1], (SUB, LANES))
                gath[pl.ds(rg * width + f * 64 + s, 8, stride=8), :] = level[0] * on
        return carry

    lax.fori_loop(0, groups, gather, 0)
    wide = jnp.concatenate([gath[rg * width : (rg + 1) * width, :] for rg in range(groups)], axis=1)
    solved = jnp.dot(inverse[...], wide, precision=lax.Precision.HIGHEST, preferred_element_type=F32)
    for rg in range(groups):
        answer[rg * width : (rg + 1) * width, :] = solved[:, rg * LANES : (rg + 1) * LANES]

    def spread(rg, carry):
        at, code, alive, least = codes(rg)
        cs = [jnp.broadcast_to(code[s : s + 1], (SUB, LANES)) for s in range(8)]
        values = [[answer[pl.ds(rg * width + f * 64 + s, 8, stride=8), :] for f in range(4)] for s in range(8)]
        for k in range(32):
            acc = [None] * 4
            for s in range(8):
                here = cs[s] == k
                for f in range(4):
                    term = jnp.where(here, values[s][f], 0.0)
                    acc[f] = term if acc[f] is None else acc[f] + term
            for h in (0, 1):
                both = jnp.concatenate([acc[2 * h], acc[2 * h + 1]], axis=0)
                hi = both.astype(jnp.bfloat16)
                rows = pl.ds(k * 32 + h * 16, 16)
                e_hi[rows, at] = hi
                e_lo[rows, at] = (both - hi.astype(F32)).astype(jnp.bfloat16)
        return carry

    lax.fori_loop(0, groups, spread, 0)
    hot = []
    for rg in range(groups):
        _, _, _, least = codes(rg)
        depth = lax.broadcasted_iota(jnp.int32, (LANES, LANES), 0)
        hot.append(jnp.where(depth == jnp.broadcast_to(least, (LANES, LANES)), 1.0, 0.0).astype(jnp.bfloat16))
    hot = jnp.concatenate(hot, axis=1)
    dims = (((1,), (1,)), ((), ()))
    both = lax.dot_general(e_hi[...], hot, dims, preferred_element_type=F32)
    both = both + lax.dot_general(e_lo[...], hot, dims, preferred_element_type=F32)
    for n in range(64):
        v[n] = both[n * 8 : n * 8 + 8] + pltpu.roll(both[512 + n * 8 : 512 + n * 8 + 8], 1, 1)
    for x in range(4):
        for yy in (0, 1):
            for f in range(4):
                swap_store(
                    par_y, v[(x * 4 + yy) * 4 + f], v[(x * 4 + 2 + yy) * 4 + f], v0, v1, (x * 2 + yy) * 4 + f
                )


def sum_kernel(idx, v, r0, r1, s, m0, m1):
    par_x, par_y = is_even(idx, 0), is_even(idx, 1)
    for x in range(4):
        for yy in (0, 1):
            for f in range(4):
                n = (x * 2 + yy) * 4 + f
                a, b = r0[n], r1[n]
                hi, lo = (x * 4 + 2 + yy) * 4 + f, (x * 4 + yy) * 4 + f
                s[hi] = v[hi] + jnp.where(par_y, a, b)
                s[lo] = v[lo] + jnp.where(par_y, b, a)
    for n in range(32):
        swap_store(par_x, s[n], s[32 + n], m0, m1, n)


def last_kernel(
    idx, basis, s, r0, r1, u1, rhs, invd, rx0, rx1, ry0, ry1, out_hbm, out, own, ringx, ringy, ex, ey, work, sems
):
    even_x, even_y = sublane_bits()
    par_x = is_even(idx, 0)
    combine_outer(idx, 0, even_x, rx0, rx1, FACE, 16, 2, ex)
    combine_outer(idx, 1, even_y, ry0, ry1, FACE, 24, 1, ey)

    def total(x, y, f):
        n = ((x % 2) * 4 + y) * 4 + f
        a, b = r0[n], r1[n]
        if x < 2:
            a, b = b, a
        return s[(x * 4 + y) * 4 + f] + jnp.where(par_x, a, b)

    for f in range(4):
        for x in (0, 1):
            for y in (0, 1):
                rows = pl.ds((f * 4 + x * 2 + y) * 8, 8)
                own[rows, :] = total(x + 1, y + 1, f)
                ringx[rows, :] = total(3 if x else 0, y + 1, f)
                ringy[rows, :] = total(x + 1, 3 if y else 0, f)

    def pair(g, carry):
        def take(ref, n):
            return ref[pl.ds(g * 64 + n, 8, stride=8), :]

        coarse = [take(own, n) for n in range(8)]
        for i in range(NODES):
            fine = prolong_face([combine(TABLE[i], [coarse[n], coarse[4 + n]]) for n in range(4)])
            for n in range(FACE):
                at = node(i, 0, 0) + n
                out[g, at] = u1[g, at] + fine[n]
        xr = [jnp.where(even_x, take(ringx, 4 + n), take(ringx, n)) for n in range(4)]
        yr = [
            jnp.where(even_y, take(ringy, a * 4 + 2 + c), take(ringy, a * 4 + c)) for a in (0, 1) for c in (0, 1)
        ]
        for n, v in enumerate(prolong_face(xr)):
            ex[g, n] = ex[g, n] + v
        for n, v in enumerate(prolong_face(yr)):
            ey[g, n] = ey[g, n] + v

        def load(i):
            vals = []
            for j in range(NODES):
                for k in range(NODES):
                    v = rhs[g, node(i, j, k)]
                    extra = couple(lambda n: out[g, n], i, j, k, lambda n: ex[g, n], lambda n: ey[g, n])
                    vals.append(v if extra is None else v + FACE_PENALTY * extra)
            return vals

        def finish(i, vals):
            for n in range(FACE):
                at = node(i, 0, 0) + n
                out[g, at] = KEPT * out[g, at] + DAMPING * vals[n]

        smooth(load, finish, basis, invd, work)
        return carry

    lax.fori_loop(0, 2, pair, 0)
    copies = []
    for f in range(out_hbm.shape[0]):
        half = SUB // 2
        src = out.at[f // 2, :, pl.ds(half * (f % 2), half), :]
        copies.append(pltpu.make_async_copy(src, out_hbm.at[f], sems.at[f]))
    for c in copies:
        c.start()
    for c in copies:
        c.wait()


SMEM = pl.BlockSpec(memory_space=pltpu.SMEM)
VMEM = pl.BlockSpec(memory_space=pltpu.VMEM)
ANY = pl.BlockSpec(memory_space=pl.ANY)


def regs(*lead):
    return jax.ShapeDtypeStruct((*lead, SUB, LANES), F32)


def call(kernel, ins, outs, out_specs, scratch=(), limit=24):
    return pl.pallas_call(
        kernel,
        in_specs=ins,
        out_specs=out_specs,
        out_shape=outs,
        scratch_shapes=scratch,
        compiler_params=pltpu.CompilerParams(vmem_limit_bytes=limit << 20),
    )


def swaps(axis, m0, m1):
    peers = lax.axis_size(axis)
    got = []
    for colour, m in enumerate((m0, m1)):
        pairs = []
        for i in range(colour, peers - 1, 2):
            pairs += [(i, i + 1), (i + 1, i)]
        got.append(lax.ppermute(m, axis, pairs))
    return got


def per_device(
    right_side, first_guess, coefficient, modal_basis, modal_values, patch_inverse, patch_elements, patch_mask
):
    fields, _, _, _, span_x, span_y, layers = right_side.shape
    rows_all = span_y * lax.axis_size("py")
    flat = (fields, CUBE, span_x * span_y, layers)
    idx = jnp.stack([lax.axis_index("px"), lax.axis_index("py")]).astype(jnp.int32)
    coef = coefficient.reshape(span_x * span_y, layers)
    coef = jnp.concatenate([coef, coef], axis=0)
    field_sems = pltpu.SemaphoreType.DMA((fields,))

    u, fx0, fx1, fy0, fy1 = call(
        faces_kernel, [SMEM, ANY], [regs(2, CUBE)] + [regs(FACE)] * 4, [VMEM] * 5, [field_sems]
    )(idx, first_guess.reshape(flat))
    fx = swaps("px", fx0, fx1)
    fy = swaps("py", fy0, fy1)
    rhs, w, crd, invd = call(
        local_kernel,
        [SMEM, SMEM, VMEM, VMEM, ANY],
        [regs(2, CUBE), regs(2, CUBE), regs(2, 8), regs(len(TRIPLES))],
        [VMEM] * 4,
        [field_sems],
    )(modal_basis, modal_values, u, coef, right_side.reshape(flat))
    outer = pltpu.VMEM((2, FACE, SUB, LANES), F32)
    work = pltpu.VMEM((CUBE, SUB, LANES), F32)
    u1, c0, xpk, yf, yface, mx0, mx1 = call(
        first_kernel,
        [SMEM, SMEM] + [VMEM] * 8,
        [regs(2, CUBE), regs(2, 8), regs(2, 4), regs(2, 4), regs(2, FACE), regs(16 + FACE), regs(16 + FACE)],
        [VMEM] * 7,
        [outer, outer, work],
    )(idx, modal_basis, *fx, *fy, u, w, crd, invd)
    rx = swaps("px", mx0, mx1)
    c1, ring, _, ypk, my0, my1 = call(
        middle_kernel,
        [SMEM] + [VMEM] * 6,
        [regs(2, 8), regs(2, 8), regs(2, 4), regs(2, 2, 4), regs(24 + FACE), regs(24 + FACE)],
        [VMEM] * 6,
    )(idx, *rx, c0, xpk, yf, yface)
    ry = swaps("py", my0, my1)
    rows = patch_elements.shape[0]
    slots = patch_elements.shape[1]
    width = patch_inverse.shape[0]
    v, v0, v1 = call(
        functools.partial(patch_kernel, rows_all, (span_x, span_y, layers)),
        [SMEM] + [VMEM] * 8,
        [regs(64), regs(32), regs(32)],
        [VMEM] * 3,
        [
            pltpu.VMEM((512, LANES), F32),
            pltpu.VMEM((width * rows // LANES, LANES), F32),
            pltpu.VMEM((width * rows // LANES, LANES), F32),
            pltpu.VMEM((1024, rows), jnp.bfloat16),
            pltpu.VMEM((1024, rows), jnp.bfloat16),
        ],
    )(idx, *ry, c1, ring, ypk, patch_elements.T, patch_mask.T, patch_inverse)
    rv = swaps("py", v0, v1)
    s, m0, m1 = call(sum_kernel, [SMEM] + [VMEM] * 3, [regs(64), regs(32), regs(32)], [VMEM] * 3)(idx, v, *rv)
    rs = swaps("px", m0, m1)
    table = pltpu.VMEM((128, LANES), F32)
    out = call(
        last_kernel,
        [SMEM, SMEM] + [VMEM] * 10,
        jax.ShapeDtypeStruct(flat, F32),
        ANY,
        [pltpu.VMEM((2, CUBE, SUB, LANES), F32), table, table, table, outer, outer, work, field_sems],
    )(idx, modal_basis, s, *rs, u1, rhs, invd, *rx, *ry)
    return out.reshape(right_side.shape)


def solution(mesh):
    in_specs = (
        P(None, None, None, None, "px", "py", None),
        P(None, None, None, None, "px", "py", None),
        P("px", "py", None),
        P(),
        P(),
        P(),
        P(("px", "py"), None),
        P(("px", "py"), None),
    )
    out_specs = P(None, None, None, None, "px", "py", None)
    return jax.shard_map(
        per_device, mesh=mesh, in_specs=in_specs, out_specs=out_specs, check_vma=False
    )
```

profile of v0, /device:TPU:22, one launch (start us, length us, event | category | flops | bytes accessed | tf_op | source)
XLA Modules:
  0.0 58.2 jit_solution(9996686407101086304)
XLA Ops:
  0.0 0.1 pad_add_fusion.idx
  0.1 1.2 %copy-done = f32[4,5,5,5,2,2,128]{6,5,4,3,2,1,0:T(2,128)S(1)} copy-done((f32[4,5,5,5,2,2,128]{6,5,4,3,2,1,0:T(2,128)S(1)}, f32[4,5,5,5,2,2,128]{6,5,4,3,2,1,0:T(2,128)}, u32[]{:S(2)}) %copy-start) | copy-done | bytes 1024024
  1.3 0.8 %shard_map.82 = (f32[2,125,8,128]{3,2,1,0:T(8,128)S(1)}, f32[25,8,128]{2,1,0:T(8,128)S(1)}, f32[25,8,128]{2,1,0:T(8,128)S(1)}, f32[25,8,128]{2,1,0:T(8,128)S(1)}, f32[25,8,128]{2,1,0:T(8,128)S(1)}) custom-call(s32[2]{0:T(128)S(1)} %pad_add_fusion.idx, f32[4,125,4,128]{3,2,1,0:T(4,128)S(1)} %bitcast.8), custom_call_target="tpu_custom_call" | custom-call | tf_op jit(solution)/shard_map/pallas_call | solution.py:663
  2.1 0.6 collective-permute-start
  2.7 4.4 %collective-permute-start.1 = (f32[25,8,128]{2,1,0:T(8,128)S(1)}, f32[25,8,128]{2,1,0:T(8,128)S(1)}, u32[]{:S(2)}, u32[]{:S(2)}) collective-permute-start(f32[25,8,128]{2,1,0:T(8,128)S(1)} %get-tuple-element.33), channel_id=1, source_target_pairs={{4,8},{8,4},{12,16},{16,12},{20,24},{24,20},{5,9},{9,5},{13,17},{1... | collective-permute-start | bytes 307208 | tf_op jit(solution)/shard_map/ppermute | solution.py:648
  7.1 0.0 copy-start.7
  7.1 0.1 collective-permute-start.2
  7.2 2.5 %collective-permute-start.3 = (f32[25,8,128]{2,1,0:T(8,128)S(1)}, f32[25,8,128]{2,1,0:T(8,128)S(1)}, u32[]{:S(2)}, u32[]{:S(2)}) collective-permute-start(f32[25,8,128]{2,1,0:T(8,128)S(1)} %get-tuple-element.35), channel_id=1, source_target_pairs={{1,2},{2,1},{5,6},{6,5},{9,10},{10,9},{13,14},{14,13},{17,18},{18,... | collective-permute-start | bytes 307208 | tf_op jit(solution)/shard_map/ppermute | solution.py:648
  9.8 0.0 copy-start.3
  9.8 0.0 copy-start.6
  9.8 0.6 %copy-done.3 = f32[5,5]{1,0:T(8,128)S(1)} copy-done((f32[5,5]{1,0:T(8,128)S(1)}, f32[5,5]{1,0:T(8,128)}, u32[]{:S(2)}) %copy-start.3) | copy-done | bytes 124
  10.4 1.8 %shard_map.83 = (f32[2,125,8,128]{3,2,1,0:T(8,128)S(1)}, f32[2,125,8,128]{3,2,1,0:T(8,128)S(1)}, f32[2,8,8,128]{3,2,1,0:T(8,128)S(1)}, f32[35,8,128]{2,1,0:T(8,128)S(1)}) custom-call(f32[5,5]{1,0:T(8,128)S(1)} %copy-done.3, f32[5]{0:T(128)S(1)} %copy-done.6, f32[2,125,8,128]{3,2,1,0:T(8,128)S(1)} %get-tuple-element.36.u, f32[8,128]{1,0:T(8,128)S(1)} %pad_maximum_fusion.coef, ...), custom_call_target="tpu_custom_call" | custom-call | tf_op jit(solution)/shard_map/pallas_call | solution.py:668
  12.2 0.0 collective-permute-done.fx0
  12.2 0.0 collective-permute-done.1.fx1
  12.2 0.9 %collective-permute-done.3.fy1 = f32[25,8,128]{2,1,0:T(8,128)S(1)} collective-permute-done((f32[25,8,128]{2,1,0:T(8,128)S(1)}, f32[25,8,128]{2,1,0:T(8,128)S(1)}, u32[]{:S(2)}, u32[]{:S(2)}) %collective-permute-start.3) | collective-permute-done | bytes 102432 | tf_op jit(solution)/shard_map/ppermute | solution.py:648
  13.2 2.9 %shard_map.84 = (f32[2,125,8,128]{3,2,1,0:T(8,128)S(1)}, f32[2,8,8,128]{3,2,1,0:T(8,128)S(1)}, f32[2,4,8,128]{3,2,1,0:T(8,128)S(1)}, f32[2,4,8,128]{3,2,1,0:T(8,...) custom-call(s32[2]{0:T(128)S(1)} %pad_add_fusion.idx, ...), custom_call_target="tpu_custom_call" | custom-call | tf_op jit(solution)/shard_map/pallas_call | solution.py:677
  16.1 0.1 collective-permute-start.4
  16.2 2.3 %collective-permute-start.5 = (f32[41,8,128]{2,1,0:T(8,128)S(1)}, f32[41,8,128]{2,1,0:T(8,128)S(1)}, u32[]{:S(2)}, u32[]{:S(2)}) collective-permute-start(f32[41,8,128]{2,1,0:T(8,128)S(1)} %get-tuple-element.41), channel_id=1, source_target_pairs={{4,8},{8,4},{12,16},{16,12},{20,24},{24,20},{5,9},{9,5},{13,17},{1... | collective-permute-start | bytes 503816 | tf_op jit(solution)/shard_map/ppermute | solution.py:648
  18.5 6.2 %collective-permute-done.4.rx0 = f32[41,8,128]{2,1,0:T(8,128)S(1)} collective-permute-done((f32[41,8,128]{2,1,0:T(8,128)S(1)}, f32[41,8,128]{2,1,0:T(8,128)S(1)}, u32[]{:S(2)}, u32[]{:S(2)}) %collective-permute-start.4) | collective-permute-done | bytes 167968 | tf_op jit(solution)/shard_map/ppermute | solution.py:648
  24.7 1.2 %shard_map.85 = (f32[2,8,8,128]{3,2,1,0:T(8,128)S(1)}, f32[2,8,8,128]{3,2,1,0:T(8,128)S(1)}, f32[2,4,8,128]{3,2,1,0:T(8,128)}, f32[2,2,4,8,128]{4,3,2,1,0:T(8,12...) custom-call(s32[2]{0:T(128)S(1)} %pad_add_fusion.idx, f32[41,8,128]{2,1,0:T(8,128)S(1)} %collective-permute-done.4.rx0, ...), custom_call_target="tpu_custom_call" | custom-call | tf_op jit(solution)/shard_map/pallas_call | solution.py:685
  25.9 1.9 %collective-permute-start.7 = (f32[49,8,128]{2,1,0:T(8,128)S(1)}, f32[49,8,128]{2,1,0:T(8,128)S(1)}, u32[]{:S(2)}, u32[]{:S(2)}) collective-permute-start(f32[49,8,128]{2,1,0:T(8,128)S(1)} %get-tuple-element.47), channel_id=1, source_target_pairs={{1,2},{2,1},{5,6},{6,5},{9,10},{10,9},{13,14},{14,13},{17,18},{18,... | collective-permute-start | bytes 602120 | tf_op jit(solution)/shard_map/ppermute | solution.py:648
  27.8 5.1 %collective-permute-done.7.ry1 = f32[49,8,128]{2,1,0:T(8,128)S(1)} collective-permute-done((f32[49,8,128]{2,1,0:T(8,128)S(1)}, f32[49,8,128]{2,1,0:T(8,128)S(1)}, u32[]{:S(2)}, u32[]{:S(2)}) %collective-permute-start.7) | collective-permute-done | bytes 200736 | tf_op jit(solution)/shard_map/ppermute | solution.py:648
  32.9 4.8 %shard_map.86 = (f32[64,8,128]{2,1,0:T(8,128)S(1)}, f32[32,8,128]{2,1,0:T(8,128)S(1)}, f32[32,8,128]{2,1,0:T(8,128)S(1)}) custom-call(s32[2]{0:T(128)S(1)} %pad_add_fusion.idx, f32[49,8,128]{2,1,0:T(8,128)S(1)} %collective-permute-done.6.ry0, f32[49,8,128]{2,1,0:T(8,128)S(1)} %collective-permute-done.7.ry1, f32[2,8,8,128]{3,2,1,0:T(8,128)S(1)} %get-tuple-element.48.c1, ...), custom_call_target="tpu_custom_call" | custom-call | tf_op jit(solution)/shard_map/pallas_call | solution.py:695
  37.7 0.1 collective-permute-start.8
  37.8 1.9 %collective-permute-start.9 = (f32[32,8,128]{2,1,0:T(8,128)S(1)}, f32[32,8,128]{2,1,0:T(8,128)S(1)}, u32[]{:S(2)}, u32[]{:S(2)}) collective-permute-start(f32[32,8,128]{2,1,0:T(8,128)S(1)} %get-tuple-element.53), channel_id=1, source_target_pairs={{1,2},{2,1},{5,6},{6,5},{9,10},{10,9},{13,14},{14,13},{17,18},{18,... | collective-permute-start | bytes 393224 | tf_op jit(solution)/shard_map/ppermute | solution.py:648
  39.8 4.3 %collective-permute-done.9.r1 = f32[32,8,128]{2,1,0:T(8,128)S(1)} collective-permute-done((f32[32,8,128]{2,1,0:T(8,128)S(1)}, f32[32,8,128]{2,1,0:T(8,128)S(1)}, u32[]{:S(2)}, u32[]{:S(2)}) %collective-permute-start.9) | collective-permute-done | bytes 131104 | tf_op jit(solution)/shard_map/ppermute | solution.py:648
  44.1 0.6 %shard_map.87 = (f32[64,8,128]{2,1,0:T(8,128)S(1)}, f32[32,8,128]{2,1,0:T(8,128)S(1)}, f32[32,8,128]{2,1,0:T(8,128)S(1)}) custom-call(s32[2]{0:T(128)S(1)} %pad_add_fusion.idx, f32[64,8,128]{2,1,0:T(8,128)S(1)} %get-tuple-element.51.v, f32[32,8,128]{2,1,0:T(8,128)S(1)} %collective-permute-done.8.r0, f32[32,8,128]{2,1,0:T(8,128)S(1)} %collective-permute-done.9.r1), custom_call_target="tpu_custom_call" | custom-call | tf_op jit(solution)/shard_map/pallas_call | solution.py:709
  44.7 1.7 %collective-permute-start.10 = (f32[32,8,128]{2,1,0:T(8,128)S(1)}, f32[32,8,128]{2,1,0:T(8,128)S(1)}, u32[]{:S(2)}, u32[]{:S(2)}) collective-permute-start(f32[32,8,128]{2,1,0:T(8,128)S(1)} %get-tuple-element.55), channel_id=1, source_target_pairs={{0,4},{4,0},{8,12},{12,8},{16,20},{20,16},{24,28},{28,24},{1,5},{5... | collective-permute-start | bytes 393224 | tf_op jit(solution)/shard_map/ppermute | solution.py:648
  46.4 1.9 %collective-permute-start.11 = (f32[32,8,128]{2,1,0:T(8,128)S(1)}, f32[32,8,128]{2,1,0:T(8,128)S(1)}, u32[]{:S(2)}, u32[]{:S(2)}) collective-permute-start(f32[32,8,128]{2,1,0:T(8,128)S(1)} %get-tuple-element.56), channel_id=1, source_target_pairs={{4,8},{8,4},{12,16},{16,12},{20,24},{24,20},{5,9},{9,5},{13,17},{1... | collective-permute-start | bytes 393224 | tf_op jit(solution)/shard_map/ppermute | solution.py:648
  48.3 1.4 %collective-permute-done.10.r0 = f32[32,8,128]{2,1,0:T(8,128)S(1)} collective-permute-done((f32[32,8,128]{2,1,0:T(8,128)S(1)}, f32[32,8,128]{2,1,0:T(8,128)S(1)}, u32[]{:S(2)}, u32[]{:S(2)}) %collective-permute-start.10) | collective-permute-done | bytes 131104 | tf_op jit(solution)/shard_map/ppermute | solution.py:648
  49.7 4.4 %collective-permute-done.11.r1 = f32[32,8,128]{2,1,0:T(8,128)S(1)} collective-permute-done((f32[32,8,128]{2,1,0:T(8,128)S(1)}, f32[32,8,128]{2,1,0:T(8,128)S(1)}, u32[]{:S(2)}, u32[]{:S(2)}) %collective-permute-start.11) | collective-permute-done | bytes 131104 | tf_op jit(solution)/shard_map/ppermute | solution.py:648
  54.2 4.0 %shard_map.88 = f32[4,125,4,128]{3,2,1,0:T(4,128)} custom-call(s32[2]{0:T(128)S(1)} %pad_add_fusion.idx, f32[5,5]{1,0:T(8,128)S(1)} %copy-done.3, f32[64,8,128]{2,1,0:T(8,128)S(1)} %get-tuple-element.54.s, f32[32,8,128]{2,1,0:T(8,128)S(1)} %collective-permute-done.10.r0, f32[32,8,128]{2,1,0:T(8,128)S(1)} %collective-permute-done.11.r1, ...), custom_call_target="tpu_custom_call" | custom-call | tf_op jit(solution)/shard_map/pallas_call | solution.py:712
  (17 shorter events, 0.0 us)
Async XLA Ops:
  0.1 1.2 %copy-start = (f32[4,5,5,5,2,2,128]{6,5,4,3,2,1,0:T(2,128)S(1)}, f32[4,5,5,5,2,2,128]{6,5,4,3,2,1,0:T(2,128)}, u32[]{:S(2)}) copy-start(f32[4,5,5,5,2,2,128]{6,5,4,3,2,1,0:T(2,128)} %param.9) | copy-start | bytes 3072004
  1.3 8.5 %copy-start.1 = (f32[4,5,5,5,2,2,128]{6,5,4,3,2,1,0:T(2,128)S(1)}, f32[4,5,5,5,2,2,128]{6,5,4,3,2,1,0:T(2,128)}, u32[]{:S(2)}) copy-start(f32[4,5,5,5,2,2,128]{6,5,4,3,2,1,0:T(2,128)} %param.8) | copy-start | bytes 3072004
  2.1 10.1 %collective-permute-start = (f32[25,8,128]{2,1,0:T(8,128)S(1)}, f32[25,8,128]{2,1,0:T(8,128)S(1)}, u32[]{:S(2)}, u32[]{:S(2)}) collective-permute-start(f32[25,8,128]{2,1,0:T(8,128)S(1)} %get-tuple-element.32), channel_id=1, source_target_pairs={{0,4},{4,0},{8,12},{12,8},{16,20},{20,16},{24,28},{28,24},{1,5},{5... | collective-permute-start | bytes 307208 | tf_op jit(solution)/shard_map/ppermute | solution.py:648
  2.7 9.5 %collective-permute-start.1 = (f32[25,8,128]{2,1,0:T(8,128)S(1)}, f32[25,8,128]{2,1,0:T(8,128)S(1)}, u32[]{:S(2)}, u32[]{:S(2)}) collective-permute-start(f32[25,8,128]{2,1,0:T(8,128)S(1)} %get-tuple-element.33), channel_id=1, source_target_pairs={{4,8},{8,4},{12,16},{16,12},{20,24},{24,20},{5,9},{9,5},{13,17},{1... | collective-permute-start | bytes 307208 | tf_op jit(solution)/shard_map/ppermute | solution.py:648
  7.1 2.6 %copy-start.7 = (f32[2,2,128]{2,1,0:T(2,128)S(1)}, f32[2,2,128]{2,1,0:T(2,128)}, u32[]{:S(2)}) copy-start(f32[2,2,128]{2,1,0:T(2,128)} %param.10) | copy-start | bytes 6148
  7.1 5.1 %collective-permute-start.2 = (f32[25,8,128]{2,1,0:T(8,128)S(1)}, f32[25,8,128]{2,1,0:T(8,128)S(1)}, u32[]{:S(2)}, u32[]{:S(2)}) collective-permute-start(f32[25,8,128]{2,1,0:T(8,128)S(1)} %get-tuple-element.34), channel_id=1, source_target_pairs={{0,1},{1,0},{2,3},{3,2},{4,5},{5,4},{6,7},{7,6},{8,9},{9,8},{10,11... | collective-permute-start | bytes 307208 | tf_op jit(solution)/shard_map/ppermute | solution.py:648
  7.2 6.0 %collective-permute-start.3 = (f32[25,8,128]{2,1,0:T(8,128)S(1)}, f32[25,8,128]{2,1,0:T(8,128)S(1)}, u32[]{:S(2)}, u32[]{:S(2)}) collective-permute-start(f32[25,8,128]{2,1,0:T(8,128)S(1)} %get-tuple-element.35), channel_id=1, source_target_pairs={{1,2},{2,1},{5,6},{6,5},{9,10},{10,9},{13,14},{14,13},{17,18},{18,... | collective-permute-start | bytes 307208 | tf_op jit(solution)/shard_map/ppermute | solution.py:648
  9.8 0.7 %copy-start.3 = (f32[5,5]{1,0:T(8,128)S(1)}, f32[5,5]{1,0:T(8,128)}, u32[]{:S(2)}) copy-start(f32[5,5]{1,0:T(8,128)} %basis.5) | copy-start | bytes 304
  9.8 0.7 %copy-start.6 = (f32[5]{0:T(128)S(1)}, f32[5]{0:T(128)}, u32[]{:S(2)}) copy-start(f32[5]{0:T(128)} %lam.1) | copy-start | bytes 64
  16.1 8.6 %collective-permute-start.4 = (f32[41,8,128]{2,1,0:T(8,128)S(1)}, f32[41,8,128]{2,1,0:T(8,128)S(1)}, u32[]{:S(2)}, u32[]{:S(2)}) collective-permute-start(f32[41,8,128]{2,1,0:T(8,128)S(1)} %get-tuple-element.40), channel_id=1, source_target_pairs={{0,4},{4,0},{8,12},{12,8},{16,20},{20,16},{24,28},{28,24},{1,5},{5... | collective-permute-start | bytes 503816 | tf_op jit(solution)/shard_map/ppermute | solution.py:648
  16.2 8.5 %collective-permute-start.5 = (f32[41,8,128]{2,1,0:T(8,128)S(1)}, f32[41,8,128]{2,1,0:T(8,128)S(1)}, u32[]{:S(2)}, u32[]{:S(2)}) collective-permute-start(f32[41,8,128]{2,1,0:T(8,128)S(1)} %get-tuple-element.41), channel_id=1, source_target_pairs={{4,8},{8,4},{12,16},{16,12},{20,24},{24,20},{5,9},{9,5},{13,17},{1... | collective-permute-start | bytes 503816 | tf_op jit(solution)/shard_map/ppermute | solution.py:648
  24.7 8.2 %copy-start.2 = (f32[256,256]{1,0:T(8,128)S(1)}, f32[256,256]{1,0:T(8,128)}, u32[]{:S(2)}) copy-start(f32[256,256]{1,0:T(8,128)} %inverse.1) | copy-start | bytes 786436
  24.7 8.2 %copy-start.4 = (s32[512,8]{0,1:T(8,128)S(1)}, s32[512,8]{0,1:T(8,128)}, u32[]{:S(2)}) copy-start(s32[512,8]{0,1:T(8,128)} %param.14) | copy-start | bytes 49156
  24.7 8.2 %copy-start.5 = (s32[512,8]{0,1:T(8,128)S(1)}, s32[512,8]{0,1:T(8,128)}, u32[]{:S(2)}) copy-start(s32[512,8]{0,1:T(8,128)} %param.15) | copy-start | bytes 49156
  25.9 1.9 %collective-permute-start.6 = (f32[49,8,128]{2,1,0:T(8,128)S(1)}, f32[49,8,128]{2,1,0:T(8,128)S(1)}, u32[]{:S(2)}, u32[]{:S(2)}) collective-permute-start(f32[49,8,128]{2,1,0:T(8,128)S(1)} %get-tuple-element.46), channel_id=1, source_target_pairs={{0,1},{1,0},{2,3},{3,2},{4,5},{5,4},{6,7},{7,6},{8,9},{9,8},{10,11... | collective-permute-start | bytes 602120 | tf_op jit(solution)/shard_map/ppermute | solution.py:648
  25.9 7.0 %collective-permute-start.7 = (f32[49,8,128]{2,1,0:T(8,128)S(1)}, f32[49,8,128]{2,1,0:T(8,128)S(1)}, u32[]{:S(2)}, u32[]{:S(2)}) collective-permute-start(f32[49,8,128]{2,1,0:T(8,128)S(1)} %get-tuple-element.47), channel_id=1, source_target_pairs={{1,2},{2,1},{5,6},{6,5},{9,10},{10,9},{13,14},{14,13},{17,18},{18,... | collective-permute-start | bytes 602120 | tf_op jit(solution)/shard_map/ppermute | solution.py:648
  37.7 2.0 %collective-permute-start.8 = (f32[32,8,128]{2,1,0:T(8,128)S(1)}, f32[32,8,128]{2,1,0:T(8,128)S(1)}, u32[]{:S(2)}, u32[]{:S(2)}) collective-permute-start(f32[32,8,128]{2,1,0:T(8,128)S(1)} %get-tuple-element.52), channel_id=1, source_target_pairs={{0,1},{1,0},{2,3},{3,2},{4,5},{5,4},{6,7},{7,6},{8,9},{9,8},{10,11... | collective-permute-start | bytes 393224 | tf_op jit(solution)/shard_map/ppermute | solution.py:648
  37.8 6.3 %collective-permute-start.9 = (f32[32,8,128]{2,1,0:T(8,128)S(1)}, f32[32,8,128]{2,1,0:T(8,128)S(1)}, u32[]{:S(2)}, u32[]{:S(2)}) collective-permute-start(f32[32,8,128]{2,1,0:T(8,128)S(1)} %get-tuple-element.53), channel_id=1, source_target_pairs={{1,2},{2,1},{5,6},{6,5},{9,10},{10,9},{13,14},{14,13},{17,18},{18,... | collective-permute-start | bytes 393224 | tf_op jit(solution)/shard_map/ppermute | solution.py:648
  44.7 5.0 %collective-permute-start.10 = (f32[32,8,128]{2,1,0:T(8,128)S(1)}, f32[32,8,128]{2,1,0:T(8,128)S(1)}, u32[]{:S(2)}, u32[]{:S(2)}) collective-permute-start(f32[32,8,128]{2,1,0:T(8,128)S(1)} %get-tuple-element.55), channel_id=1, source_target_pairs={{0,4},{4,0},{8,12},{12,8},{16,20},{20,16},{24,28},{28,24},{1,5},{5... | collective-permute-start | bytes 393224 | tf_op jit(solution)/shard_map/ppermute | solution.py:648
  46.4 7.7 %collective-permute-start.11 = (f32[32,8,128]{2,1,0:T(8,128)S(1)}, f32[32,8,128]{2,1,0:T(8,128)S(1)}, u32[]{:S(2)}, u32[]{:S(2)}) collective-permute-start(f32[32,8,128]{2,1,0:T(8,128)S(1)} %get-tuple-element.56), channel_id=1, source_target_pairs={{4,8},{8,4},{12,16},{16,12},{20,24},{24,20},{5,9},{9,5},{13,17},{1... | collective-permute-start | bytes 393224 | tf_op jit(solution)/shard_map/ppermute | solution.py:648
where the time goes:
time: 58.5 us; the launch traced here: 58.2 us
  waiting for transfers between devices  22.4 us (38%)
  starting transfers between devices  17.5 us (30%)
  Pallas kernels  16.1 us (28%)
  local copies, waits for them, and re-layouts  1.89 us (3%)
    ppermute x12, waiting for transfers between devices, swaps(): got.append(lax.ppermute(m, axis, pairs))  22.4 us
    ppermute x12, starting transfers between devices, swaps(): got.append(lax.ppermute(m, axis, pairs))  17.5 us
    pallas_call x1, Pallas kernels, per_device(): call(functools.partial(patch_kernel, rows_all, (span_x, span_y, layers)),...  4.82 us
    pallas_call x1, Pallas kernels, per_device(): call(last_kernel, [SMEM, SMEM] + [VMEM] * 10, jax.ShapeDtypeStruct(flat,...  3.99 us
    pallas_call x1, Pallas kernels, per_device(): call(first_kernel, [SMEM, SMEM] + [VMEM] * 8, [regs(2, CUBE), regs(2, 8),...  2.94 us
    unnamed x16, local copies, waits for them, and re-layouts  1.89 us
    pallas_call x1, Pallas kernels, per_device(): call(local_kernel, [SMEM, SMEM, VMEM, VMEM, ANY], [regs(2, CUBE), regs(2,...  1.75 us
    pallas_call x1, Pallas kernels, per_device(): call(middle_kernel, [SMEM] + [VMEM] * 6, [regs(2, 8), regs(2, 8), regs(2,...  1.18 us
  transfers between devices with their start and end apart: 12, of which 6 were waited for; matrix products, arithmetic and copies ran while one was open for 0% of the time, Pallas kernels for 3%

commit v1 on v0

--- a/solution.py
+++ b/solution.py
@@ -36,6 +36,15 @@
     return lax.broadcasted_iota(jnp.int32, (SUB, LANES), 1)
 
 
+def coefficient_bits():
+    sub = lax.broadcasted_iota(jnp.int32, (SUB, LANES), 0)
+    return (sub & 4) != 0, (sub & 2) != 0
+
+
+def at_ring(x, y, f):
+    return (x * 4 + y) * 4 + f
+
+
 def down(v, by):
     return pltpu.roll(v, SUB - by, 0)
 
@@ -68,8 +77,8 @@
     return [combine(TABLE[k], half[j]) for j in range(NODES) for k in range(NODES)]
 
 
-def is_even(idx_ref, which):
-    return (jnp.full((SUB, LANES), idx_ref[which], jnp.int32) & 1) == 0
+def is_even(axis):
+    return (jnp.full((SUB, LANES), lax.axis_index(axis), jnp.int32) & 1) == 0
 
 
 def pack_lo(first, v0, v1, by):
@@ -107,26 +116,30 @@
 
 
 def smooth(load_plane, finish, basis, invd, work):
-    fwd = [[basis[i, a] for i in range(NODES)] for a in range(NODES)]
-    bwd = [[basis[i, a] for a in range(NODES)] for i in range(NODES)]
+    def columns():
+        return [[basis[i * NODES + a] for i in range(NODES)] for a in range(NODES)]
+
+    def rows():
+        return [[basis[i * NODES + a] for a in range(NODES)] for i in range(NODES)]
 
     def plane(vals, mats):
         mid = [[combine(m, vals[j * NODES : (j + 1) * NODES]) for m in mats] for j in range(NODES)]
         return [[combine(m, [mid[j][c] for j in range(NODES)]) for c in range(NODES)] for m in mats]
 
     for i in range(NODES):
-        out = plane(load_plane(i), fwd)
+        out = plane(load_plane(i), columns())
         for b in range(NODES):
             for c in range(NODES):
                 work[node(i, b, c)] = out[b][c]
     for b in range(NODES):
+        fwd, bwd = columns(), rows()
         for c in range(NODES):
             vals = [work[node(i, b, c)] for i in range(NODES)]
             modal = [combine(fwd[a], vals) * invd[order_of(a, b, c)] for a in range(NODES)]
             for i in range(NODES):
                 work[node(i, b, c)] = combine(bwd[i], modal)
     for i in range(NODES):
-        out = plane([work[node(i, 0, 0) + n] for n in range(FACE)], bwd)
+        out = plane([work[node(i, 0, 0) + n] for n in range(FACE)], rows())
         finish(i, [out[j][k] for j in range(NODES) for k in range(NODES)])
 
 
@@ -187,11 +200,17 @@
     return copies
 
 
-def faces_kernel(idx, u_hbm, u, mx0, mx1, my0, my1, sems):
-    for c in take_in(u_hbm, u, sems):
+def faces_kernel(u_hbm, basis, lam, coef, u, basis_out, lam_out, coef_out, mx0, mx1, my0, my1, sems, few):
+    copies = take_in(u_hbm, u, sems)
+    half = SUB // 2
+    more = ((basis, basis_out), (lam, lam_out), (coef, coef_out.at[0:half]), (coef, coef_out.at[half:SUB]))
+    more = [pltpu.make_async_copy(src, dst, few.at[n]) for n, (src, dst) in enumerate(more)]
+    for c in more:
+        c.start()
+    for c in copies + more:
         c.wait()
     even_x, even_y = sublane_bits()
-    par_x, par_y = is_even(idx, 0), is_even(idx, 1)
+    par_x, par_y = is_even("px"), is_even("py")
     for p in range(NODES):
         for q in range(NODES):
             n = p * NODES + q
@@ -211,18 +230,22 @@
             )
 
 
-def local_kernel(basis, lam, u, coef, rhs_hbm, rhs, w, crd, invd, sems):
+def local_kernel(basis_in, lam_in, coef, u, rhs_hbm, rhs, w, crd, invd, basis, wide_ref, sems):
     copies = take_in(rhs_hbm, rhs, sems)
     scale = coef[...]
+    for i in range(NODES):
+        for a in range(NODES):
+            basis[i * NODES + a] = jnp.broadcast_to(basis_in[i : i + 1, a : a + 1], (SUB, LANES))
+    lam = [jnp.broadcast_to(lam_in[0:1, a : a + 1], (SUB, LANES)) for a in range(NODES)]
     for t, (a, b, c) in enumerate(TRIPLES):
         invd[t] = 1.0 / (scale * (lam[a] + lam[b] + lam[c]) + MASS_SHIFT)
-    wide = []
     for c in (0, 1):
         modal = [
-            lam[m] * combine([1.0] * NODES, [basis[i, m] * TABLE[i][c] for i in range(NODES)])
+            lam[m] * combine([1.0] * NODES, [basis[i * NODES + m] * TABLE[i][c] for i in range(NODES)])
             for m in range(NODES)
         ]
-        wide.append([combine([1.0] * NODES, [basis[i, m] * modal[m] for m in range(NODES)]) for i in range(NODES)])
+        for i in range(NODES):
+            wide_ref[c * NODES + i] = combine([1.0] * NODES, [basis[i * NODES + m] * modal[m] for m in range(NODES)])
     for cp in copies:
         cp.wait()
 
@@ -230,6 +253,7 @@
         def val(n):
             return u[g, n]
 
+        wide = [[wide_ref[c * NODES + i] for i in range(NODES)] for c in (0, 1)]
         plain, stiff = [], []
         for i in range(NODES):
             t, s, r = [], [], []
@@ -266,18 +290,18 @@
     lax.fori_loop(0, 2, pair, 0)
 
 
-def combine_outer(idx, which, first, r0, r1, rows, base, by, out):
-    even = is_even(idx, which)
+def combine_outer(axis, first, r0, r1, rows, base, by, out):
+    even = is_even(axis)
     for n in range(rows):
         a, b = r0[base + n], r1[base + n]
         plus, minus = jnp.where(even, a, b), jnp.where(even, b, a)
         out[0, n], out[1, n] = outer_pair(first, plus, minus, by)
 
 
-def first_kernel(idx, basis, fx0, fx1, fy0, fy1, u, w, crd, invd, u1, c0, xpk, yf, yface, mx0, mx1, ex, ey, work):
+def first_kernel(basis, fx0, fx1, fy0, fy1, u, w, crd, invd, u1, c0, xpk, yf, ux0, ux1, my0, my1, mx0, mx1, ex, ey, work):
     even_x, even_y = sublane_bits()
-    combine_outer(idx, 0, even_x, fx0, fx1, FACE, 0, 2, ex)
-    combine_outer(idx, 1, even_y, fy0, fy1, FACE, 0, 1, ey)
+    combine_outer("px", even_x, fx0, fx1, FACE, 0, 2, ex)
+    combine_outer("py", even_y, fy0, fy1, FACE, 0, 1, ey)
 
     def pair(g, carry):
         def load(i):
@@ -328,7 +352,7 @@
         return carry
 
     lax.fori_loop(0, 2, pair_keep, 0)
-    par_x = is_even(idx, 0)
+    par_x, par_y = is_even("px"), is_even("py")
     for n in range(8):
         swap_store(
             par_x, pack_lo(even_x, c0[0, n], c0[1, n], 2), pack_hi(even_x, c0[0, n], c0[1, n], 2), mx0, mx1, n
@@ -349,16 +373,20 @@
                 par_x,
                 pack_lo(even_x, u1[0, lo], u1[1, lo], 2),
                 pack_hi(even_x, u1[0, hi], u1[1, hi], 2),
-                mx0, mx1, 16 + n,
+                ux0, ux1, n,
             )
             lo, hi = node(p, 0, q), node(p, TOP, q)
-            yface[0, n] = pack_lo(even_y, u1[0, lo], u1[1, lo], 1)
-            yface[1, n] = pack_hi(even_y, u1[0, hi], u1[1, hi], 1)
-
-
-def middle_kernel(idx, rx0, rx1, c0, xpk, yf, yface, c1, ring, pyf, ypk, my0, my1):
+            swap_store(
+                par_y,
+                pack_lo(even_y, u1[0, lo], u1[1, lo], 1),
+                pack_hi(even_y, u1[0, hi], u1[1, hi], 1),
+                my0, my1, 24 + n,
+            )
+
+
+def middle_kernel(rx0, rx1, c0, xpk, yf, _0, _1, c1, ring, ypk, my0, my1):
     even_x, even_y = sublane_bits()
-    par_x, par_y = is_even(idx, 0), is_even(idx, 1)
+    par_x, par_y = is_even("px"), is_even("py")
 
     def received(n):
         a, b = rx0[n], rx1[n]
@@ -374,7 +402,6 @@
             plus, minus = received(a * 4 + n)
             ring[0, a * 4 + n] = plus if a else plus + FACE_PENALTY * xpk[1, n]
             ring[1, a * 4 + n] = minus + FACE_PENALTY * xpk[0, n] if a else minus
-        pyf[0, n], pyf[1, n] = received(12 + n)
     for n in range(8):
         swap_store(
             par_y, pack_lo(even_y, c1[0, n], c1[1, n], 1), pack_hi(even_y, c1[0, n], c1[1, n], 1), my0, my1, n
@@ -386,12 +413,11 @@
             my0, my1, 8 + n,
         )
     for n in range(4):
-        for part, (v0, v1) in enumerate(((yf[0, n], yf[1, n]), (pyf[1, n], pyf[0, n]))):
+        plus, minus = received(12 + n)
+        for part, (v0, v1) in enumerate(((yf[0, n], yf[1, n]), (minus, plus))):
             lo, hi = pack_lo(even_y, v0, v1, 1), pack_hi(even_y, v0, v1, 1)
             ypk[part, 0, n], ypk[part, 1, n] = lo, hi
             swap_store(par_y, lo, hi, my0, my1, 16 + part * 4 + n)
-    for n in range(FACE):
-        swap_store(par_y, yface[0, n], yface[1, n], my0, my1, 24 + n)
 
 
 def block_of(x, y, f):
@@ -413,10 +439,10 @@
 
 
 def patch_kernel(
-    rows_all, spans, idx, ry0, ry1, c1, ring, ypk, elements, mask, inverse, v, v0, v1, table, gath, answer, e_hi, e_lo
+    rows_all, spans, ry0, ry1, c1, ring, ypk, elements, mask, inverse, v, v0, v1, table, gath, answer, e_hi, e_lo
 ):
-    even_x, even_y = sublane_bits()
-    par_y = is_even(idx, 1)
+    _, even_y = sublane_bits()
+    par_y = is_even("py")
 
     def received(n):
         a, b = ry0[n], ry1[n]
@@ -459,14 +485,14 @@
         column_of = quotient(e, layers)
         z = e - column_of * layers
         x = quotient(column_of, rows_all)
-        y = column_of - x * rows_all - (idx[1] * span_y - 1)
-        x = x - (idx[0] * span_x - 1)
+        y = column_of - x * rows_all - (lax.axis_index("py") * span_y - 1)
+        x = x - (lax.axis_index("px") * span_x - 1)
         least = jnp.min(jnp.where(live, z, layers - 1), axis=0, keepdims=True)
         code = (z - least) * 16 + x * 4 + y
         return at, jnp.where(live, code, -1), jnp.where(live, 1.0, 0.0), least
 
     def gather(rg, carry):
-        at, code, alive, least = codes(rg)
+        _, code, alive, least = codes(rg)
         z0 = jnp.broadcast_to(least, (SUB, LANES))
         z1 = jnp.minimum(z0 + 1, layers - 1)
         for f in range(4):
@@ -495,7 +521,7 @@
         answer[rg * width : (rg + 1) * width, :] = solved[:, rg * LANES : (rg + 1) * LANES]
 
     def spread(rg, carry):
-        at, code, alive, least = codes(rg)
+        at, code, _, _ = codes(rg)
         cs = [jnp.broadcast_to(code[s : s + 1], (SUB, LANES)) for s in range(8)]
         values = [[answer[pl.ds(rg * width + f * 64 + s, 8, stride=8), :] for f in range(4)] for s in range(8)]
         for k in range(32):
@@ -525,50 +551,66 @@
     both = both + lax.dot_general(e_lo[...], hot, dims, preferred_element_type=F32)
     for n in range(64):
         v[n] = both[n * 8 : n * 8 + 8] + pltpu.roll(both[512 + n * 8 : 512 + n * 8 + 8], 1, 1)
-    for x in range(4):
-        for yy in (0, 1):
-            for f in range(4):
-                swap_store(
-                    par_y, v[(x * 4 + yy) * 4 + f], v[(x * 4 + 2 + yy) * 4 + f], v0, v1, (x * 2 + yy) * 4 + f
-                )
-
-
-def sum_kernel(idx, v, r0, r1, s, m0, m1):
-    par_x, par_y = is_even(idx, 0), is_even(idx, 1)
-    for x in range(4):
-        for yy in (0, 1):
-            for f in range(4):
-                n = (x * 2 + yy) * 4 + f
-                a, b = r0[n], r1[n]
-                hi, lo = (x * 4 + 2 + yy) * 4 + f, (x * 4 + yy) * 4 + f
-                s[hi] = v[hi] + jnp.where(par_y, a, b)
-                s[lo] = v[lo] + jnp.where(par_y, b, a)
-    for n in range(32):
-        swap_store(par_x, s[n], s[32 + n], m0, m1, n)
+    high_b = coefficient_bits()[1]
+    for f in range(4):
+        for x in range(4):
+            swap_store(par_y, v[at_ring(x, 0, f)], v[at_ring(x, 3, f)], v0, v1, x * 4 + f)
+        for x in (0, 2):
+            lo = jnp.where(high_b, up(v[at_ring(x + 1, 1, f)], 2), v[at_ring(x, 1, f)])
+            hi = jnp.where(high_b, v[at_ring(x, 2, f)], down(v[at_ring(x + 1, 2, f)], 2))
+            swap_store(par_y, lo, hi, v0, v1, 16 + x * 2 + f)
+
+
+def sum_kernel(v, r0, r1, s, m0, m1):
+    par_x, par_y = is_even("px"), is_even("py")
+    high_a, high_b = coefficient_bits()
+
+    def received(n):
+        a, b = r0[n], r1[n]
+        return jnp.where(par_y, a, b), jnp.where(par_y, b, a)
+
+    for f in range(4):
+        for x in range(4):
+            plus, minus = received(x * 4 + f)
+            s[at_ring(x, 2, f)] = v[at_ring(x, 2, f)] + plus
+            s[at_ring(x, 1, f)] = v[at_ring(x, 1, f)] + minus
+        for x in (0, 2):
+            plus, minus = received(16 + x * 2 + f)
+            s[at_ring(x, 3, f)] = v[at_ring(x, 3, f)] + plus
+            s[at_ring(x + 1, 3, f)] = v[at_ring(x + 1, 3, f)] + down(plus, 2)
+            s[at_ring(x, 0, f)] = v[at_ring(x, 0, f)] + minus
+            s[at_ring(x + 1, 0, f)] = v[at_ring(x + 1, 0, f)] + up(minus, 2)
+        for y in (1, 2):
+            swap_store(par_x, s[at_ring(0, y, f)], s[at_ring(3, y, f)], m0, m1, (y - 1) * 4 + f)
+        lo = jnp.where(high_b, s[at_ring(0, 0, f)], s[at_ring(0, 3, f)])
+        hi = jnp.where(high_b, s[at_ring(3, 0, f)], s[at_ring(3, 3, f)])
+        swap_store(par_x, lo, hi, m0, m1, 8 + f)
+        lo = jnp.where(high_a, up(s[at_ring(1, 2, f)], 4), s[at_ring(1, 1, f)])
+        hi = jnp.where(high_a, s[at_ring(2, 2, f)], down(s[at_ring(2, 1, f)], 4))
+        swap_store(par_x, lo, hi, m0, m1, 12 + f)
 
 
 def last_kernel(
-    idx, basis, s, r0, r1, u1, rhs, invd, rx0, rx1, ry0, ry1, out_hbm, out, own, ringx, ringy, ex, ey, work, sems
+    basis, s, r0, r1, u1, rhs, invd, rx0, rx1, ry0, ry1, out_hbm, out, own, ringx, ringy, ex, ey, work, sems
 ):
     even_x, even_y = sublane_bits()
-    par_x = is_even(idx, 0)
-    combine_outer(idx, 0, even_x, rx0, rx1, FACE, 16, 2, ex)
-    combine_outer(idx, 1, even_y, ry0, ry1, FACE, 24, 1, ey)
-
-    def total(x, y, f):
-        n = ((x % 2) * 4 + y) * 4 + f
-        a, b = r0[n], r1[n]
-        if x < 2:
-            a, b = b, a
-        return s[(x * 4 + y) * 4 + f] + jnp.where(par_x, a, b)
+    par_x = is_even("px")
+    combine_outer("px", even_x, rx0, rx1, FACE, 0, 2, ex)
+    combine_outer("py", even_y, ry0, ry1, FACE, 24, 1, ey)
+
+    def received(x, n):
+        a, b = (r0[n], r1[n]) if x else (r1[n], r0[n])
+        return jnp.where(par_x, a, b)
 
     for f in range(4):
         for x in (0, 1):
+            edge_y, edge_x = received(x, 8 + f), received(x, 12 + f)
             for y in (0, 1):
                 rows = pl.ds((f * 4 + x * 2 + y) * 8, 8)
-                own[rows, :] = total(x + 1, y + 1, f)
-                ringx[rows, :] = total(3 if x else 0, y + 1, f)
-                ringy[rows, :] = total(x + 1, 3 if y else 0, f)
+                own[rows, :] = s[at_ring(x + 1, y + 1, f)] + received(x, y * 4 + f)
+                far = edge_x if x != y else (down(edge_x, 4) if x else up(edge_x, 4))
+                ringx[rows, :] = s[at_ring(3 if x else 0, y + 1, f)] + far
+                ringy[rows, :] = s[at_ring(x + 1, 3 if y else 0, f)] + edge_y
 
     def pair(g, carry):
         def take(ref, n):
@@ -604,48 +646,49 @@
                 out[g, at] = KEPT * out[g, at] + DAMPING * vals[n]
 
         smooth(load, finish, basis, invd, work)
+        for c in put_out(g):
+            c.start()
         return carry
 
+    def put_out(g):
+        half = SUB // 2
+        for f in (0, 1):
+            src = out.at[g, :, pl.ds(half * f, half), :]
+            yield pltpu.make_async_copy(src, out_hbm.at[2 * g + f], sems.at[2 * g + f])
+
     lax.fori_loop(0, 2, pair, 0)
-    copies = []
-    for f in range(out_hbm.shape[0]):
-        half = SUB // 2
-        src = out.at[f // 2, :, pl.ds(half * (f % 2), half), :]
-        copies.append(pltpu.make_async_copy(src, out_hbm.at[f], sems.at[f]))
-    for c in copies:
-        c.start()
-    for c in copies:
+    for c in [c for g in range(2) for c in put_out(g)]:
         c.wait()
 
 
-SMEM = pl.BlockSpec(memory_space=pltpu.SMEM)
 VMEM = pl.BlockSpec(memory_space=pltpu.VMEM)
-ANY = pl.BlockSpec(memory_space=pl.ANY)
+HBM = pl.BlockSpec(memory_space=pltpu.HBM)
 
 
 def regs(*lead):
     return jax.ShapeDtypeStruct((*lead, SUB, LANES), F32)
 
 
-def call(kernel, ins, outs, out_specs, scratch=(), limit=24):
+def call(kernel, ins, outs, out_specs, scratch=(), limit=24, aliases=None):
     return pl.pallas_call(
         kernel,
         in_specs=ins,
         out_specs=out_specs,
         out_shape=outs,
         scratch_shapes=scratch,
+        input_output_aliases=aliases or {},
         compiler_params=pltpu.CompilerParams(vmem_limit_bytes=limit << 20),
     )
 
 
 def swaps(axis, m0, m1):
     peers = lax.axis_size(axis)
-    got = []
-    for colour, m in enumerate((m0, m1)):
+    got = [None, None]
+    for colour in (1, 0):
         pairs = []
         for i in range(colour, peers - 1, 2):
             pairs += [(i, i + 1), (i + 1, i)]
-        got.append(lax.ppermute(m, axis, pairs))
+        got[colour] = lax.ppermute((m0, m1)[colour], axis, pairs)
     return got
 
 
@@ -655,47 +698,57 @@
     fields, _, _, _, span_x, span_y, layers = right_side.shape
     rows_all = span_y * lax.axis_size("py")
     flat = (fields, CUBE, span_x * span_y, layers)
-    idx = jnp.stack([lax.axis_index("px"), lax.axis_index("py")]).astype(jnp.int32)
-    coef = coefficient.reshape(span_x * span_y, layers)
-    coef = jnp.concatenate([coef, coef], axis=0)
     field_sems = pltpu.SemaphoreType.DMA((fields,))
 
-    u, fx0, fx1, fy0, fy1 = call(
-        faces_kernel, [SMEM, ANY], [regs(2, CUBE)] + [regs(FACE)] * 4, [VMEM] * 5, [field_sems]
-    )(idx, first_guess.reshape(flat))
+    stay = functools.partial(pltpu.with_memory_space_constraint, memory_space=pltpu.HBM)
+    few = (modal_basis, modal_values.reshape(1, NODES), coefficient.reshape(span_x * span_y, layers))
+    u, *few, fx0, fx1, fy0, fy1 = call(
+        faces_kernel,
+        [HBM] * 4,
+        [
+            regs(2, CUBE),
+            jax.ShapeDtypeStruct((NODES, NODES), F32),
+            jax.ShapeDtypeStruct((1, NODES), F32),
+            regs(),
+            *[regs(FACE)] * 4,
+        ],
+        [VMEM] * 8,
+        [field_sems, pltpu.SemaphoreType.DMA((4,))],
+    )(*[stay(v) for v in (first_guess.reshape(flat), *few)])
     fx = swaps("px", fx0, fx1)
     fy = swaps("py", fy0, fy1)
-    rhs, w, crd, invd = call(
+    rhs, w, crd, invd, basis = call(
         local_kernel,
-        [SMEM, SMEM, VMEM, VMEM, ANY],
-        [regs(2, CUBE), regs(2, CUBE), regs(2, 8), regs(len(TRIPLES))],
-        [VMEM] * 4,
-        [field_sems],
-    )(modal_basis, modal_values, u, coef, right_side.reshape(flat))
+        [VMEM, VMEM, VMEM, VMEM, HBM],
+        [regs(2, CUBE), regs(2, CUBE), regs(2, 8), regs(len(TRIPLES)), regs(FACE)],
+        [VMEM] * 5,
+        [pltpu.VMEM((2 * NODES, SUB, LANES), F32), field_sems],
+    )(*few, u, right_side.reshape(flat))
     outer = pltpu.VMEM((2, FACE, SUB, LANES), F32)
     work = pltpu.VMEM((CUBE, SUB, LANES), F32)
-    u1, c0, xpk, yf, yface, mx0, mx1 = call(
+    u1, c0, xpk, yf, ux0, ux1, my0, my1, mx0, mx1 = call(
         first_kernel,
-        [SMEM, SMEM] + [VMEM] * 8,
-        [regs(2, CUBE), regs(2, 8), regs(2, 4), regs(2, 4), regs(2, FACE), regs(16 + FACE), regs(16 + FACE)],
+        [VMEM] * 9,
+        [regs(2, CUBE), regs(2, 8), regs(2, 4), regs(2, 4)] + [regs(n) for n in (FACE, 24 + FACE, 16) for _ in (0, 1)],
+        [VMEM] * 10,
+        [outer, outer, work],
+    )(basis, *fx, *fy, u, w, crd, invd)
+    rx = swaps("px", mx0, mx1)
+    c1, ring, ypk, my0, my1 = call(
+        middle_kernel,
         [VMEM] * 7,
-        [outer, outer, work],
-    )(idx, modal_basis, *fx, *fy, u, w, crd, invd)
-    rx = swaps("px", mx0, mx1)
-    c1, ring, _, ypk, my0, my1 = call(
-        middle_kernel,
-        [SMEM] + [VMEM] * 6,
-        [regs(2, 8), regs(2, 8), regs(2, 4), regs(2, 2, 4), regs(24 + FACE), regs(24 + FACE)],
-        [VMEM] * 6,
-    )(idx, *rx, c0, xpk, yf, yface)
+        [regs(2, 8), regs(2, 8), regs(2, 2, 4), regs(24 + FACE), regs(24 + FACE)],
+        [VMEM] * 5,
+        aliases={5: 3, 6: 4},
+    )(*rx, c0, xpk, yf, my0, my1)
     ry = swaps("py", my0, my1)
+    ux = swaps("px", ux0, ux1)
     rows = patch_elements.shape[0]
-    slots = patch_elements.shape[1]
     width = patch_inverse.shape[0]
-    v, v0, v1 = call(
+    patches = call(
         functools.partial(patch_kernel, rows_all, (span_x, span_y, layers)),
-        [SMEM] + [VMEM] * 8,
-        [regs(64), regs(32), regs(32)],
+        [VMEM] * 8,
+        [regs(64), regs(24), regs(24)],
         [VMEM] * 3,
         [
             pltpu.VMEM((512, LANES), F32),
@@ -704,18 +757,19 @@
             pltpu.VMEM((1024, rows), jnp.bfloat16),
             pltpu.VMEM((1024, rows), jnp.bfloat16),
         ],
-    )(idx, *ry, c1, ring, ypk, patch_elements.T, patch_mask.T, patch_inverse)
+    )
+    v, v0, v1 = patches(*ry, c1, ring, ypk, patch_elements.T, patch_mask.T, patch_inverse)
     rv = swaps("py", v0, v1)
-    s, m0, m1 = call(sum_kernel, [SMEM] + [VMEM] * 3, [regs(64), regs(32), regs(32)], [VMEM] * 3)(idx, v, *rv)
+    s, m0, m1 = call(sum_kernel, [VMEM] * 3, [regs(64), regs(16), regs(16)], [VMEM] * 3)(v, *rv)
     rs = swaps("px", m0, m1)
     table = pltpu.VMEM((128, LANES), F32)
     out = call(
         last_kernel,
-        [SMEM, SMEM] + [VMEM] * 10,
+        [VMEM] * 11,
         jax.ShapeDtypeStruct(flat, F32),
-        ANY,
+        HBM,
         [pltpu.VMEM((2, CUBE, SUB, LANES), F32), table, table, table, outer, outer, work, field_sems],
-    )(idx, modal_basis, s, *rs, u1, rhs, invd, *rx, *ry)
+    )(basis, s, *rs, u1, rhs, invd, *ux, *ry)
     return out.reshape(right_side.shape)
 
 
@@ -731,6 +785,5 @@
         P(("px", "py"), None),
     )
     out_specs = P(None, None, None, None, "px", "py", None)
-    return jax.shard_map(
-        per_device, mesh=mesh, in_specs=in_specs, out_specs=out_specs, check_vma=False
-    )
+
+    return jax.shard_map(per_device, mesh=mesh, in_specs=in_specs, out_specs=out_specs, check_vma=False)

time: 58.5 us -> 53 us (0.906); the launches traced: 58.2 us -> 52.1 us
  waiting for transfers between devices: 22.4 us -> 16.3 us
  starting transfers between devices: 17.5 us -> 22.8 us
  Pallas kernels: 16.1 us -> 12.8 us
  local copies, waits for them, and re-layouts: 1.89 us -> 0.01 us
    ppermute x12 -> x14, waiting for transfers between devices: 22.4 us -> 16.3 us  [swaps(): got[colour] = lax.ppermute((m0, m1)[colour], axis, pairs)]
    ppermute x12 -> x14, starting transfers between devices: 17.5 us -> 22.8 us  [swaps(): got[colour] = lax.ppermute((m0, m1)[colour], axis, pairs)]
    pallas_call x7, Pallas kernels: 16.1 us -> 12.8 us  [the longest x1 4.29 us: per_device(): patches(*ry, c1, ring, ypk, patch_elements.T, patch_mask.T, patch_inverse)]
    unnamed x16 -> x8, local copies, waits for them, and re-layouts: 1.89 us -> 0.01 us
  transfers between devices with their start and end apart: 12 -> 14, of which waited for: 6 -> 6; matrix products, arithmetic and copies ran while one was open for 0% -> 0% of each run, Pallas kernels for 3% -> 2%
where the time goes in v1:
time: 53 us; the launch traced here: 52.1 us
  starting transfers between devices  22.8 us (43%)
  waiting for transfers between devices  16.3 us (31%)
  Pallas kernels  12.8 us (24%)
    ppermute x14, starting transfers between devices, swaps(): got[colour] = lax.ppermute((m0, m1)[colour], axis, pairs)  22.8 us
    ppermute x14, waiting for transfers between devices, swaps(): got[colour] = lax.ppermute((m0, m1)[colour], axis, pairs)  16.3 us
    pallas_call x1, Pallas kernels, per_device(): patches(*ry, c1, ring, ypk, patch_elements.T, patch_mask.T, patch_inverse)  4.29 us
    pallas_call x1, Pallas kernels, per_device(): call(last_kernel, [VMEM] * 11, jax.ShapeDtypeStruct(flat, F32), HBM, [plt...  3.27 us
    pallas_call x1, Pallas kernels, per_device(): call(first_kernel, [VMEM] * 9, [regs(2, CUBE), regs(2, 8), regs(2, 4), re...  2.37 us
    pallas_call x1, Pallas kernels, per_device(): call(faces_kernel, [HBM] * 4, [regs(2, CUBE), jax.ShapeDtypeStruct((NODES...  1.57 us
    pallas_call x1, Pallas kernels, per_device(): call(local_kernel, [VMEM, VMEM, VMEM, VMEM, HBM], [regs(2, CUBE), regs(2,...  1.2 us
  transfers between devices with their start and end apart: 14, of which 6 were waited for; matrix products, arithmetic and copies ran while one was open for 0% of the time, Pallas kernels for 2%

profile of v1, /device:TPU:22, one launch (start us, length us, event | category | flops | bytes accessed | tf_op | source)
XLA Modules:
  0.0 52.1 jit_solution(7997257099783801817)
XLA Ops:
  0.0 1.6 %shard_map.82 = (f32[2,125,8,128]{3,2,1,0:T(8,128)S(1)}, f32[5,5]{1,0:T(8,128)S(1)}, f32[1,5]{1,0:T(1,128)S(1)}, f32[8,128]{1,0:T(8,128)S(1)}, f32[25,8,128]{2,1...) custom-call(f32[4,125,4,128]{3,2,1,0:T(4,128)} %bitcast.10, ...), custom_call_target="tpu_custom_call" | custom-call | tf_op jit(solution)/shard_map/pallas_call | solution.py:705
  1.6 0.6 %collective-permute-start = (f32[25,8,128]{2,1,0:T(8,128)S(1)}, f32[25,8,128]{2,1,0:T(8,128)S(1)}, u32[]{:S(2)}, u32[]{:S(2)}) collective-permute-start(f32[25,8,128]{2,1,0:T(8,128)S(1)} %get-tuple-element.44), channel_id=1, source_target_pairs={{0,4},{4,0},{8,12},{12,8},{16,20},{20,16},{24,28},{28,24},{1,5},{5... | collective-permute-start | bytes 307208 | tf_op jit(solution)/shard_map/ppermute | solution.py:691
  2.2 4.4 %collective-permute-start.1 = (f32[25,8,128]{2,1,0:T(8,128)S(1)}, f32[25,8,128]{2,1,0:T(8,128)S(1)}, u32[]{:S(2)}, u32[]{:S(2)}) collective-permute-start(f32[25,8,128]{2,1,0:T(8,128)S(1)} %get-tuple-element.45), channel_id=1, source_target_pairs={{4,8},{8,4},{12,16},{16,12},{20,24},{24,20},{5,9},{9,5},{13,17},{1... | collective-permute-start | bytes 307208 | tf_op jit(solution)/shard_map/ppermute | solution.py:691
  6.6 0.1 collective-permute-start.2
  6.7 2.5 %collective-permute-start.3 = (f32[25,8,128]{2,1,0:T(8,128)S(1)}, f32[25,8,128]{2,1,0:T(8,128)S(1)}, u32[]{:S(2)}, u32[]{:S(2)}) collective-permute-start(f32[25,8,128]{2,1,0:T(8,128)S(1)} %get-tuple-element.47), channel_id=1, source_target_pairs={{1,2},{2,1},{5,6},{6,5},{9,10},{10,9},{13,14},{14,13},{17,18},{18,... | collective-permute-start | bytes 307208 | tf_op jit(solution)/shard_map/ppermute | solution.py:691
  9.2 1.2 %shard_map.83 = (f32[2,125,8,128]{3,2,1,0:T(8,128)S(1)}, f32[2,125,8,128]{3,2,1,0:T(8,128)S(1)}, f32[2,8,8,128]{3,2,1,0:T(8,128)S(1)}, f32[35,8,128]{2,1,0:T(8,128)S(1)}, f32[25,8,128]{2,1,0:T(8,128)S(1)}) custom-call(f32[5,5]{1,0:T(8,128)S(1)} %get-tuple-element.39.basis_in, f32[1,5]{1,0:T(1,128)S(1)} %get-tuple-element.40.lam_in, ...), custom_call_target="tpu_custom_call" | custom-call | tf_op jit(solution)/shard_map/pallas_call | solution.py:720
  10.4 0.0 collective-permute-done.fx0
  10.4 0.0 collective-permute-done.1.fx1
  10.4 0.0 collective-permute-done.2.fy0
  10.5 2.2 %collective-permute-done.3.fy1 = f32[25,8,128]{2,1,0:T(8,128)S(1)} collective-permute-done((f32[25,8,128]{2,1,0:T(8,128)S(1)}, f32[25,8,128]{2,1,0:T(8,128)S(1)}, u32[]{:S(2)}, u32[]{:S(2)}) %collective-permute-start.3) | collective-permute-done | bytes 102432 | tf_op jit(solution)/shard_map/ppermute | solution.py:691
  12.6 2.4 %shard_map.84 = (f32[2,125,8,128]{3,2,1,0:T(8,128)S(1)}, f32[2,8,8,128]{3,2,1,0:T(8,128)S(1)}, f32[2,4,8,128]{3,2,1,0:T(8,128)S(1)}, f32[2,4,8,128]{3,2,1,0:T(8,...) custom-call(f32[25,8,128]{2,1,0:T(8,128)S(1)} %get-tuple-element.43., ...), custom_call_target="tpu_custom_call" | custom-call | tf_op jit(solution)/shard_map/pallas_call | solution.py:729
  15.0 0.1 collective-permute-start.4
  15.1 2.3 %collective-permute-start.5 = (f32[16,8,128]{2,1,0:T(8,128)S(1)}, f32[16,8,128]{2,1,0:T(8,128)S(1)}, u32[]{:S(2)}, u32[]{:S(2)}) collective-permute-start(f32[16,8,128]{2,1,0:T(8,128)S(1)} %get-tuple-element.52), channel_id=1, source_target_pairs={{4,8},{8,4},{12,16},{16,12},{20,24},{24,20},{5,9},{9,5},{13,17},{1... | collective-permute-start | bytes 196616 | tf_op jit(solution)/shard_map/ppermute | solution.py:691
  17.4 1.9 %collective-permute-done.4.rx0 = f32[16,8,128]{2,1,0:T(8,128)S(1)} collective-permute-done((f32[16,8,128]{2,1,0:T(8,128)S(1)}, f32[16,8,128]{2,1,0:T(8,128)S(1)}, u32[]{:S(2)}, u32[]{:S(2)}) %collective-permute-start.4) | collective-permute-done | bytes 65568 | tf_op jit(solution)/shard_map/ppermute | solution.py:691
  19.4 2.8 %collective-permute-done.5.rx1 = f32[16,8,128]{2,1,0:T(8,128)S(1)} collective-permute-done((f32[16,8,128]{2,1,0:T(8,128)S(1)}, f32[16,8,128]{2,1,0:T(8,128)S(1)}, u32[]{:S(2)}, u32[]{:S(2)}) %collective-permute-start.5) | collective-permute-done | bytes 65568 | tf_op jit(solution)/shard_map/ppermute | solution.py:691
  22.2 0.1 collective-permute-start.6
  22.3 1.9 %collective-permute-start.7 = (f32[49,8,128]{2,1,0:T(8,128)S(1)}, f32[49,8,128]{2,1,0:T(8,128)S(1)}, u32[]{:S(2)}, u32[]{:S(2)}) collective-permute-start(f32[49,8,128]{2,1,0:T(8,128)S(1)} %get-tuple-element.59), channel_id=1, source_target_pairs={{1,2},{2,1},{5,6},{6,5},{9,10},{10,9},{13,14},{14,13},{17,18},{18,... | collective-permute-start | bytes 602120 | tf_op jit(solution)/shard_map/ppermute | solution.py:691
  24.2 0.0 collective-permute-done.6.ry0
  24.2 5.1 %collective-permute-done.7.ry1 = f32[49,8,128]{2,1,0:T(8,128)S(1)} collective-permute-done((f32[49,8,128]{2,1,0:T(8,128)S(1)}, f32[49,8,128]{2,1,0:T(8,128)S(1)}, u32[]{:S(2)}, u32[]{:S(2)}) %collective-permute-start.7) | collective-permute-done | bytes 200736 | tf_op jit(solution)/shard_map/ppermute | solution.py:691
  29.3 4.3 %shard_map.86 = (f32[64,8,128]{2,1,0:T(8,128)S(1)}, f32[24,8,128]{2,1,0:T(8,128)S(1)}, f32[24,8,128]{2,1,0:T(8,128)S(1)}) custom-call(f32[49,8,128]{2,1,0:T(8,128)S(1)} %collective-permute-done.6.ry0, f32[49,8,128]{2,1,0:T(8,128)S(1)} %collective-permute-done.7.ry1, f32[2,8,8,128]{3,2,1,0:T(8,128)S(1)} %get-tuple-element.60.c1, ...), custom_call_target="tpu_custom_call" | custom-call | tf_op jit(solution)/shard_map/pallas_call | solution.py:761
  33.6 0.1 collective-permute-start.8
  33.7 1.9 %collective-permute-start.9 = (f32[24,8,128]{2,1,0:T(8,128)S(1)}, f32[24,8,128]{2,1,0:T(8,128)S(1)}, u32[]{:S(2)}, u32[]{:S(2)}) collective-permute-start(f32[24,8,128]{2,1,0:T(8,128)S(1)} %get-tuple-element.65), channel_id=1, source_target_pairs={{1,2},{2,1},{5,6},{6,5},{9,10},{10,9},{13,14},{14,13},{17,18},{18,... | collective-permute-start | bytes 294920 | tf_op jit(solution)/shard_map/ppermute | solution.py:691
  35.6 2.1 %collective-permute-start.12 = (f32[25,8,128]{2,1,0:T(8,128)S(1)}, f32[25,8,128]{2,1,0:T(8,128)S(1)}, u32[]{:S(2)}, u32[]{:S(2)}) collective-permute-start(f32[25,8,128]{2,1,0:T(8,128)S(1)} %get-tuple-element.71), channel_id=1, source_target_pairs={{0,4},{4,0},{8,12},{12,8},{16,20},{20,16},{24,28},{28,24},{1,5},{5... | collective-permute-start | bytes 307208 | tf_op jit(solution)/shard_map/ppermute | solution.py:691
  37.7 1.9 %collective-permute-start.13 = (f32[25,8,128]{2,1,0:T(8,128)S(1)}, f32[25,8,128]{2,1,0:T(8,128)S(1)}, u32[]{:S(2)}, u32[]{:S(2)}) collective-permute-start(f32[25,8,128]{2,1,0:T(8,128)S(1)} %get-tuple-element.72), channel_id=1, source_target_pairs={{4,8},{8,4},{12,16},{16,12},{20,24},{24,20},{5,9},{9,5},{13,17},{1... | collective-permute-start | bytes 307208 | tf_op jit(solution)/shard_map/ppermute | solution.py:691
  39.6 0.0 collective-permute-done.8.r0
  39.6 0.0 collective-permute-done.9.r1
  39.7 2.1 %collective-permute-start.10 = (f32[16,8,128]{2,1,0:T(8,128)S(1)}, f32[16,8,128]{2,1,0:T(8,128)S(1)}, u32[]{:S(2)}, u32[]{:S(2)}) collective-permute-start(f32[16,8,128]{2,1,0:T(8,128)S(1)} %get-tuple-element.67), channel_id=1, source_target_pairs={{0,4},{4,0},{8,12},{12,8},{16,20},{20,16},{24,28},{28,24},{1,5},{5... | collective-permute-start | bytes 196616 | tf_op jit(solution)/shard_map/ppermute | solution.py:691
  41.8 2.8 %collective-permute-start.11 = (f32[16,8,128]{2,1,0:T(8,128)S(1)}, f32[16,8,128]{2,1,0:T(8,128)S(1)}, u32[]{:S(2)}, u32[]{:S(2)}) collective-permute-start(f32[16,8,128]{2,1,0:T(8,128)S(1)} %get-tuple-element.68), channel_id=1, source_target_pairs={{4,8},{8,4},{12,16},{16,12},{20,24},{24,20},{5,9},{9,5},{13,17},{1... | collective-permute-start | bytes 196616 | tf_op jit(solution)/shard_map/ppermute | solution.py:691
  44.6 0.5 %collective-permute-done.13.rx1 = f32[25,8,128]{2,1,0:T(8,128)S(1)} collective-permute-done((f32[25,8,128]{2,1,0:T(8,128)S(1)}, f32[25,8,128]{2,1,0:T(8,128)S(1)}, u32[]{:S(2)}, u32[]{:S(2)}) %collective-permute-start.13) | collective-permute-done | bytes 102432 | tf_op jit(solution)/shard_map/ppermute | solution.py:691
  45.1 0.0 collective-permute-done.10.r0
  45.2 3.7 %collective-permute-done.11.r1 = f32[16,8,128]{2,1,0:T(8,128)S(1)} collective-permute-done((f32[16,8,128]{2,1,0:T(8,128)S(1)}, f32[16,8,128]{2,1,0:T(8,128)S(1)}, u32[]{:S(2)}, u32[]{:S(2)}) %collective-permute-start.11) | collective-permute-done | bytes 65568 | tf_op jit(solution)/shard_map/ppermute | solution.py:691
  48.8 3.3 %shard_map.88 = f32[4,125,4,128]{3,2,1,0:T(4,128)} custom-call(f32[25,8,128]{2,1,0:T(8,128)S(1)} %get-tuple-element.43.basis, f32[64,8,128]{2,1,0:T(8,128)S(1)} %get-tuple-element.66.s, f32[16,8,128]{2,1,0:T(8,128)S(1)} %collective-permute-done.10.r0, f32[16,8,128]{2,1,0:T(8,128)S(1)} %collective-permute-done.11.r1, ...), custom_call_target="tpu_custom_call" | custom-call | tf_op jit(solution)/shard_map/pallas_call | solution.py:766
  (11 shorter events, 0.1 us)
Async XLA Ops:
  0.0 9.2 %copy-start = (f32[4,5,5,5,2,2,128]{6,5,4,3,2,1,0:T(2,128)S(1)}, f32[4,5,5,5,2,2,128]{6,5,4,3,2,1,0:T(2,128)}, u32[]{:S(2)}) copy-start(f32[4,5,5,5,2,2,128]{6,5,4,3,2,1,0:T(2,128)} %param.8) | copy-start | bytes 3072004
  1.6 8.9 %collective-permute-start = (f32[25,8,128]{2,1,0:T(8,128)S(1)}, f32[25,8,128]{2,1,0:T(8,128)S(1)}, u32[]{:S(2)}, u32[]{:S(2)}) collective-permute-start(f32[25,8,128]{2,1,0:T(8,128)S(1)} %get-tuple-element.44), channel_id=1, source_target_pairs={{0,4},{4,0},{8,12},{12,8},{16,20},{20,16},{24,28},{28,24},{1,5},{5... | collective-permute-start | bytes 307208 | tf_op jit(solution)/shard_map/ppermute | solution.py:691
  2.2 8.3 %collective-permute-start.1 = (f32[25,8,128]{2,1,0:T(8,128)S(1)}, f32[25,8,128]{2,1,0:T(8,128)S(1)}, u32[]{:S(2)}, u32[]{:S(2)}) collective-permute-start(f32[25,8,128]{2,1,0:T(8,128)S(1)} %get-tuple-element.45), channel_id=1, source_target_pairs={{4,8},{8,4},{12,16},{16,12},{20,24},{24,20},{5,9},{9,5},{13,17},{1... | collective-permute-start | bytes 307208 | tf_op jit(solution)/shard_map/ppermute | solution.py:691
  6.6 3.9 %collective-permute-start.2 = (f32[25,8,128]{2,1,0:T(8,128)S(1)}, f32[25,8,128]{2,1,0:T(8,128)S(1)}, u32[]{:S(2)}, u32[]{:S(2)}) collective-permute-start(f32[25,8,128]{2,1,0:T(8,128)S(1)} %get-tuple-element.46), channel_id=1, source_target_pairs={{0,1},{1,0},{2,3},{3,2},{4,5},{5,4},{6,7},{7,6},{8,9},{9,8},{10,11... | collective-permute-start | bytes 307208 | tf_op jit(solution)/shard_map/ppermute | solution.py:691
  6.7 6.0 %collective-permute-start.3 = (f32[25,8,128]{2,1,0:T(8,128)S(1)}, f32[25,8,128]{2,1,0:T(8,128)S(1)}, u32[]{:S(2)}, u32[]{:S(2)}) collective-permute-start(f32[25,8,128]{2,1,0:T(8,128)S(1)} %get-tuple-element.47), channel_id=1, source_target_pairs={{1,2},{2,1},{5,6},{6,5},{9,10},{10,9},{13,14},{14,13},{17,18},{18,... | collective-permute-start | bytes 307208 | tf_op jit(solution)/shard_map/ppermute | solution.py:691
  15.0 4.3 %collective-permute-start.4 = (f32[16,8,128]{2,1,0:T(8,128)S(1)}, f32[16,8,128]{2,1,0:T(8,128)S(1)}, u32[]{:S(2)}, u32[]{:S(2)}) collective-permute-start(f32[16,8,128]{2,1,0:T(8,128)S(1)} %get-tuple-element.51), channel_id=1, source_target_pairs={{0,4},{4,0},{8,12},{12,8},{16,20},{20,16},{24,28},{28,24},{1,5},{5... | collective-permute-start | bytes 196616 | tf_op jit(solution)/shard_map/ppermute | solution.py:691
  15.1 7.1 %collective-permute-start.5 = (f32[16,8,128]{2,1,0:T(8,128)S(1)}, f32[16,8,128]{2,1,0:T(8,128)S(1)}, u32[]{:S(2)}, u32[]{:S(2)}) collective-permute-start(f32[16,8,128]{2,1,0:T(8,128)S(1)} %get-tuple-element.52), channel_id=1, source_target_pairs={{4,8},{8,4},{12,16},{16,12},{20,24},{24,20},{5,9},{9,5},{13,17},{1... | collective-permute-start | bytes 196616 | tf_op jit(solution)/shard_map/ppermute | solution.py:691
  22.2 7.2 %copy-start.1 = (f32[256,256]{1,0:T(8,128)S(1)}, f32[256,256]{1,0:T(8,128)}, u32[]{:S(2)}) copy-start(f32[256,256]{1,0:T(8,128)} %inverse.1) | copy-start | bytes 786436
  22.2 7.2 %copy-start.2 = (s32[512,8]{0,1:T(8,128)S(1)}, s32[512,8]{0,1:T(8,128)}, u32[]{:S(2)}) copy-start(s32[512,8]{0,1:T(8,128)} %param.14) | copy-start | bytes 49156
  22.2 7.2 %copy-start.3 = (s32[512,8]{0,1:T(8,128)S(1)}, s32[512,8]{0,1:T(8,128)}, u32[]{:S(2)}) copy-start(s32[512,8]{0,1:T(8,128)} %param.15) | copy-start | bytes 49156
  22.2 2.0 %collective-permute-start.6 = (f32[49,8,128]{2,1,0:T(8,128)S(1)}, f32[49,8,128]{2,1,0:T(8,128)S(1)}, u32[]{:S(2)}, u32[]{:S(2)}) collective-permute-start(f32[49,8,128]{2,1,0:T(8,128)S(1)} %get-tuple-element.58), channel_id=1, source_target_pairs={{0,1},{1,0},{2,3},{3,2},{4,5},{5,4},{6,7},{7,6},{8,9},{9,8},{10,11... | collective-permute-start | bytes 602120 | tf_op jit(solution)/shard_map/ppermute | solution.py:691
  22.3 7.0 %collective-permute-start.7 = (f32[49,8,128]{2,1,0:T(8,128)S(1)}, f32[49,8,128]{2,1,0:T(8,128)S(1)}, u32[]{:S(2)}, u32[]{:S(2)}) collective-permute-start(f32[49,8,128]{2,1,0:T(8,128)S(1)} %get-tuple-element.59), channel_id=1, source_target_pairs={{1,2},{2,1},{5,6},{6,5},{9,10},{10,9},{13,14},{14,13},{17,18},{18,... | collective-permute-start | bytes 602120 | tf_op jit(solution)/shard_map/ppermute | solution.py:691
  33.6 6.0 %collective-permute-start.8 = (f32[24,8,128]{2,1,0:T(8,128)S(1)}, f32[24,8,128]{2,1,0:T(8,128)S(1)}, u32[]{:S(2)}, u32[]{:S(2)}) collective-permute-start(f32[24,8,128]{2,1,0:T(8,128)S(1)} %get-tuple-element.64), channel_id=1, source_target_pairs={{0,1},{1,0},{2,3},{3,2},{4,5},{5,4},{6,7},{7,6},{8,9},{9,8},{10,11... | collective-permute-start | bytes 294920 | tf_op jit(solution)/shard_map/ppermute | solution.py:691
  33.7 5.9 %collective-permute-start.9 = (f32[24,8,128]{2,1,0:T(8,128)S(1)}, f32[24,8,128]{2,1,0:T(8,128)S(1)}, u32[]{:S(2)}, u32[]{:S(2)}) collective-permute-start(f32[24,8,128]{2,1,0:T(8,128)S(1)} %get-tuple-element.65), channel_id=1, source_target_pairs={{1,2},{2,1},{5,6},{6,5},{9,10},{10,9},{13,14},{14,13},{17,18},{18,... | collective-permute-start | bytes 294920 | tf_op jit(solution)/shard_map/ppermute | solution.py:691
  35.6 9.0 %collective-permute-start.12 = (f32[25,8,128]{2,1,0:T(8,128)S(1)}, f32[25,8,128]{2,1,0:T(8,128)S(1)}, u32[]{:S(2)}, u32[]{:S(2)}) collective-permute-start(f32[25,8,128]{2,1,0:T(8,128)S(1)} %get-tuple-element.71), channel_id=1, source_target_pairs={{0,4},{4,0},{8,12},{12,8},{16,20},{20,16},{24,28},{28,24},{1,5},{5... | collective-permute-start | bytes 307208 | tf_op jit(solution)/shard_map/ppermute | solution.py:691
  37.7 7.4 %collective-permute-start.13 = (f32[25,8,128]{2,1,0:T(8,128)S(1)}, f32[25,8,128]{2,1,0:T(8,128)S(1)}, u32[]{:S(2)}, u32[]{:S(2)}) collective-permute-start(f32[25,8,128]{2,1,0:T(8,128)S(1)} %get-tuple-element.72), channel_id=1, source_target_pairs={{4,8},{8,4},{12,16},{16,12},{20,24},{24,20},{5,9},{9,5},{13,17},{1... | collective-permute-start | bytes 307208 | tf_op jit(solution)/shard_map/ppermute | solution.py:691
  39.7 5.4 %collective-permute-start.10 = (f32[16,8,128]{2,1,0:T(8,128)S(1)}, f32[16,8,128]{2,1,0:T(8,128)S(1)}, u32[]{:S(2)}, u32[]{:S(2)}) collective-permute-start(f32[16,8,128]{2,1,0:T(8,128)S(1)} %get-tuple-element.67), channel_id=1, source_target_pairs={{0,4},{4,0},{8,12},{12,8},{16,20},{20,16},{24,28},{28,24},{1,5},{5... | collective-permute-start | bytes 196616 | tf_op jit(solution)/shard_map/ppermute | solution.py:691
  41.8 7.0 %collective-permute-start.11 = (f32[16,8,128]{2,1,0:T(8,128)S(1)}, f32[16,8,128]{2,1,0:T(8,128)S(1)}, u32[]{:S(2)}, u32[]{:S(2)}) collective-permute-start(f32[16,8,128]{2,1,0:T(8,128)S(1)} %get-tuple-element.68), channel_id=1, source_target_pairs={{4,8},{8,4},{12,16},{16,12},{20,24},{24,20},{5,9},{9,5},{13,17},{1... | collective-permute-start | bytes 196616 | tf_op jit(solution)/shard_map/ppermute | solution.py:691

commit v2 on v1

--- a/solution.py
+++ b/solution.py
@@ -487,62 +487,98 @@
         x = quotient(column_of, rows_all)
         y = column_of - x * rows_all - (lax.axis_index("py") * span_y - 1)
         x = x - (lax.axis_index("px") * span_x - 1)
-        least = jnp.min(jnp.where(live, z, layers - 1), axis=0, keepdims=True)
-        code = (z - least) * 16 + x * 4 + y
-        return at, jnp.where(live, code, -1), jnp.where(live, 1.0, 0.0), least
+        lx, ly, lz = [
+            jnp.min(jnp.where(live, v, top), axis=0, keepdims=True) for v, top in ((x, 3), (y, 3), (z, layers - 1))
+        ]
+        place = (x - lx) * 4 + (y - ly) * 2 + (z - lz)
+        corner = [jnp.broadcast_to(v, (SUB, LANES)) for v in (lx, ly, lz)]
+        return jnp.where(live, place, -1), jnp.where(live, 1.0, 0.0), corner
+
+    def row(v, s):
+        return jnp.broadcast_to(v[s : s + 1], (SUB, LANES))
+
+    def two_of_four(v, bit0, bit1):
+        near = jnp.where(bit1, jnp.where(bit0, v[3], v[2]), jnp.where(bit0, v[1], v[0]))
+        return near, jnp.where(bit1, v[3], jnp.where(bit0, v[2], v[1]))
 
     def gather(rg, carry):
-        _, code, alive, least = codes(rg)
-        z0 = jnp.broadcast_to(least, (SUB, LANES))
+        place, alive, (lx, ly, z0) = codes(rg)
         z1 = jnp.minimum(z0 + 1, layers - 1)
+        x_bits = (lx & 1) != 0, (lx & 2) != 0
+        y_bits = (ly & 1) != 0, (ly & 2) != 0
         for f in range(4):
-            picks = []
-            for z in (z0, z1):
-                for x in range(4):
-                    for y in range(4):
-                        block = table[pl.ds(block_of(x, y, f) * 8, 8), :]
-                        picks.append(jnp.take_along_axis(block, z, axis=1, mode="promise_in_bounds"))
+            cube = [None] * 8
+            for dz, z in enumerate((z0, z1)):
+                lines = []
+                for y in range(4):
+                    line = [
+                        jnp.take_along_axis(
+                            table[pl.ds(block_of(x, y, f) * 8, 8), :], z, axis=1, mode="promise_in_bounds"
+                        )
+                        for x in range(4)
+                    ]
+                    lines.append(two_of_four(line, *x_bits))
+                for dx in (0, 1):
+                    pair = two_of_four([lines[y][dx] for y in range(4)], *y_bits)
+                    cube[dx * 4 + dz], cube[dx * 4 + 2 + dz] = pair
             for s in range(8):
-                cs = jnp.broadcast_to(code[s : s + 1], (SUB, LANES))
-                level = picks
-                bit = 1
-                while len(level) > 1:
-                    odd = (cs & bit) != 0
+                ps = row(place, s)
+                level = cube
+                for bit in (1, 2, 4):
+                    odd = (ps & bit) != 0
                     level = [jnp.where(odd, level[2 * m + 1], level[2 * m]) for m in range(len(level) // 2)]
-                    bit *= 2
-                on = jnp.broadcast_to(alive[s : s + 1], (SUB, LANES))
-                gath[pl.ds(rg * width + f * 64 + s, 8, stride=8), :] = level[0] * on
+                gath[pl.ds(rg * width + f * 64 + s, 8, stride=8), :] = level[0] * row(alive, s)
         return carry
 
     lax.fori_loop(0, groups, gather, 0)
+    inv = inverse[...]
     wide = jnp.concatenate([gath[rg * width : (rg + 1) * width, :] for rg in range(groups)], axis=1)
-    solved = jnp.dot(inverse[...], wide, precision=lax.Precision.HIGHEST, preferred_element_type=F32)
+
+    def halves(v):
+        hi = v.astype(jnp.bfloat16)
+        return hi, (v - hi.astype(F32)).astype(jnp.bfloat16)
+
+    (ih, il), (wh, wl) = halves(inv), halves(wide)
+    solved = jnp.dot(ih, wl, preferred_element_type=F32) + jnp.dot(il, wh, preferred_element_type=F32)
+    solved = solved + jnp.dot(ih, wh, preferred_element_type=F32)
     for rg in range(groups):
         answer[rg * width : (rg + 1) * width, :] = solved[:, rg * LANES : (rg + 1) * LANES]
 
     def spread(rg, carry):
-        at, code, _, _ = codes(rg)
-        cs = [jnp.broadcast_to(code[s : s + 1], (SUB, LANES)) for s in range(8)]
-        values = [[answer[pl.ds(rg * width + f * 64 + s, 8, stride=8), :] for f in range(4)] for s in range(8)]
-        for k in range(32):
-            acc = [None] * 4
-            for s in range(8):
-                here = cs[s] == k
-                for f in range(4):
-                    term = jnp.where(here, values[s][f], 0.0)
-                    acc[f] = term if acc[f] is None else acc[f] + term
-            for h in (0, 1):
-                both = jnp.concatenate([acc[2 * h], acc[2 * h + 1]], axis=0)
-                hi = both.astype(jnp.bfloat16)
-                rows = pl.ds(k * 32 + h * 16, 16)
-                e_hi[rows, at] = hi
-                e_lo[rows, at] = (both - hi.astype(F32)).astype(jnp.bfloat16)
+        at = pl.ds(pl.multiple_of(rg * LANES, LANES), LANES)
+        place, _, (lx, ly, _) = codes(rg)
+        ps = [row(place, s) for s in range(8)]
+        x_is = [lx == n for n in range(4)]
+        y_is = [ly == n for n in range(4)]
+
+        def placed(near_is, n, near, far):
+            out = jnp.where(near_is[n - 1], far, 0.0) if n else jnp.zeros((SUB, LANES), F32)
+            return jnp.where(near_is[n], near, out)
+
+        for h in (0, 1):
+            cubes = []
+            for f in (2 * h, 2 * h + 1):
+                values = [answer[pl.ds(rg * width + f * 64 + s, 8, stride=8), :] for s in range(8)]
+                cube = []
+                for p in range(8):
+                    v = jnp.zeros((SUB, LANES), F32)
+                    for s in range(8):
+                        v = jnp.where(ps[s] == p, values[s], v)
+                    cube.append(v)
+                cubes.append(cube)
+            for dz in (0, 1):
+                for x in range(4):
+                    cols = [[placed(x_is, x, c[2 * dy + dz], c[4 + 2 * dy + dz]) for dy in (0, 1)] for c in cubes]
+                    for y in range(4):
+                        both = jnp.concatenate([placed(y_is, y, *col) for col in cols], axis=0)
+                        rows = pl.ds((dz * 16 + x * 4 + y) * 32 + h * 16, 16)
+                        e_hi[rows, at], e_lo[rows, at] = halves(both)
         return carry
 
     lax.fori_loop(0, groups, spread, 0)
     hot = []
     for rg in range(groups):
-        _, _, _, least = codes(rg)
+        least = codes(rg)[2][2][0:1]
         depth = lax.broadcasted_iota(jnp.int32, (LANES, LANES), 0)
         hot.append(jnp.where(depth == jnp.broadcast_to(least, (LANES, LANES)), 1.0, 0.0).astype(jnp.bfloat16))
     hot = jnp.concatenate(hot, axis=1)

time: 53 us -> 51.8 us (0.977)
  Pallas kernels: 12.8 us -> 11.6 us
    pallas_call x1, Pallas kernels: 4.29 us -> 3.08 us  [per_device(): patches(*ry, c1, ring, ypk, patch_elements.T, patch_mask.T, patch_inverse)]
where the time goes in v2:
time: 51.8 us; the launch traced here: 50.9 us
  starting transfers between devices  22.8 us (44%)
  waiting for transfers between devices  16.3 us (31%)
  Pallas kernels  11.6 us (22%)
    ppermute x14, starting transfers between devices, swaps(): got[colour] = lax.ppermute((m0, m1)[colour], axis, pairs)  22.8 us
    ppermute x14, waiting for transfers between devices, swaps(): got[colour] = lax.ppermute((m0, m1)[colour], axis, pairs)  16.3 us
    pallas_call x1, Pallas kernels, per_device(): call(last_kernel, [VMEM] * 11, jax.ShapeDtypeStruct(flat, F32), HBM, [plt...  3.27 us
    pallas_call x1, Pallas kernels, per_device(): patches(*ry, c1, ring, ypk, patch_elements.T, patch_mask.T, patch_inverse)  3.08 us
    pallas_call x1, Pallas kernels, per_device(): call(first_kernel, [VMEM] * 9, [regs(2, CUBE), regs(2, 8), regs(2, 4), re...  2.37 us
    pallas_call x1, Pallas kernels, per_device(): call(faces_kernel, [HBM] * 4, [regs(2, CUBE), jax.ShapeDtypeStruct((NODES...  1.57 us
    pallas_call x1, Pallas kernels, per_device(): call(local_kernel, [VMEM, VMEM, VMEM, VMEM, HBM], [regs(2, CUBE), regs(2,...  1.2 us
  transfers between devices with their start and end apart: 14, of which 6 were waited for; matrix products, arithmetic and copies ran while one was open for 0% of the time, Pallas kernels for 2%

profile of v2, /device:TPU:22, one launch (start us, length us, event | category | flops | bytes accessed | tf_op | source)
XLA Modules:
  0.0 50.9 jit_solution(5001029489225015115)
XLA Ops:
  0.0 1.6 %shard_map.82 = (f32[2,125,8,128]{3,2,1,0:T(8,128)S(1)}, f32[5,5]{1,0:T(8,128)S(1)}, f32[1,5]{1,0:T(1,128)S(1)}, f32[8,128]{1,0:T(8,128)S(1)}, f32[25,8,128]{2,1...) custom-call(f32[4,125,4,128]{3,2,1,0:T(4,128)} %bitcast.10, ...), custom_call_target="tpu_custom_call" | custom-call | tf_op jit(solution)/shard_map/pallas_call | solution.py:741
  1.6 0.6 %collective-permute-start = (f32[25,8,128]{2,1,0:T(8,128)S(1)}, f32[25,8,128]{2,1,0:T(8,128)S(1)}, u32[]{:S(2)}, u32[]{:S(2)}) collective-permute-start(f32[25,8,128]{2,1,0:T(8,128)S(1)} %get-tuple-element.44), channel_id=1, source_target_pairs={{0,4},{4,0},{8,12},{12,8},{16,20},{20,16},{24,28},{28,24},{1,5},{5... | collective-permute-start | bytes 307208 | tf_op jit(solution)/shard_map/ppermute | solution.py:727
  2.2 4.4 %collective-permute-start.1 = (f32[25,8,128]{2,1,0:T(8,128)S(1)}, f32[25,8,128]{2,1,0:T(8,128)S(1)}, u32[]{:S(2)}, u32[]{:S(2)}) collective-permute-start(f32[25,8,128]{2,1,0:T(8,128)S(1)} %get-tuple-element.45), channel_id=1, source_target_pairs={{4,8},{8,4},{12,16},{16,12},{20,24},{24,20},{5,9},{9,5},{13,17},{1... | collective-permute-start | bytes 307208 | tf_op jit(solution)/shard_map/ppermute | solution.py:727
  6.6 0.1 collective-permute-start.2
  6.7 2.5 %collective-permute-start.3 = (f32[25,8,128]{2,1,0:T(8,128)S(1)}, f32[25,8,128]{2,1,0:T(8,128)S(1)}, u32[]{:S(2)}, u32[]{:S(2)}) collective-permute-start(f32[25,8,128]{2,1,0:T(8,128)S(1)} %get-tuple-element.47), channel_id=1, source_target_pairs={{1,2},{2,1},{5,6},{6,5},{9,10},{10,9},{13,14},{14,13},{17,18},{18,... | collective-permute-start | bytes 307208 | tf_op jit(solution)/shard_map/ppermute | solution.py:727
  9.2 1.2 %shard_map.83 = (f32[2,125,8,128]{3,2,1,0:T(8,128)S(1)}, f32[2,125,8,128]{3,2,1,0:T(8,128)S(1)}, f32[2,8,8,128]{3,2,1,0:T(8,128)S(1)}, f32[35,8,128]{2,1,0:T(8,128)S(1)}, f32[25,8,128]{2,1,0:T(8,128)S(1)}) custom-call(f32[5,5]{1,0:T(8,128)S(1)} %get-tuple-element.39.basis_in, f32[1,5]{1,0:T(1,128)S(1)} %get-tuple-element.40.lam_in, ...), custom_call_target="tpu_custom_call" | custom-call | tf_op jit(solution)/shard_map/pallas_call | solution.py:756
  10.4 0.0 collective-permute-done.fx0
  10.4 0.0 collective-permute-done.1.fx1
  10.4 0.0 collective-permute-done.2.fy0
  10.5 2.2 %collective-permute-done.3.fy1 = f32[25,8,128]{2,1,0:T(8,128)S(1)} collective-permute-done((f32[25,8,128]{2,1,0:T(8,128)S(1)}, f32[25,8,128]{2,1,0:T(8,128)S(1)}, u32[]{:S(2)}, u32[]{:S(2)}) %collective-permute-start.3) | collective-permute-done | bytes 102432 | tf_op jit(solution)/shard_map/ppermute | solution.py:727
  12.6 2.4 %shard_map.84 = (f32[2,125,8,128]{3,2,1,0:T(8,128)S(1)}, f32[2,8,8,128]{3,2,1,0:T(8,128)S(1)}, f32[2,4,8,128]{3,2,1,0:T(8,128)S(1)}, f32[2,4,8,128]{3,2,1,0:T(8,...) custom-call(f32[25,8,128]{2,1,0:T(8,128)S(1)} %get-tuple-element.43., ...), custom_call_target="tpu_custom_call" | custom-call | tf_op jit(solution)/shard_map/pallas_call | solution.py:765
  15.0 0.1 collective-permute-start.4
  15.1 2.3 %collective-permute-start.5 = (f32[16,8,128]{2,1,0:T(8,128)S(1)}, f32[16,8,128]{2,1,0:T(8,128)S(1)}, u32[]{:S(2)}, u32[]{:S(2)}) collective-permute-start(f32[16,8,128]{2,1,0:T(8,128)S(1)} %get-tuple-element.52), channel_id=1, source_target_pairs={{4,8},{8,4},{12,16},{16,12},{20,24},{24,20},{5,9},{9,5},{13,17},{1... | collective-permute-start | bytes 196616 | tf_op jit(solution)/shard_map/ppermute | solution.py:727
  17.4 1.9 %collective-permute-done.4.rx0 = f32[16,8,128]{2,1,0:T(8,128)S(1)} collective-permute-done((f32[16,8,128]{2,1,0:T(8,128)S(1)}, f32[16,8,128]{2,1,0:T(8,128)S(1)}, u32[]{:S(2)}, u32[]{:S(2)}) %collective-permute-start.4) | collective-permute-done | bytes 65568 | tf_op jit(solution)/shard_map/ppermute | solution.py:727
  19.4 2.8 %collective-permute-done.5.rx1 = f32[16,8,128]{2,1,0:T(8,128)S(1)} collective-permute-done((f32[16,8,128]{2,1,0:T(8,128)S(1)}, f32[16,8,128]{2,1,0:T(8,128)S(1)}, u32[]{:S(2)}, u32[]{:S(2)}) %collective-permute-start.5) | collective-permute-done | bytes 65568 | tf_op jit(solution)/shard_map/ppermute | solution.py:727
  22.2 0.1 collective-permute-start.6
  22.3 1.9 %collective-permute-start.7 = (f32[49,8,128]{2,1,0:T(8,128)S(1)}, f32[49,8,128]{2,1,0:T(8,128)S(1)}, u32[]{:S(2)}, u32[]{:S(2)}) collective-permute-start(f32[49,8,128]{2,1,0:T(8,128)S(1)} %get-tuple-element.59), channel_id=1, source_target_pairs={{1,2},{2,1},{5,6},{6,5},{9,10},{10,9},{13,14},{14,13},{17,18},{18,... | collective-permute-start | bytes 602120 | tf_op jit(solution)/shard_map/ppermute | solution.py:727
  24.2 0.0 collective-permute-done.6.ry0
  24.2 5.1 %collective-permute-done.7.ry1 = f32[49,8,128]{2,1,0:T(8,128)S(1)} collective-permute-done((f32[49,8,128]{2,1,0:T(8,128)S(1)}, f32[49,8,128]{2,1,0:T(8,128)S(1)}, u32[]{:S(2)}, u32[]{:S(2)}) %collective-permute-start.7) | collective-permute-done | bytes 200736 | tf_op jit(solution)/shard_map/ppermute | solution.py:727
  29.3 3.1 %shard_map.86 = (f32[64,8,128]{2,1,0:T(8,128)S(1)}, f32[24,8,128]{2,1,0:T(8,128)S(1)}, f32[24,8,128]{2,1,0:T(8,128)S(1)}) custom-call(f32[49,8,128]{2,1,0:T(8,128)S(1)} %collective-permute-done.6.ry0, f32[49,8,128]{2,1,0:T(8,128)S(1)} %collective-permute-done.7.ry1, f32[2,8,8,128]{3,2,1,0:T(8,128)S(1)} %get-tuple-element.60.c1, ...), custom_call_target="tpu_custom_call" | custom-call | tf_op jit(solution)/shard_map/pallas_call | solution.py:797
  32.4 0.1 collective-permute-start.8
  32.5 1.9 %collective-permute-start.9 = (f32[24,8,128]{2,1,0:T(8,128)S(1)}, f32[24,8,128]{2,1,0:T(8,128)S(1)}, u32[]{:S(2)}, u32[]{:S(2)}) collective-permute-start(f32[24,8,128]{2,1,0:T(8,128)S(1)} %get-tuple-element.65), channel_id=1, source_target_pairs={{1,2},{2,1},{5,6},{6,5},{9,10},{10,9},{13,14},{14,13},{17,18},{18,... | collective-permute-start | bytes 294920 | tf_op jit(solution)/shard_map/ppermute | solution.py:727
  34.4 2.1 %collective-permute-start.12 = (f32[25,8,128]{2,1,0:T(8,128)S(1)}, f32[25,8,128]{2,1,0:T(8,128)S(1)}, u32[]{:S(2)}, u32[]{:S(2)}) collective-permute-start(f32[25,8,128]{2,1,0:T(8,128)S(1)} %get-tuple-element.71), channel_id=1, source_target_pairs={{0,4},{4,0},{8,12},{12,8},{16,20},{20,16},{24,28},{28,24},{1,5},{5... | collective-permute-start | bytes 307208 | tf_op jit(solution)/shard_map/ppermute | solution.py:727
  36.5 1.9 %collective-permute-start.13 = (f32[25,8,128]{2,1,0:T(8,128)S(1)}, f32[25,8,128]{2,1,0:T(8,128)S(1)}, u32[]{:S(2)}, u32[]{:S(2)}) collective-permute-start(f32[25,8,128]{2,1,0:T(8,128)S(1)} %get-tuple-element.72), channel_id=1, source_target_pairs={{4,8},{8,4},{12,16},{16,12},{20,24},{24,20},{5,9},{9,5},{13,17},{1... | collective-permute-start | bytes 307208 | tf_op jit(solution)/shard_map/ppermute | solution.py:727
  38.4 0.0 collective-permute-done.8.r0
  38.4 0.0 collective-permute-done.9.r1
  38.5 2.1 %collective-permute-start.10 = (f32[16,8,128]{2,1,0:T(8,128)S(1)}, f32[16,8,128]{2,1,0:T(8,128)S(1)}, u32[]{:S(2)}, u32[]{:S(2)}) collective-permute-start(f32[16,8,128]{2,1,0:T(8,128)S(1)} %get-tuple-element.67), channel_id=1, source_target_pairs={{0,4},{4,0},{8,12},{12,8},{16,20},{20,16},{24,28},{28,24},{1,5},{5... | collective-permute-start | bytes 196616 | tf_op jit(solution)/shard_map/ppermute | solution.py:727
  40.6 2.8 %collective-permute-start.11 = (f32[16,8,128]{2,1,0:T(8,128)S(1)}, f32[16,8,128]{2,1,0:T(8,128)S(1)}, u32[]{:S(2)}, u32[]{:S(2)}) collective-permute-start(f32[16,8,128]{2,1,0:T(8,128)S(1)} %get-tuple-element.68), channel_id=1, source_target_pairs={{4,8},{8,4},{12,16},{16,12},{20,24},{24,20},{5,9},{9,5},{13,17},{1... | collective-permute-start | bytes 196616 | tf_op jit(solution)/shard_map/ppermute | solution.py:727
  43.4 0.5 %collective-permute-done.13.rx1 = f32[25,8,128]{2,1,0:T(8,128)S(1)} collective-permute-done((f32[25,8,128]{2,1,0:T(8,128)S(1)}, f32[25,8,128]{2,1,0:T(8,128)S(1)}, u32[]{:S(2)}, u32[]{:S(2)}) %collective-permute-start.13) | collective-permute-done | bytes 102432 | tf_op jit(solution)/shard_map/ppermute | solution.py:727
  43.9 0.0 collective-permute-done.10.r0
  43.9 3.7 %collective-permute-done.11.r1 = f32[16,8,128]{2,1,0:T(8,128)S(1)} collective-permute-done((f32[16,8,128]{2,1,0:T(8,128)S(1)}, f32[16,8,128]{2,1,0:T(8,128)S(1)}, u32[]{:S(2)}, u32[]{:S(2)}) %collective-permute-start.11) | collective-permute-done | bytes 65568 | tf_op jit(solution)/shard_map/ppermute | solution.py:727
  47.6 3.3 %shard_map.88 = f32[4,125,4,128]{3,2,1,0:T(4,128)} custom-call(f32[25,8,128]{2,1,0:T(8,128)S(1)} %get-tuple-element.43.basis, f32[64,8,128]{2,1,0:T(8,128)S(1)} %get-tuple-element.66.s, f32[16,8,128]{2,1,0:T(8,128)S(1)} %collective-permute-done.10.r0, f32[16,8,128]{2,1,0:T(8,128)S(1)} %collective-permute-done.11.r1, ...), custom_call_target="tpu_custom_call" | custom-call | tf_op jit(solution)/shard_map/pallas_call | solution.py:802
  (11 shorter events, 0.1 us)
Async XLA Ops:
  0.0 9.2 %copy-start = (f32[4,5,5,5,2,2,128]{6,5,4,3,2,1,0:T(2,128)S(1)}, f32[4,5,5,5,2,2,128]{6,5,4,3,2,1,0:T(2,128)}, u32[]{:S(2)}) copy-start(f32[4,5,5,5,2,2,128]{6,5,4,3,2,1,0:T(2,128)} %param.8) | copy-start | bytes 3072004
  1.6 8.9 %collective-permute-start = (f32[25,8,128]{2,1,0:T(8,128)S(1)}, f32[25,8,128]{2,1,0:T(8,128)S(1)}, u32[]{:S(2)}, u32[]{:S(2)}) collective-permute-start(f32[25,8,128]{2,1,0:T(8,128)S(1)} %get-tuple-element.44), channel_id=1, source_target_pairs={{0,4},{4,0},{8,12},{12,8},{16,20},{20,16},{24,28},{28,24},{1,5},{5... | collective-permute-start | bytes 307208 | tf_op jit(solution)/shard_map/ppermute | solution.py:727
  2.2 8.3 %collective-permute-start.1 = (f32[25,8,128]{2,1,0:T(8,128)S(1)}, f32[25,8,128]{2,1,0:T(8,128)S(1)}, u32[]{:S(2)}, u32[]{:S(2)}) collective-permute-start(f32[25,8,128]{2,1,0:T(8,128)S(1)} %get-tuple-element.45), channel_id=1, source_target_pairs={{4,8},{8,4},{12,16},{16,12},{20,24},{24,20},{5,9},{9,5},{13,17},{1... | collective-permute-start | bytes 307208 | tf_op jit(solution)/shard_map/ppermute | solution.py:727
  6.6 3.9 %collective-permute-start.2 = (f32[25,8,128]{2,1,0:T(8,128)S(1)}, f32[25,8,128]{2,1,0:T(8,128)S(1)}, u32[]{:S(2)}, u32[]{:S(2)}) collective-permute-start(f32[25,8,128]{2,1,0:T(8,128)S(1)} %get-tuple-element.46), channel_id=1, source_target_pairs={{0,1},{1,0},{2,3},{3,2},{4,5},{5,4},{6,7},{7,6},{8,9},{9,8},{10,11... | collective-permute-start | bytes 307208 | tf_op jit(solution)/shard_map/ppermute | solution.py:727
  6.7 6.0 %collective-permute-start.3 = (f32[25,8,128]{2,1,0:T(8,128)S(1)}, f32[25,8,128]{2,1,0:T(8,128)S(1)}, u32[]{:S(2)}, u32[]{:S(2)}) collective-permute-start(f32[25,8,128]{2,1,0:T(8,128)S(1)} %get-tuple-element.47), channel_id=1, source_target_pairs={{1,2},{2,1},{5,6},{6,5},{9,10},{10,9},{13,14},{14,13},{17,18},{18,... | collective-permute-start | bytes 307208 | tf_op jit(solution)/shard_map/ppermute | solution.py:727
  15.0 4.3 %collective-permute-start.4 = (f32[16,8,128]{2,1,0:T(8,128)S(1)}, f32[16,8,128]{2,1,0:T(8,128)S(1)}, u32[]{:S(2)}, u32[]{:S(2)}) collective-permute-start(f32[16,8,128]{2,1,0:T(8,128)S(1)} %get-tuple-element.51), channel_id=1, source_target_pairs={{0,4},{4,0},{8,12},{12,8},{16,20},{20,16},{24,28},{28,24},{1,5},{5... | collective-permute-start | bytes 196616 | tf_op jit(solution)/shard_map/ppermute | solution.py:727
  15.1 7.1 %collective-permute-start.5 = (f32[16,8,128]{2,1,0:T(8,128)S(1)}, f32[16,8,128]{2,1,0:T(8,128)S(1)}, u32[]{:S(2)}, u32[]{:S(2)}) collective-permute-start(f32[16,8,128]{2,1,0:T(8,128)S(1)} %get-tuple-element.52), channel_id=1, source_target_pairs={{4,8},{8,4},{12,16},{16,12},{20,24},{24,20},{5,9},{9,5},{13,17},{1... | collective-permute-start | bytes 196616 | tf_op jit(solution)/shard_map/ppermute | solution.py:727
  22.2 7.2 %copy-start.1 = (f32[256,256]{1,0:T(8,128)S(1)}, f32[256,256]{1,0:T(8,128)}, u32[]{:S(2)}) copy-start(f32[256,256]{1,0:T(8,128)} %inverse.1) | copy-start | bytes 786436
  22.2 7.2 %copy-start.2 = (s32[512,8]{0,1:T(8,128)S(1)}, s32[512,8]{0,1:T(8,128)}, u32[]{:S(2)}) copy-start(s32[512,8]{0,1:T(8,128)} %param.14) | copy-start | bytes 49156
  22.2 7.2 %copy-start.3 = (s32[512,8]{0,1:T(8,128)S(1)}, s32[512,8]{0,1:T(8,128)}, u32[]{:S(2)}) copy-start(s32[512,8]{0,1:T(8,128)} %param.15) | copy-start | bytes 49156
  22.2 2.0 %collective-permute-start.6 = (f32[49,8,128]{2,1,0:T(8,128)S(1)}, f32[49,8,128]{2,1,0:T(8,128)S(1)}, u32[]{:S(2)}, u32[]{:S(2)}) collective-permute-start(f32[49,8,128]{2,1,0:T(8,128)S(1)} %get-tuple-element.58), channel_id=1, source_target_pairs={{0,1},{1,0},{2,3},{3,2},{4,5},{5,4},{6,7},{7,6},{8,9},{9,8},{10,11... | collective-permute-start | bytes 602120 | tf_op jit(solution)/shard_map/ppermute | solution.py:727
  22.3 7.0 %collective-permute-start.7 = (f32[49,8,128]{2,1,0:T(8,128)S(1)}, f32[49,8,128]{2,1,0:T(8,128)S(1)}, u32[]{:S(2)}, u32[]{:S(2)}) collective-permute-start(f32[49,8,128]{2,1,0:T(8,128)S(1)} %get-tuple-element.59), channel_id=1, source_target_pairs={{1,2},{2,1},{5,6},{6,5},{9,10},{10,9},{13,14},{14,13},{17,18},{18,... | collective-permute-start | bytes 602120 | tf_op jit(solution)/shard_map/ppermute | solution.py:727
  32.4 6.0 %collective-permute-start.8 = (f32[24,8,128]{2,1,0:T(8,128)S(1)}, f32[24,8,128]{2,1,0:T(8,128)S(1)}, u32[]{:S(2)}, u32[]{:S(2)}) collective-permute-start(f32[24,8,128]{2,1,0:T(8,128)S(1)} %get-tuple-element.64), channel_id=1, source_target_pairs={{0,1},{1,0},{2,3},{3,2},{4,5},{5,4},{6,7},{7,6},{8,9},{9,8},{10,11... | collective-permute-start | bytes 294920 | tf_op jit(solution)/shard_map/ppermute | solution.py:727
  32.5 5.9 %collective-permute-start.9 = (f32[24,8,128]{2,1,0:T(8,128)S(1)}, f32[24,8,128]{2,1,0:T(8,128)S(1)}, u32[]{:S(2)}, u32[]{:S(2)}) collective-permute-start(f32[24,8,128]{2,1,0:T(8,128)S(1)} %get-tuple-element.65), channel_id=1, source_target_pairs={{1,2},{2,1},{5,6},{6,5},{9,10},{10,9},{13,14},{14,13},{17,18},{18,... | collective-permute-start | bytes 294920 | tf_op jit(solution)/shard_map/ppermute | solution.py:727
  34.4 9.0 %collective-permute-start.12 = (f32[25,8,128]{2,1,0:T(8,128)S(1)}, f32[25,8,128]{2,1,0:T(8,128)S(1)}, u32[]{:S(2)}, u32[]{:S(2)}) collective-permute-start(f32[25,8,128]{2,1,0:T(8,128)S(1)} %get-tuple-element.71), channel_id=1, source_target_pairs={{0,4},{4,0},{8,12},{12,8},{16,20},{20,16},{24,28},{28,24},{1,5},{5... | collective-permute-start | bytes 307208 | tf_op jit(solution)/shard_map/ppermute | solution.py:727
  36.5 7.4 %collective-permute-start.13 = (f32[25,8,128]{2,1,0:T(8,128)S(1)}, f32[25,8,128]{2,1,0:T(8,128)S(1)}, u32[]{:S(2)}, u32[]{:S(2)}) collective-permute-start(f32[25,8,128]{2,1,0:T(8,128)S(1)} %get-tuple-element.72), channel_id=1, source_target_pairs={{4,8},{8,4},{12,16},{16,12},{20,24},{24,20},{5,9},{9,5},{13,17},{1... | collective-permute-start | bytes 307208 | tf_op jit(solution)/shard_map/ppermute | solution.py:727
  38.5 5.4 %collective-permute-start.10 = (f32[16,8,128]{2,1,0:T(8,128)S(1)}, f32[16,8,128]{2,1,0:T(8,128)S(1)}, u32[]{:S(2)}, u32[]{:S(2)}) collective-permute-start(f32[16,8,128]{2,1,0:T(8,128)S(1)} %get-tuple-element.67), channel_id=1, source_target_pairs={{0,4},{4,0},{8,12},{12,8},{16,20},{20,16},{24,28},{28,24},{1,5},{5... | collective-permute-start | bytes 196616 | tf_op jit(solution)/shard_map/ppermute | solution.py:727
  40.6 7.0 %collective-permute-start.11 = (f32[16,8,128]{2,1,0:T(8,128)S(1)}, f32[16,8,128]{2,1,0:T(8,128)S(1)}, u32[]{:S(2)}, u32[]{:S(2)}) collective-permute-start(f32[16,8,128]{2,1,0:T(8,128)S(1)} %get-tuple-element.68), channel_id=1, source_target_pairs={{4,8},{8,4},{12,16},{16,12},{20,24},{24,20},{5,9},{9,5},{13,17},{1... | collective-permute-start | bytes 196616 | tf_op jit(solution)/shard_map/ppermute | solution.py:727

commit v3 on v2

--- a/solution.py
+++ b/solution.py
@@ -70,11 +70,6 @@
 def restrict_face(vals):
     rows = [[combine(column(c), vals[j * NODES : (j + 1) * NODES]) for c in (0, 1)] for j in range(NODES)]
     return [combine(column(b), [rows[j][c] for j in range(NODES)]) for b in (0, 1) for c in (0, 1)]
-
-
-def prolong_face(coarse):
-    half = [[combine(TABLE[j], [coarse[c], coarse[2 + c]]) for c in (0, 1)] for j in range(NODES)]
-    return [combine(TABLE[k], half[j]) for j in range(NODES) for k in range(NODES)]
 
 
 def is_even(axis):
@@ -115,32 +110,41 @@
     return combine([1.0] * len(terms), terms) if terms else None
 
 
-def smooth(load_plane, finish, basis, invd, work):
-    def columns():
-        return [[basis[i * NODES + a] for i in range(NODES)] for a in range(NODES)]
-
-    def rows():
-        return [[basis[i * NODES + a] for a in range(NODES)] for i in range(NODES)]
-
-    def plane(vals, mats):
-        mid = [[combine(m, vals[j * NODES : (j + 1) * NODES]) for m in mats] for j in range(NODES)]
-        return [[combine(m, [mid[j][c] for j in range(NODES)]) for c in range(NODES)] for m in mats]
-
+def columns(basis):
+    return [[basis[i * NODES + a] for i in range(NODES)] for a in range(NODES)]
+
+
+def rows(basis):
+    return [[basis[i * NODES + a] for a in range(NODES)] for i in range(NODES)]
+
+
+def plane(vals, mats):
+    mid = [[combine(m, vals[j * NODES : (j + 1) * NODES]) for m in mats] for j in range(NODES)]
+    return [combine(m, [mid[j][c] for j in range(NODES)]) for m in mats for c in range(NODES)]
+
+
+def to_modal(load_plane, store, basis, work):
     for i in range(NODES):
-        out = plane(load_plane(i), columns())
-        for b in range(NODES):
-            for c in range(NODES):
-                work[node(i, b, c)] = out[b][c]
+        for n, v in enumerate(plane(load_plane(i), columns(basis))):
+            work[node(i, 0, 0) + n] = v
     for b in range(NODES):
-        fwd, bwd = columns(), rows()
+        mats = columns(basis)
         for c in range(NODES):
             vals = [work[node(i, b, c)] for i in range(NODES)]
-            modal = [combine(fwd[a], vals) * invd[order_of(a, b, c)] for a in range(NODES)]
+            for a in range(NODES):
+                store(node(a, b, c), combine(mats[a], vals))
+
+
+def from_modal(modal_plane, finish, basis, work):
+    for a in range(NODES):
+        for n, v in enumerate(plane(modal_plane(a), rows(basis))):
+            work[node(a, 0, 0) + n] = v
+    for j in range(NODES):
+        mats = rows(basis)
+        for k in range(NODES):
+            vals = [work[node(a, j, k)] for a in range(NODES)]
             for i in range(NODES):
-                work[node(i, b, c)] = combine(bwd[i], modal)
-    for i in range(NODES):
-        out = plane([work[node(i, 0, 0) + n] for n in range(FACE)], rows())
-        finish(i, [out[j][k] for j in range(NODES) for k in range(NODES)])
+                finish(node(i, j, k), combine(mats[i], vals))
 
 
 TRIPLES = [(a, b, c) for a in range(NODES) for b in range(a, NODES) for c in range(b, NODES)]
@@ -230,7 +234,7 @@
             )
 
 
-def local_kernel(basis_in, lam_in, coef, u, rhs_hbm, rhs, w, crd, invd, basis, wide_ref, sems):
+def local_kernel(basis_in, lam_in, coef, u, rhs_hbm, rhs, w, crd, invd, basis, wide_ref, work, sems):
     copies = take_in(rhs_hbm, rhs, sems)
     scale = coef[...]
     for i in range(NODES):
@@ -240,10 +244,11 @@
     for t, (a, b, c) in enumerate(TRIPLES):
         invd[t] = 1.0 / (scale * (lam[a] + lam[b] + lam[c]) + MASS_SHIFT)
     for c in (0, 1):
-        modal = [
-            lam[m] * combine([1.0] * NODES, [basis[i * NODES + m] * TABLE[i][c] for i in range(NODES)])
-            for m in range(NODES)
-        ]
+        modal = []
+        for m in range(NODES):
+            v = combine(column(c), [basis[i * NODES + m] for i in range(NODES)])
+            basis[FACE + 2 * m + c] = v
+            modal.append(lam[m] * v)
         for i in range(NODES):
             wide_ref[c * NODES + i] = combine([1.0] * NODES, [basis[i * NODES + m] * modal[m] for m in range(NODES)])
     for cp in copies:
@@ -253,6 +258,19 @@
         def val(n):
             return u[g, n]
 
+        def load(i):
+            vals = []
+            for j in range(NODES):
+                for k in range(NODES):
+                    extra = couple(val, i, j, k)
+                    v = rhs[g, node(i, j, k)]
+                    vals.append(v if extra is None else v + FACE_PENALTY * extra)
+            return vals
+
+        def store(n, v):
+            w[g, n] = v
+
+        to_modal(load, store, basis, work)
         wide = [[wide_ref[c * NODES + i] for i in range(NODES)] for c in (0, 1)]
         plain, stiff = [], []
         for i in range(NODES):
@@ -260,9 +278,6 @@
             for j in range(NODES):
                 here = [u[g, node(i, j, k)] for k in range(NODES)]
                 right = [rhs[g, node(i, j, k)] for k in range(NODES)]
-                for k in range(NODES):
-                    extra = couple(val, i, j, k)
-                    w[g, node(i, j, k)] = right[k] if extra is None else right[k] + FACE_PENALTY * extra
                 t.append([combine(column(c), here) for c in (0, 1)])
                 s.append([combine(wide[c], here) for c in (0, 1)])
                 r.append([combine(column(c), [x - y for x, y in zip(right, here)]) for c in (0, 1)])
@@ -298,34 +313,35 @@
         out[0, n], out[1, n] = outer_pair(first, plus, minus, by)
 
 
-def first_kernel(basis, fx0, fx1, fy0, fy1, u, w, crd, invd, u1, c0, xpk, yf, ux0, ux1, my0, my1, mx0, mx1, ex, ey, work):
+def first_kernel(basis, fx0, fx1, fy0, fy1, u, w, crd, invd, u1, c0, xpk, yf, ux0, ux1, uy0, uy1, mx0, mx1, ex, ey, work):
     even_x, even_y = sublane_bits()
     combine_outer("px", even_x, fx0, fx1, FACE, 0, 2, ex)
     combine_outer("py", even_y, fy0, fy1, FACE, 0, 1, ey)
 
     def pair(g, carry):
-        def load(i):
+        back = -DAMPING
+        faces_x, faces_y = [ex[g, n] for n in range(FACE)], [ey[g, n] for n in range(FACE)]
+        ox = [back * v for v in restrict_face(faces_x)]
+        for n, v in enumerate(plane(faces_x, columns(basis))):
+            ex[g, n] = FACE_PENALTY * v
+        oy = [back * v for v in restrict_face(faces_y)]
+        for n, v in enumerate(plane(faces_y, columns(basis))):
+            ey[g, n] = FACE_PENALTY * v
+
+        def modal_plane(a):
             vals = []
-            for j in range(NODES):
-                for k in range(NODES):
-                    v = w[g, node(i, j, k)]
-                    if i == TOP:
-                        v = v + jnp.where(even_x, 0.0, FACE_PENALTY * ex[g, j * NODES + k])
-                    if i == 0:
-                        v = v + jnp.where(even_x, FACE_PENALTY * ex[g, j * NODES + k], 0.0)
-                    if j == TOP:
-                        v = v + jnp.where(even_y, 0.0, FACE_PENALTY * ey[g, i * NODES + k])
-                    if j == 0:
-                        v = v + jnp.where(even_y, FACE_PENALTY * ey[g, i * NODES + k], 0.0)
-                    vals.append(v)
+            wx = jnp.where(even_x, basis[a], basis[TOP * NODES + a])
+            for b in range(NODES):
+                wy = jnp.where(even_y, basis[b], basis[TOP * NODES + b])
+                for c in range(NODES):
+                    v = w[g, node(a, b, c)] + wx * ex[g, b * NODES + c] + wy * ey[g, a * NODES + c]
+                    vals.append(v * invd[order_of(a, b, c)])
             return vals
 
-        def finish(i, vals):
-            for n in range(FACE):
-                at = node(i, 0, 0) + n
-                u1[g, at] = KEPT * u[g, at] + DAMPING * vals[n]
-
-        smooth(load, finish, basis, invd, work)
+        def finish(n, v):
+            u1[g, n] = KEPT * u[g, n] + DAMPING * v
+
+        from_modal(modal_plane, finish, basis, work)
 
         def val(n):
             return u1[g, n]
@@ -333,9 +349,6 @@
         rx = [restrict_face(x_face(val, s)) for s in (0, TOP)]
         ry = [restrict_face(y_face(val, s)) for s in (0, TOP)]
         rz = [restrict_face(z_face(val, s)) for s in (0, TOP)]
-        back = -DAMPING
-        ox = [back * v for v in restrict_face([ex[g, n] for n in range(FACE)])]
-        oy = [back * v for v in restrict_face([ey[g, n] for n in range(FACE)])]
         both = inner_restricted(rx, ry, rz, ox, oy)
         for n in range(8):
             c0[g, n] = crd[g, n] + FACE_PENALTY * both[n]
@@ -380,11 +393,11 @@
                 par_y,
                 pack_lo(even_y, u1[0, lo], u1[1, lo], 1),
                 pack_hi(even_y, u1[0, hi], u1[1, hi], 1),
-                my0, my1, 24 + n,
+                uy0, uy1, n,
             )
 
 
-def middle_kernel(rx0, rx1, c0, xpk, yf, _0, _1, c1, ring, ypk, my0, my1):
+def middle_kernel(rx0, rx1, c0, xpk, yf, c1, ring, ypk, my0, my1):
     even_x, even_y = sublane_bits()
     par_x, par_y = is_even("px"), is_even("py")
 
@@ -626,13 +639,34 @@
         swap_store(par_x, lo, hi, m0, m1, 12 + f)
 
 
-def last_kernel(
-    basis, s, r0, r1, u1, rhs, invd, rx0, rx1, ry0, ry1, out_hbm, out, own, ringx, ringy, ex, ey, work, sems
-):
+def early_kernel(basis, u1, rhs, rx0, rx1, ry0, ry1, modal, ex, ey, work):
     even_x, even_y = sublane_bits()
+    combine_outer("px", even_x, rx0, rx1, FACE, 0, 2, ex)
+    combine_outer("py", even_y, ry0, ry1, FACE, 0, 1, ey)
+
+    def pair(g, carry):
+        def load(i):
+            vals = []
+            for j in range(NODES):
+                for k in range(NODES):
+                    v = rhs[g, node(i, j, k)]
+                    extra = couple(lambda n: u1[g, n], i, j, k, lambda n: ex[g, n], lambda n: ey[g, n])
+                    vals.append(v if extra is None else v + FACE_PENALTY * extra)
+            return vals
+
+        def store(n, v):
+            modal[g, n] = v
+
+        to_modal(load, store, basis, work)
+        return carry
+
+    lax.fori_loop(0, 2, pair, 0)
+
+
+def last_kernel(basis, s, r0, r1, u1, modal, invd, out_hbm, out, own, ringx, ringy, work, sems):
+    even_x, even_y = sublane_bits()
+    lane = lane_ids()
     par_x = is_even("px")
-    combine_outer("px", even_x, rx0, rx1, FACE, 0, 2, ex)
-    combine_outer("py", even_y, ry0, ry1, FACE, 24, 1, ey)
 
     def received(x, n):
         a, b = (r0[n], r1[n]) if x else (r1[n], r0[n])
@@ -653,35 +687,53 @@
             return ref[pl.ds(g * 64 + n, 8, stride=8), :]
 
         coarse = [take(own, n) for n in range(8)]
-        for i in range(NODES):
-            fine = prolong_face([combine(TABLE[i], [coarse[n], coarse[4 + n]]) for n in range(4)])
-            for n in range(FACE):
-                at = node(i, 0, 0) + n
-                out[g, at] = u1[g, at] + fine[n]
-        xr = [jnp.where(even_x, take(ringx, 4 + n), take(ringx, n)) for n in range(4)]
-        yr = [
-            jnp.where(even_y, take(ringy, a * 4 + 2 + c), take(ringy, a * 4 + c)) for a in (0, 1) for c in (0, 1)
-        ]
-        for n, v in enumerate(prolong_face(xr)):
-            ex[g, n] = ex[g, n] + v
-        for n, v in enumerate(prolong_face(yr)):
-            ey[g, n] = ey[g, n] + v
-
-        def load(i):
+        faces_x, faces_y, faces_z = [[], []], [[], []], [[], []]
+        for p in (0, 1):
+            for q in (0, 1):
+                n = p * 2 + q
+                xr = jnp.where(even_x, take(ringx, 4 + n), take(ringx, n))
+                faces_x[0].append(jnp.where(even_x, xr, up(coarse[4 + n], 2)))
+                faces_x[1].append(jnp.where(even_x, down(coarse[n], 2), xr))
+                n = p * 4 + q
+                yr = jnp.where(even_y, take(ringy, n + 2), take(ringy, n))
+                faces_y[0].append(jnp.where(even_y, yr, up(coarse[n + 2], 1)))
+                faces_y[1].append(jnp.where(even_y, down(coarse[n], 1), yr))
+                n = p * 4 + q * 2
+                faces_z[0].append(jnp.where(lane > 0, pltpu.roll(coarse[n + 1], 1, 1), 0.0))
+                faces_z[1].append(jnp.where(lane < LANES - 1, pltpu.roll(coarse[n], LANES - 1, 1), 0.0))
+        for group in (faces_x, faces_y, faces_z):
+            for end in (0, 1):
+                group[end] = [FACE_PENALTY * v for v in group[end]]
+        share = KEPT / DAMPING
+
+        def modal_plane(a):
+            ends = [basis[a], basis[TOP * NODES + a]]
+            thin = [basis[FACE + 2 * a + c] for c in (0, 1)]
+            along_x = [combine(ends, [faces_x[0][n], faces_x[1][n]]) for n in range(4)]
+            along_y = [[combine(thin, [faces_y[e][q], faces_y[e][2 + q]]) for q in (0, 1)] for e in (0, 1)]
+            along_z = [[combine(thin, [faces_z[e][q], faces_z[e][2 + q]]) for q in (0, 1)] for e in (0, 1)]
+            fine = [share * combine(thin, [coarse[n], coarse[4 + n]]) for n in range(4)]
             vals = []
-            for j in range(NODES):
-                for k in range(NODES):
-                    v = rhs[g, node(i, j, k)]
-                    extra = couple(lambda n: out[g, n], i, j, k, lambda n: ex[g, n], lambda n: ey[g, n])
-                    vals.append(v if extra is None else v + FACE_PENALTY * extra)
+            for b in range(NODES):
+                ends_b = [basis[b], basis[TOP * NODES + b]]
+                thin_b = [basis[FACE + 2 * b + c] for c in (0, 1)]
+                mixed = [
+                    combine(thin_b + ends_b, [along_x[q], along_x[2 + q], along_y[0][q], along_y[1][q]])
+                    for q in (0, 1)
+                ]
+                flat = [combine(thin_b, along_z[e]) for e in (0, 1)]
+                line = [combine(thin_b, [fine[q], fine[2 + q]]) for q in (0, 1)]
+                for c in range(NODES):
+                    ends_c = [basis[c], basis[TOP * NODES + c]]
+                    thin_c = [basis[FACE + 2 * c + q] for q in (0, 1)]
+                    v = modal[g, node(a, b, c)] + combine(thin_c + ends_c, mixed + flat)
+                    vals.append(v * invd[order_of(a, b, c)] + combine(thin_c, line))
             return vals
 
-        def finish(i, vals):
-            for n in range(FACE):
-                at = node(i, 0, 0) + n
-                out[g, at] = KEPT * out[g, at] + DAMPING * vals[n]
-
-        smooth(load, finish, basis, invd, work)
+        def finish(n, v):
+            out[g, n] = KEPT * u1[g, n] + DAMPING * v
+
+        from_modal(modal_plane, finish, basis, work)
         for c in put_out(g):
             c.start()
         return carry
@@ -735,6 +787,8 @@
     rows_all = span_y * lax.axis_size("py")
     flat = (fields, CUBE, span_x * span_y, layers)
     field_sems = pltpu.SemaphoreType.DMA((fields,))
+    outer = pltpu.VMEM((2, FACE, SUB, LANES), F32)
+    work = pltpu.VMEM((CUBE, SUB, LANES), F32)
 
     stay = functools.partial(pltpu.with_memory_space_constraint, memory_space=pltpu.HBM)
     few = (modal_basis, modal_values.reshape(1, NODES), coefficient.reshape(span_x * span_y, layers))
@@ -756,29 +810,28 @@
     rhs, w, crd, invd, basis = call(
         local_kernel,
         [VMEM, VMEM, VMEM, VMEM, HBM],
-        [regs(2, CUBE), regs(2, CUBE), regs(2, 8), regs(len(TRIPLES)), regs(FACE)],
+        [regs(2, CUBE), regs(2, CUBE), regs(2, 8), regs(len(TRIPLES)), regs(FACE + 2 * NODES)],
         [VMEM] * 5,
-        [pltpu.VMEM((2 * NODES, SUB, LANES), F32), field_sems],
+        [pltpu.VMEM((2 * NODES, SUB, LANES), F32), work, field_sems],
     )(*few, u, right_side.reshape(flat))
-    outer = pltpu.VMEM((2, FACE, SUB, LANES), F32)
-    work = pltpu.VMEM((CUBE, SUB, LANES), F32)
-    u1, c0, xpk, yf, ux0, ux1, my0, my1, mx0, mx1 = call(
+    u1, c0, xpk, yf, ux0, ux1, uy0, uy1, mx0, mx1 = call(
         first_kernel,
         [VMEM] * 9,
-        [regs(2, CUBE), regs(2, 8), regs(2, 4), regs(2, 4)] + [regs(n) for n in (FACE, 24 + FACE, 16) for _ in (0, 1)],
+        [regs(2, CUBE), regs(2, 8), regs(2, 4), regs(2, 4)] + [regs(n) for n in (FACE, FACE, 16) for _ in (0, 1)],
         [VMEM] * 10,
         [outer, outer, work],
     )(basis, *fx, *fy, u, w, crd, invd)
     rx = swaps("px", mx0, mx1)
-    c1, ring, ypk, my0, my1 = call(
+    ux = swaps("px", ux0, ux1)
+    middle = call(
         middle_kernel,
-        [VMEM] * 7,
-        [regs(2, 8), regs(2, 8), regs(2, 2, 4), regs(24 + FACE), regs(24 + FACE)],
         [VMEM] * 5,
-        aliases={5: 3, 6: 4},
-    )(*rx, c0, xpk, yf, my0, my1)
+        [regs(2, 8), regs(2, 8), regs(2, 2, 4), regs(24), regs(24)],
+        [VMEM] * 5,
+    )
+    c1, ring, ypk, my0, my1 = middle(*rx, c0, xpk, yf)
     ry = swaps("py", my0, my1)
-    ux = swaps("px", ux0, ux1)
+    uy = swaps("py", uy0, uy1)
     rows = patch_elements.shape[0]
     width = patch_inverse.shape[0]
     patches = call(
@@ -798,14 +851,16 @@
     rv = swaps("py", v0, v1)
     s, m0, m1 = call(sum_kernel, [VMEM] * 3, [regs(64), regs(16), regs(16)], [VMEM] * 3)(v, *rv)
     rs = swaps("px", m0, m1)
+    early = call(early_kernel, [VMEM] * 7, regs(2, CUBE), VMEM, [outer, outer, work])
+    modal = early(basis, u1, rhs, *ux, *uy)
     table = pltpu.VMEM((128, LANES), F32)
     out = call(
         last_kernel,
-        [VMEM] * 11,
+        [VMEM] * 7,
         jax.ShapeDtypeStruct(flat, F32),
         HBM,
-        [pltpu.VMEM((2, CUBE, SUB, LANES), F32), table, table, table, outer, outer, work, field_sems],
-    )(basis, s, *rs, u1, rhs, invd, *ux, *ry)
+        [pltpu.VMEM((2, CUBE, SUB, LANES), F32), table, table, table, work, field_sems],
+    )(basis, s, *rs, u1, modal, invd)
     return out.reshape(right_side.shape)
 
 

time: 51.8 us -> 52.9 us (1.021)
  waiting for transfers between devices: 16.3 us -> 12.6 us
  starting transfers between devices: 22.8 us -> 26.3 us
  Pallas kernels: 11.6 us -> 12.8 us
    ppermute x14 -> x16, waiting for transfers between devices: 16.3 us -> 12.6 us  [swaps(): got[colour] = lax.ppermute((m0, m1)[colour], axis, pairs)]
    ppermute x14 -> x16, starting transfers between devices: 22.8 us -> 26.3 us  [swaps(): got[colour] = lax.ppermute((m0, m1)[colour], axis, pairs)]
    pallas_call x1, Pallas kernels: 1.2 us -> 2.25 us  [per_device(): call(local_kernel, [VMEM, VMEM, VMEM, VMEM, HBM], [regs(2, CUBE), regs(2,...]
    pallas_call x2 -> x3, Pallas kernels: 3.31 us -> 4.03 us  [the longest x1 2.66 us: per_device(): call(last_kernel, [VMEM] * 7, jax.ShapeDtypeStruct(flat, F32), HBM, [pltp...]
    pallas_call x1, Pallas kernels: 2.37 us -> 1.8 us  [per_device(): call(first_kernel, [VMEM] * 9, [regs(2, CUBE), regs(2, 8), regs(2, 4), re...]
  transfers between devices with their start and end apart: 14 -> 16, of which waited for: 6 -> 5; matrix products, arithmetic and copies ran while one was open for 0% -> 0% of each run, Pallas kernels for 2% -> 7%
where the time goes in v3:
time: 52.9 us; the launch traced here: 52 us
  starting transfers between devices  26.3 us (50%)
  Pallas kernels  12.8 us (24%)
  waiting for transfers between devices  12.6 us (24%)
    ppermute x16, starting transfers between devices, swaps(): got[colour] = lax.ppermute((m0, m1)[colour], axis, pairs)  26.3 us
    ppermute x16, waiting for transfers between devices, swaps(): got[colour] = lax.ppermute((m0, m1)[colour], axis, pairs)  12.6 us
    pallas_call x1, Pallas kernels, per_device(): patches(*ry, c1, ring, ypk, patch_elements.T, patch_mask.T, patch_inverse)  3.07 us
    pallas_call x1, Pallas kernels, per_device(): call(last_kernel, [VMEM] * 7, jax.ShapeDtypeStruct(flat, F32), HBM, [pltp...  2.66 us
    pallas_call x1, Pallas kernels, per_device(): call(local_kernel, [VMEM, VMEM, VMEM, VMEM, HBM], [regs(2, CUBE), regs(2,...  2.25 us
    pallas_call x1, Pallas kernels, per_device(): call(first_kernel, [VMEM] * 9, [regs(2, CUBE), regs(2, 8), regs(2, 4), re...  1.8 us
    pallas_call x1, Pallas kernels, per_device(): call(faces_kernel, [HBM] * 4, [regs(2, CUBE), jax.ShapeDtypeStruct((NODES...  1.57 us
    pallas_call x1, Pallas kernels, per_device(): modal = early(basis, u1, rhs, *ux, *uy)  1.33 us
  transfers between devices with their start and end apart: 16, of which 5 were waited for; matrix products, arithmetic and copies ran while one was open for 0% of the time, Pallas kernels for 7%

profile of v3, /device:TPU:22, one launch (start us, length us, event | category | flops | bytes accessed | tf_op | source)
XLA Modules:
  0.0 52.0 jit_solution(7502795567285812096)
XLA Ops:
  0.0 1.6 %shard_map.82 = (f32[2,125,8,128]{3,2,1,0:T(8,128)S(1)}, f32[5,5]{1,0:T(8,128)S(1)}, f32[1,5]{1,0:T(1,128)S(1)}, f32[8,128]{1,0:T(8,128)S(1)}, f32[25,8,128]{2,1...) custom-call(f32[4,125,4,128]{3,2,1,0:T(4,128)} %bitcast.10, ...), custom_call_target="tpu_custom_call" | custom-call | tf_op jit(solution)/shard_map/pallas_call | solution.py:795
  1.6 0.6 %collective-permute-start = (f32[25,8,128]{2,1,0:T(8,128)S(1)}, f32[25,8,128]{2,1,0:T(8,128)S(1)}, u32[]{:S(2)}, u32[]{:S(2)}) collective-permute-start(f32[25,8,128]{2,1,0:T(8,128)S(1)} %get-tuple-element.44), channel_id=1, source_target_pairs={{0,4},{4,0},{8,12},{12,8},{16,20},{20,16},{24,28},{28,24},{1,5},{5... | collective-permute-start | bytes 307208 | tf_op jit(solution)/shard_map/ppermute | solution.py:779
  2.2 4.4 %collective-permute-start.1 = (f32[25,8,128]{2,1,0:T(8,128)S(1)}, f32[25,8,128]{2,1,0:T(8,128)S(1)}, u32[]{:S(2)}, u32[]{:S(2)}) collective-permute-start(f32[25,8,128]{2,1,0:T(8,128)S(1)} %get-tuple-element.45), channel_id=1, source_target_pairs={{4,8},{8,4},{12,16},{16,12},{20,24},{24,20},{5,9},{9,5},{13,17},{1... | collective-permute-start | bytes 307208 | tf_op jit(solution)/shard_map/ppermute | solution.py:779
  6.6 0.1 collective-permute-start.2
  6.7 2.5 %collective-permute-start.3 = (f32[25,8,128]{2,1,0:T(8,128)S(1)}, f32[25,8,128]{2,1,0:T(8,128)S(1)}, u32[]{:S(2)}, u32[]{:S(2)}) collective-permute-start(f32[25,8,128]{2,1,0:T(8,128)S(1)} %get-tuple-element.47), channel_id=1, source_target_pairs={{1,2},{2,1},{5,6},{6,5},{9,10},{10,9},{13,14},{14,13},{17,18},{18,... | collective-permute-start | bytes 307208 | tf_op jit(solution)/shard_map/ppermute | solution.py:779
  9.2 2.2 %shard_map.83 = (f32[2,125,8,128]{3,2,1,0:T(8,128)S(1)}, f32[2,125,8,128]{3,2,1,0:T(8,128)S(1)}, f32[2,8,8,128]{3,2,1,0:T(8,128)S(1)}, f32[35,8,128]{2,1,0:T(8,128)S(1)}, f32[35,8,128]{2,1,0:T(8,128)S(1)}) custom-call(f32[5,5]{1,0:T(8,128)S(1)} %get-tuple-element.39.basis_in, f32[1,5]{1,0:T(1,128)S(1)} %get-tuple-element.40.lam_in, ...), custom_call_target="tpu_custom_call" | custom-call | tf_op jit(solution)/shard_map/pallas_call | solution.py:810
  11.5 0.0 collective-permute-done.fx0
  11.5 0.0 collective-permute-done.2.fy0
  11.5 1.1 %collective-permute-done.3.fy1 = f32[25,8,128]{2,1,0:T(8,128)S(1)} collective-permute-done((f32[25,8,128]{2,1,0:T(8,128)S(1)}, f32[25,8,128]{2,1,0:T(8,128)S(1)}, u32[]{:S(2)}, u32[]{:S(2)}) %collective-permute-start.3) | collective-permute-done | bytes 102432 | tf_op jit(solution)/shard_map/ppermute | solution.py:779
  12.7 1.8 %shard_map.84 = (f32[2,125,8,128]{3,2,1,0:T(8,128)S(1)}, f32[2,8,8,128]{3,2,1,0:T(8,128)S(1)}, f32[2,4,8,128]{3,2,1,0:T(8,128)S(1)}, f32[2,4,8,128]{3,2,1,0:T(8,...) custom-call(f32[35,8,128]{2,1,0:T(8,128)S(1)} %get-tuple-element.43., ...), custom_call_target="tpu_custom_call" | custom-call | tf_op jit(solution)/shard_map/pallas_call | solution.py:817
  14.5 0.0 copy-start.1
  14.5 0.1 collective-permute-start.4
  14.5 2.3 %collective-permute-start.5 = (f32[16,8,128]{2,1,0:T(8,128)S(1)}, f32[16,8,128]{2,1,0:T(8,128)S(1)}, u32[]{:S(2)}, u32[]{:S(2)}) collective-permute-start(f32[16,8,128]{2,1,0:T(8,128)S(1)} %get-tuple-element.52), channel_id=1, source_target_pairs={{4,8},{8,4},{12,16},{16,12},{20,24},{24,20},{5,9},{9,5},{13,17},{1... | collective-permute-start | bytes 196616 | tf_op jit(solution)/shard_map/ppermute | solution.py:779
  16.9 2.0 %collective-permute-done.4.rx0 = f32[16,8,128]{2,1,0:T(8,128)S(1)} collective-permute-done((f32[16,8,128]{2,1,0:T(8,128)S(1)}, f32[16,8,128]{2,1,0:T(8,128)S(1)}, u32[]{:S(2)}, u32[]{:S(2)}) %collective-permute-start.4) | collective-permute-done | bytes 65568 | tf_op jit(solution)/shard_map/ppermute | solution.py:779
  18.8 2.8 %collective-permute-done.5.rx1 = f32[16,8,128]{2,1,0:T(8,128)S(1)} collective-permute-done((f32[16,8,128]{2,1,0:T(8,128)S(1)}, f32[16,8,128]{2,1,0:T(8,128)S(1)}, u32[]{:S(2)}, u32[]{:S(2)}) %collective-permute-start.5) | collective-permute-done | bytes 65568 | tf_op jit(solution)/shard_map/ppermute | solution.py:779
  21.7 0.1 collective-permute-start.6
  21.7 1.9 %collective-permute-start.7 = (f32[24,8,128]{2,1,0:T(8,128)S(1)}, f32[24,8,128]{2,1,0:T(8,128)S(1)}, u32[]{:S(2)}, u32[]{:S(2)}) collective-permute-start(f32[24,8,128]{2,1,0:T(8,128)S(1)} %get-tuple-element.57), channel_id=1, source_target_pairs={{1,2},{2,1},{5,6},{6,5},{9,10},{10,9},{13,14},{14,13},{17,18},{18,... | collective-permute-start | bytes 294920 | tf_op jit(solution)/shard_map/ppermute | solution.py:779
  23.7 0.0 collective-permute-done.6.ry0
  23.7 4.0 %collective-permute-done.7.ry1 = f32[24,8,128]{2,1,0:T(8,128)S(1)} collective-permute-done((f32[24,8,128]{2,1,0:T(8,128)S(1)}, f32[24,8,128]{2,1,0:T(8,128)S(1)}, u32[]{:S(2)}, u32[]{:S(2)}) %collective-permute-start.7) | collective-permute-done | bytes 98336 | tf_op jit(solution)/shard_map/ppermute | solution.py:779
  27.7 3.1 %shard_map.86 = (f32[64,8,128]{2,1,0:T(8,128)S(1)}, f32[24,8,128]{2,1,0:T(8,128)S(1)}, f32[24,8,128]{2,1,0:T(8,128)S(1)}) custom-call(f32[24,8,128]{2,1,0:T(8,128)S(1)} %collective-permute-done.6.ry0, f32[24,8,128]{2,1,0:T(8,128)S(1)} %collective-permute-done.7.ry1, f32[2,8,8,128]{3,2,1,0:T(8,128)S(1)} %get-tuple-element.58.c1, ...), custom_call_target="tpu_custom_call" | custom-call | tf_op jit(solution)/shard_map/pallas_call | solution.py:850
  30.8 0.1 collective-permute-start.8
  30.8 2.1 %collective-permute-start.12 = (f32[25,8,128]{2,1,0:T(8,128)S(1)}, f32[25,8,128]{2,1,0:T(8,128)S(1)}, u32[]{:S(2)}, u32[]{:S(2)}) collective-permute-start(f32[25,8,128]{2,1,0:T(8,128)S(1)} %get-tuple-element.69), channel_id=1, source_target_pairs={{0,4},{4,0},{8,12},{12,8},{16,20},{20,16},{24,28},{28,24},{1,5},{5... | collective-permute-start | bytes 307208 | tf_op jit(solution)/shard_map/ppermute | solution.py:779
  32.9 1.9 %collective-permute-start.9 = (f32[24,8,128]{2,1,0:T(8,128)S(1)}, f32[24,8,128]{2,1,0:T(8,128)S(1)}, u32[]{:S(2)}, u32[]{:S(2)}) collective-permute-start(f32[24,8,128]{2,1,0:T(8,128)S(1)} %get-tuple-element.63), channel_id=1, source_target_pairs={{1,2},{2,1},{5,6},{6,5},{9,10},{10,9},{13,14},{14,13},{17,18},{18,... | collective-permute-start | bytes 294920 | tf_op jit(solution)/shard_map/ppermute | solution.py:779
  34.8 1.9 %collective-permute-start.13 = (f32[25,8,128]{2,1,0:T(8,128)S(1)}, f32[25,8,128]{2,1,0:T(8,128)S(1)}, u32[]{:S(2)}, u32[]{:S(2)}) collective-permute-start(f32[25,8,128]{2,1,0:T(8,128)S(1)} %get-tuple-element.70), channel_id=1, source_target_pairs={{4,8},{8,4},{12,16},{16,12},{20,24},{24,20},{5,9},{9,5},{13,17},{1... | collective-permute-start | bytes 307208 | tf_op jit(solution)/shard_map/ppermute | solution.py:779
  36.7 0.1 collective-permute-start.14
  36.8 3.6 %collective-permute-start.15 = (f32[25,8,128]{2,1,0:T(8,128)S(1)}, f32[25,8,128]{2,1,0:T(8,128)S(1)}, u32[]{:S(2)}, u32[]{:S(2)}) collective-permute-start(f32[25,8,128]{2,1,0:T(8,128)S(1)} %get-tuple-element.72), channel_id=1, source_target_pairs={{1,2},{2,1},{5,6},{6,5},{9,10},{10,9},{13,14},{14,13},{17,18},{18,... | collective-permute-start | bytes 307208 | tf_op jit(solution)/shard_map/ppermute | solution.py:779
  40.5 0.0 collective-permute-done.9.r1
  40.6 1.7 %collective-permute-start.10 = (f32[16,8,128]{2,1,0:T(8,128)S(1)}, f32[16,8,128]{2,1,0:T(8,128)S(1)}, u32[]{:S(2)}, u32[]{:S(2)}) collective-permute-start(f32[16,8,128]{2,1,0:T(8,128)S(1)} %get-tuple-element.65), channel_id=1, source_target_pairs={{0,4},{4,0},{8,12},{12,8},{16,20},{20,16},{24,28},{28,24},{1,5},{5... | collective-permute-start | bytes 196616 | tf_op jit(solution)/shard_map/ppermute | solution.py:779
  42.2 2.9 %collective-permute-start.11 = (f32[16,8,128]{2,1,0:T(8,128)S(1)}, f32[16,8,128]{2,1,0:T(8,128)S(1)}, u32[]{:S(2)}, u32[]{:S(2)}) collective-permute-start(f32[16,8,128]{2,1,0:T(8,128)S(1)} %get-tuple-element.66), channel_id=1, source_target_pairs={{4,8},{8,4},{12,16},{16,12},{20,24},{24,20},{5,9},{9,5},{13,17},{1... | collective-permute-start | bytes 196616 | tf_op jit(solution)/shard_map/ppermute | solution.py:779
  45.2 1.3 %shard_map.88.modal = f32[2,125,8,128]{3,2,1,0:T(8,128)S(1)} custom-call(f32[35,8,128]{2,1,0:T(8,128)S(1)} %get-tuple-element.43.basis, f32[2,125,8,128]{3,2,1,0:T(8,128)S(1)} %get-tuple-element.67.u1, f32[2,125,8,128]{3,2,1,0:T(8,128)S(1)} %get-tuple-element.68.rhs, f32[25,8,128]{2,1,0:T(8,128)S(1)} %collective-permute-done.12.rx0, ...), custom_call_target="tpu_custom_call" | custom-call | tf_op jit(solution)/shard_map/pallas_call | solution.py:855
  46.6 2.7 %collective-permute-done.11.r1 = f32[16,8,128]{2,1,0:T(8,128)S(1)} collective-permute-done((f32[16,8,128]{2,1,0:T(8,128)S(1)}, f32[16,8,128]{2,1,0:T(8,128)S(1)}, u32[]{:S(2)}, u32[]{:S(2)}) %collective-permute-start.11) | collective-permute-done | bytes 65568 | tf_op jit(solution)/shard_map/ppermute | solution.py:779
  49.3 2.7 %shard_map.89 = f32[4,125,4,128]{3,2,1,0:T(4,128)} custom-call(f32[35,8,128]{2,1,0:T(8,128)S(1)} %get-tuple-element.43.basis, f32[64,8,128]{2,1,0:T(8,128)S(1)} %get-tuple-element.64.s, f32[16,8,128]{2,1,0:T(8,128)S(1)} %collective-permute-done.10.r0, f32[16,8,128]{2,1,0:T(8,128)S(1)} %collective-permute-done.11.r1, ...), custom_call_target="tpu_custom_call" | custom-call | tf_op jit(solution)/shard_map/pallas_call | solution.py:857
  (16 shorter events, 0.1 us)
Async XLA Ops:
  0.0 9.2 %copy-start = (f32[4,5,5,5,2,2,128]{6,5,4,3,2,1,0:T(2,128)S(1)}, f32[4,5,5,5,2,2,128]{6,5,4,3,2,1,0:T(2,128)}, u32[]{:S(2)}) copy-start(f32[4,5,5,5,2,2,128]{6,5,4,3,2,1,0:T(2,128)} %param.8) | copy-start | bytes 3072004
  1.6 9.9 %collective-permute-start = (f32[25,8,128]{2,1,0:T(8,128)S(1)}, f32[25,8,128]{2,1,0:T(8,128)S(1)}, u32[]{:S(2)}, u32[]{:S(2)}) collective-permute-start(f32[25,8,128]{2,1,0:T(8,128)S(1)} %get-tuple-element.44), channel_id=1, source_target_pairs={{0,4},{4,0},{8,12},{12,8},{16,20},{20,16},{24,28},{28,24},{1,5},{5... | collective-permute-start | bytes 307208 | tf_op jit(solution)/shard_map/ppermute | solution.py:779
  2.2 9.3 %collective-permute-start.1 = (f32[25,8,128]{2,1,0:T(8,128)S(1)}, f32[25,8,128]{2,1,0:T(8,128)S(1)}, u32[]{:S(2)}, u32[]{:S(2)}) collective-permute-start(f32[25,8,128]{2,1,0:T(8,128)S(1)} %get-tuple-element.45), channel_id=1, source_target_pairs={{4,8},{8,4},{12,16},{16,12},{20,24},{24,20},{5,9},{9,5},{13,17},{1... | collective-permute-start | bytes 307208 | tf_op jit(solution)/shard_map/ppermute | solution.py:779
  6.6 4.9 %collective-permute-start.2 = (f32[25,8,128]{2,1,0:T(8,128)S(1)}, f32[25,8,128]{2,1,0:T(8,128)S(1)}, u32[]{:S(2)}, u32[]{:S(2)}) collective-permute-start(f32[25,8,128]{2,1,0:T(8,128)S(1)} %get-tuple-element.46), channel_id=1, source_target_pairs={{0,1},{1,0},{2,3},{3,2},{4,5},{5,4},{6,7},{7,6},{8,9},{9,8},{10,11... | collective-permute-start | bytes 307208 | tf_op jit(solution)/shard_map/ppermute | solution.py:779
  6.7 6.0 %collective-permute-start.3 = (f32[25,8,128]{2,1,0:T(8,128)S(1)}, f32[25,8,128]{2,1,0:T(8,128)S(1)}, u32[]{:S(2)}, u32[]{:S(2)}) collective-permute-start(f32[25,8,128]{2,1,0:T(8,128)S(1)} %get-tuple-element.47), channel_id=1, source_target_pairs={{1,2},{2,1},{5,6},{6,5},{9,10},{10,9},{13,14},{14,13},{17,18},{18,... | collective-permute-start | bytes 307208 | tf_op jit(solution)/shard_map/ppermute | solution.py:779
  12.6 15.0 %copy-start.3 = (s32[512,8]{0,1:T(8,128)S(1)}, s32[512,8]{0,1:T(8,128)}, u32[]{:S(2)}) copy-start(s32[512,8]{0,1:T(8,128)} %param.15) | copy-start | bytes 49156
  14.5 13.2 %copy-start.1 = (f32[256,256]{1,0:T(8,128)S(1)}, f32[256,256]{1,0:T(8,128)}, u32[]{:S(2)}) copy-start(f32[256,256]{1,0:T(8,128)} %inverse.1) | copy-start | bytes 786436
  14.5 4.4 %collective-permute-start.4 = (f32[16,8,128]{2,1,0:T(8,128)S(1)}, f32[16,8,128]{2,1,0:T(8,128)S(1)}, u32[]{:S(2)}, u32[]{:S(2)}) collective-permute-start(f32[16,8,128]{2,1,0:T(8,128)S(1)} %get-tuple-element.51), channel_id=1, source_target_pairs={{0,4},{4,0},{8,12},{12,8},{16,20},{20,16},{24,28},{28,24},{1,5},{5... | collective-permute-start | bytes 196616 | tf_op jit(solution)/shard_map/ppermute | solution.py:779
  14.5 7.1 %collective-permute-start.5 = (f32[16,8,128]{2,1,0:T(8,128)S(1)}, f32[16,8,128]{2,1,0:T(8,128)S(1)}, u32[]{:S(2)}, u32[]{:S(2)}) collective-permute-start(f32[16,8,128]{2,1,0:T(8,128)S(1)} %get-tuple-element.52), channel_id=1, source_target_pairs={{4,8},{8,4},{12,16},{16,12},{20,24},{24,20},{5,9},{9,5},{13,17},{1... | collective-permute-start | bytes 196616 | tf_op jit(solution)/shard_map/ppermute | solution.py:779
  21.6 6.1 %copy-start.2 = (s32[512,8]{0,1:T(8,128)S(1)}, s32[512,8]{0,1:T(8,128)}, u32[]{:S(2)}) copy-start(s32[512,8]{0,1:T(8,128)} %param.14) | copy-start | bytes 49156
  21.7 2.0 %collective-permute-start.6 = (f32[24,8,128]{2,1,0:T(8,128)S(1)}, f32[24,8,128]{2,1,0:T(8,128)S(1)}, u32[]{:S(2)}, u32[]{:S(2)}) collective-permute-start(f32[24,8,128]{2,1,0:T(8,128)S(1)} %get-tuple-element.56), channel_id=1, source_target_pairs={{0,1},{1,0},{2,3},{3,2},{4,5},{5,4},{6,7},{7,6},{8,9},{9,8},{10,11... | collective-permute-start | bytes 294920 | tf_op jit(solution)/shard_map/ppermute | solution.py:779
  21.7 5.9 %collective-permute-start.7 = (f32[24,8,128]{2,1,0:T(8,128)S(1)}, f32[24,8,128]{2,1,0:T(8,128)S(1)}, u32[]{:S(2)}, u32[]{:S(2)}) collective-permute-start(f32[24,8,128]{2,1,0:T(8,128)S(1)} %get-tuple-element.57), channel_id=1, source_target_pairs={{1,2},{2,1},{5,6},{6,5},{9,10},{10,9},{13,14},{14,13},{17,18},{18,... | collective-permute-start | bytes 294920 | tf_op jit(solution)/shard_map/ppermute | solution.py:779
  30.8 6.1 %collective-permute-start.8 = (f32[24,8,128]{2,1,0:T(8,128)S(1)}, f32[24,8,128]{2,1,0:T(8,128)S(1)}, u32[]{:S(2)}, u32[]{:S(2)}) collective-permute-start(f32[24,8,128]{2,1,0:T(8,128)S(1)} %get-tuple-element.62), channel_id=1, source_target_pairs={{0,1},{1,0},{2,3},{3,2},{4,5},{5,4},{6,7},{7,6},{8,9},{9,8},{10,11... | collective-permute-start | bytes 294920 | tf_op jit(solution)/shard_map/ppermute | solution.py:779
  30.8 11.4 %collective-permute-start.12 = (f32[25,8,128]{2,1,0:T(8,128)S(1)}, f32[25,8,128]{2,1,0:T(8,128)S(1)}, u32[]{:S(2)}, u32[]{:S(2)}) collective-permute-start(f32[25,8,128]{2,1,0:T(8,128)S(1)} %get-tuple-element.69), channel_id=1, source_target_pairs={{0,4},{4,0},{8,12},{12,8},{16,20},{20,16},{24,28},{28,24},{1,5},{5... | collective-permute-start | bytes 307208 | tf_op jit(solution)/shard_map/ppermute | solution.py:779
  32.9 7.6 %collective-permute-start.9 = (f32[24,8,128]{2,1,0:T(8,128)S(1)}, f32[24,8,128]{2,1,0:T(8,128)S(1)}, u32[]{:S(2)}, u32[]{:S(2)}) collective-permute-start(f32[24,8,128]{2,1,0:T(8,128)S(1)} %get-tuple-element.63), channel_id=1, source_target_pairs={{1,2},{2,1},{5,6},{6,5},{9,10},{10,9},{13,14},{14,13},{17,18},{18,... | collective-permute-start | bytes 294920 | tf_op jit(solution)/shard_map/ppermute | solution.py:779
  34.8 10.4 %collective-permute-start.13 = (f32[25,8,128]{2,1,0:T(8,128)S(1)}, f32[25,8,128]{2,1,0:T(8,128)S(1)}, u32[]{:S(2)}, u32[]{:S(2)}) collective-permute-start(f32[25,8,128]{2,1,0:T(8,128)S(1)} %get-tuple-element.70), channel_id=1, source_target_pairs={{4,8},{8,4},{12,16},{16,12},{20,24},{24,20},{5,9},{9,5},{13,17},{1... | collective-permute-start | bytes 307208 | tf_op jit(solution)/shard_map/ppermute | solution.py:779
  36.7 8.5 %collective-permute-start.14 = (f32[25,8,128]{2,1,0:T(8,128)S(1)}, f32[25,8,128]{2,1,0:T(8,128)S(1)}, u32[]{:S(2)}, u32[]{:S(2)}) collective-permute-start(f32[25,8,128]{2,1,0:T(8,128)S(1)} %get-tuple-element.71), channel_id=1, source_target_pairs={{0,1},{1,0},{2,3},{3,2},{4,5},{5,4},{6,7},{7,6},{8,9},{9,8},{10,11... | collective-permute-start | bytes 307208 | tf_op jit(solution)/shard_map/ppermute | solution.py:779
  36.8 8.4 %collective-permute-start.15 = (f32[25,8,128]{2,1,0:T(8,128)S(1)}, f32[25,8,128]{2,1,0:T(8,128)S(1)}, u32[]{:S(2)}, u32[]{:S(2)}) collective-permute-start(f32[25,8,128]{2,1,0:T(8,128)S(1)} %get-tuple-element.72), channel_id=1, source_target_pairs={{1,2},{2,1},{5,6},{6,5},{9,10},{10,9},{13,14},{14,13},{17,18},{18,... | collective-permute-start | bytes 307208 | tf_op jit(solution)/shard_map/ppermute | solution.py:779
  40.6 6.0 %collective-permute-start.10 = (f32[16,8,128]{2,1,0:T(8,128)S(1)}, f32[16,8,128]{2,1,0:T(8,128)S(1)}, u32[]{:S(2)}, u32[]{:S(2)}) collective-permute-start(f32[16,8,128]{2,1,0:T(8,128)S(1)} %get-tuple-element.65), channel_id=1, source_target_pairs={{0,4},{4,0},{8,12},{12,8},{16,20},{20,16},{24,28},{28,24},{1,5},{5... | collective-permute-start | bytes 196616 | tf_op jit(solution)/shard_map/ppermute | solution.py:779
  42.2 7.0 %collective-permute-start.11 = (f32[16,8,128]{2,1,0:T(8,128)S(1)}, f32[16,8,128]{2,1,0:T(8,128)S(1)}, u32[]{:S(2)}, u32[]{:S(2)}) collective-permute-start(f32[16,8,128]{2,1,0:T(8,128)S(1)} %get-tuple-element.66), channel_id=1, source_target_pairs={{4,8},{8,4},{12,16},{16,12},{20,24},{24,20},{5,9},{9,5},{13,17},{1... | collective-permute-start | bytes 196616 | tf_op jit(solution)/shard_map/ppermute | solution.py:779

commit v4 on v3

--- a/solution.py
+++ b/solution.py
@@ -242,7 +242,7 @@
             basis[i * NODES + a] = jnp.broadcast_to(basis_in[i : i + 1, a : a + 1], (SUB, LANES))
     lam = [jnp.broadcast_to(lam_in[0:1, a : a + 1], (SUB, LANES)) for a in range(NODES)]
     for t, (a, b, c) in enumerate(TRIPLES):
-        invd[t] = 1.0 / (scale * (lam[a] + lam[b] + lam[c]) + MASS_SHIFT)
+        invd[t] = DAMPING / (scale * (lam[a] + lam[b] + lam[c]) + MASS_SHIFT)
     for c in (0, 1):
         modal = []
         for m in range(NODES):
@@ -339,7 +339,7 @@
             return vals
 
         def finish(n, v):
-            u1[g, n] = KEPT * u[g, n] + DAMPING * v
+            u1[g, n] = KEPT * u[g, n] + v
 
         from_modal(modal_plane, finish, basis, work)
 
@@ -704,7 +704,6 @@
         for group in (faces_x, faces_y, faces_z):
             for end in (0, 1):
                 group[end] = [FACE_PENALTY * v for v in group[end]]
-        share = KEPT / DAMPING
 
         def modal_plane(a):
             ends = [basis[a], basis[TOP * NODES + a]]
@@ -712,7 +711,7 @@
             along_x = [combine(ends, [faces_x[0][n], faces_x[1][n]]) for n in range(4)]
             along_y = [[combine(thin, [faces_y[e][q], faces_y[e][2 + q]]) for q in (0, 1)] for e in (0, 1)]
             along_z = [[combine(thin, [faces_z[e][q], faces_z[e][2 + q]]) for q in (0, 1)] for e in (0, 1)]
-            fine = [share * combine(thin, [coarse[n], coarse[4 + n]]) for n in range(4)]
+            fine = [KEPT * combine(thin, [coarse[n], coarse[4 + n]]) for n in range(4)]
             vals = []
             for b in range(NODES):
                 ends_b = [basis[b], basis[TOP * NODES + b]]
@@ -731,7 +730,7 @@
             return vals
 
         def finish(n, v):
-            out[g, n] = KEPT * u1[g, n] + DAMPING * v
+            out[g, n] = KEPT * u1[g, n] + v
 
         from_modal(modal_plane, finish, basis, work)
         for c in put_out(g):

time: 52.9 us -> 52.9 us (level)
  no operation moved by 1% of the time
where the time goes in v4:
time: 52.9 us; the launch traced here: 51.9 us
  starting transfers between devices  26.3 us (50%)
  Pallas kernels  12.7 us (24%)
  waiting for transfers between devices  12.6 us (24%)
    ppermute x16, starting transfers between devices, swaps(): got[colour] = lax.ppermute((m0, m1)[colour], axis, pairs)  26.3 us
    ppermute x16, waiting for transfers between devices, swaps(): got[colour] = lax.ppermute((m0, m1)[colour], axis, pairs)  12.6 us
    pallas_call x1, Pallas kernels, per_device(): patches(*ry, c1, ring, ypk, patch_elements.T, patch_mask.T, patch_inverse)  3.07 us
    pallas_call x1, Pallas kernels, per_device(): call(last_kernel, [VMEM] * 7, jax.ShapeDtypeStruct(flat, F32), HBM, [pltp...  2.62 us
    pallas_call x1, Pallas kernels, per_device(): call(local_kernel, [VMEM, VMEM, VMEM, VMEM, HBM], [regs(2, CUBE), regs(2,...  2.25 us
    pallas_call x1, Pallas kernels, per_device(): call(first_kernel, [VMEM] * 9, [regs(2, CUBE), regs(2, 8), regs(2, 4), re...  1.78 us
    pallas_call x1, Pallas kernels, per_device(): call(faces_kernel, [HBM] * 4, [regs(2, CUBE), jax.ShapeDtypeStruct((NODES...  1.57 us
    pallas_call x1, Pallas kernels, per_device(): modal = early(basis, u1, rhs, *ux, *uy)  1.33 us
  transfers between devices with their start and end apart: 16, of which 5 were waited for; matrix products, arithmetic and copies ran while one was open for 0% of the time, Pallas kernels for 7%

profile of v4, /device:TPU:22, one launch (start us, length us, event | category | flops | bytes accessed | tf_op | source)
XLA Modules:
  0.0 51.9 jit_solution(5479978213361273681)
XLA Ops:
  0.0 1.6 %shard_map.82 = (f32[2,125,8,128]{3,2,1,0:T(8,128)S(1)}, f32[5,5]{1,0:T(8,128)S(1)}, f32[1,5]{1,0:T(1,128)S(1)}, f32[8,128]{1,0:T(8,128)S(1)}, f32[25,8,128]{2,1...) custom-call(f32[4,125,4,128]{3,2,1,0:T(4,128)} %bitcast.10, ...), custom_call_target="tpu_custom_call" | custom-call | tf_op jit(solution)/shard_map/pallas_call | solution.py:794
  1.6 0.6 %collective-permute-start = (f32[25,8,128]{2,1,0:T(8,128)S(1)}, f32[25,8,128]{2,1,0:T(8,128)S(1)}, u32[]{:S(2)}, u32[]{:S(2)}) collective-permute-start(f32[25,8,128]{2,1,0:T(8,128)S(1)} %get-tuple-element.44), channel_id=1, source_target_pairs={{0,4},{4,0},{8,12},{12,8},{16,20},{20,16},{24,28},{28,24},{1,5},{5... | collective-permute-start | bytes 307208 | tf_op jit(solution)/shard_map/ppermute | solution.py:778
  2.2 4.4 %collective-permute-start.1 = (f32[25,8,128]{2,1,0:T(8,128)S(1)}, f32[25,8,128]{2,1,0:T(8,128)S(1)}, u32[]{:S(2)}, u32[]{:S(2)}) collective-permute-start(f32[25,8,128]{2,1,0:T(8,128)S(1)} %get-tuple-element.45), channel_id=1, source_target_pairs={{4,8},{8,4},{12,16},{16,12},{20,24},{24,20},{5,9},{9,5},{13,17},{1... | collective-permute-start | bytes 307208 | tf_op jit(solution)/shard_map/ppermute | solution.py:778
  6.6 0.1 collective-permute-start.2
  6.7 2.5 %collective-permute-start.3 = (f32[25,8,128]{2,1,0:T(8,128)S(1)}, f32[25,8,128]{2,1,0:T(8,128)S(1)}, u32[]{:S(2)}, u32[]{:S(2)}) collective-permute-start(f32[25,8,128]{2,1,0:T(8,128)S(1)} %get-tuple-element.47), channel_id=1, source_target_pairs={{1,2},{2,1},{5,6},{6,5},{9,10},{10,9},{13,14},{14,13},{17,18},{18,... | collective-permute-start | bytes 307208 | tf_op jit(solution)/shard_map/ppermute | solution.py:778
  9.2 2.3 %shard_map.83 = (f32[2,125,8,128]{3,2,1,0:T(8,128)S(1)}, f32[2,125,8,128]{3,2,1,0:T(8,128)S(1)}, f32[2,8,8,128]{3,2,1,0:T(8,128)S(1)}, f32[35,8,128]{2,1,0:T(8,128)S(1)}, f32[35,8,128]{2,1,0:T(8,128)S(1)}) custom-call(f32[5,5]{1,0:T(8,128)S(1)} %get-tuple-element.39.basis_in, f32[1,5]{1,0:T(1,128)S(1)} %get-tuple-element.40.lam_in, ...), custom_call_target="tpu_custom_call" | custom-call | tf_op jit(solution)/shard_map/pallas_call | solution.py:809
  11.5 0.0 collective-permute-done.2.fy0
  11.5 1.1 %collective-permute-done.3.fy1 = f32[25,8,128]{2,1,0:T(8,128)S(1)} collective-permute-done((f32[25,8,128]{2,1,0:T(8,128)S(1)}, f32[25,8,128]{2,1,0:T(8,128)S(1)}, u32[]{:S(2)}, u32[]{:S(2)}) %collective-permute-start.3) | collective-permute-done | bytes 102432 | tf_op jit(solution)/shard_map/ppermute | solution.py:778
  12.7 1.8 %shard_map.84 = (f32[2,125,8,128]{3,2,1,0:T(8,128)S(1)}, f32[2,8,8,128]{3,2,1,0:T(8,128)S(1)}, f32[2,4,8,128]{3,2,1,0:T(8,128)S(1)}, f32[2,4,8,128]{3,2,1,0:T(8,...) custom-call(f32[35,8,128]{2,1,0:T(8,128)S(1)} %get-tuple-element.43., ...), custom_call_target="tpu_custom_call" | custom-call | tf_op jit(solution)/shard_map/pallas_call | solution.py:816
  14.4 0.0 copy-start.1
  14.4 0.1 collective-permute-start.4
  14.5 2.3 %collective-permute-start.5 = (f32[16,8,128]{2,1,0:T(8,128)S(1)}, f32[16,8,128]{2,1,0:T(8,128)S(1)}, u32[]{:S(2)}, u32[]{:S(2)}) collective-permute-start(f32[16,8,128]{2,1,0:T(8,128)S(1)} %get-tuple-element.52), channel_id=1, source_target_pairs={{4,8},{8,4},{12,16},{16,12},{20,24},{24,20},{5,9},{9,5},{13,17},{1... | collective-permute-start | bytes 196616 | tf_op jit(solution)/shard_map/ppermute | solution.py:778
  16.8 2.0 %collective-permute-done.4.rx0 = f32[16,8,128]{2,1,0:T(8,128)S(1)} collective-permute-done((f32[16,8,128]{2,1,0:T(8,128)S(1)}, f32[16,8,128]{2,1,0:T(8,128)S(1)}, u32[]{:S(2)}, u32[]{:S(2)}) %collective-permute-start.4) | collective-permute-done | bytes 65568 | tf_op jit(solution)/shard_map/ppermute | solution.py:778
  18.8 2.8 %collective-permute-done.5.rx1 = f32[16,8,128]{2,1,0:T(8,128)S(1)} collective-permute-done((f32[16,8,128]{2,1,0:T(8,128)S(1)}, f32[16,8,128]{2,1,0:T(8,128)S(1)}, u32[]{:S(2)}, u32[]{:S(2)}) %collective-permute-start.5) | collective-permute-done | bytes 65568 | tf_op jit(solution)/shard_map/ppermute | solution.py:778
  21.6 0.1 collective-permute-start.6
  21.7 1.9 %collective-permute-start.7 = (f32[24,8,128]{2,1,0:T(8,128)S(1)}, f32[24,8,128]{2,1,0:T(8,128)S(1)}, u32[]{:S(2)}, u32[]{:S(2)}) collective-permute-start(f32[24,8,128]{2,1,0:T(8,128)S(1)} %get-tuple-element.57), channel_id=1, source_target_pairs={{1,2},{2,1},{5,6},{6,5},{9,10},{10,9},{13,14},{14,13},{17,18},{18,... | collective-permute-start | bytes 294920 | tf_op jit(solution)/shard_map/ppermute | solution.py:778
  23.6 0.0 collective-permute-done.6.ry0
  23.7 4.0 %collective-permute-done.7.ry1 = f32[24,8,128]{2,1,0:T(8,128)S(1)} collective-permute-done((f32[24,8,128]{2,1,0:T(8,128)S(1)}, f32[24,8,128]{2,1,0:T(8,128)S(1)}, u32[]{:S(2)}, u32[]{:S(2)}) %collective-permute-start.7) | collective-permute-done | bytes 98336 | tf_op jit(solution)/shard_map/ppermute | solution.py:778
  27.7 3.1 %shard_map.86 = (f32[64,8,128]{2,1,0:T(8,128)S(1)}, f32[24,8,128]{2,1,0:T(8,128)S(1)}, f32[24,8,128]{2,1,0:T(8,128)S(1)}) custom-call(f32[24,8,128]{2,1,0:T(8,128)S(1)} %collective-permute-done.6.ry0, f32[24,8,128]{2,1,0:T(8,128)S(1)} %collective-permute-done.7.ry1, f32[2,8,8,128]{3,2,1,0:T(8,128)S(1)} %get-tuple-element.58.c1, ...), custom_call_target="tpu_custom_call" | custom-call | tf_op jit(solution)/shard_map/pallas_call | solution.py:849
  30.7 0.1 collective-permute-start.8
  30.8 2.1 %collective-permute-start.12 = (f32[25,8,128]{2,1,0:T(8,128)S(1)}, f32[25,8,128]{2,1,0:T(8,128)S(1)}, u32[]{:S(2)}, u32[]{:S(2)}) collective-permute-start(f32[25,8,128]{2,1,0:T(8,128)S(1)} %get-tuple-element.69), channel_id=1, source_target_pairs={{0,4},{4,0},{8,12},{12,8},{16,20},{20,16},{24,28},{28,24},{1,5},{5... | collective-permute-start | bytes 307208 | tf_op jit(solution)/shard_map/ppermute | solution.py:778
  32.9 1.9 %collective-permute-start.9 = (f32[24,8,128]{2,1,0:T(8,128)S(1)}, f32[24,8,128]{2,1,0:T(8,128)S(1)}, u32[]{:S(2)}, u32[]{:S(2)}) collective-permute-start(f32[24,8,128]{2,1,0:T(8,128)S(1)} %get-tuple-element.63), channel_id=1, source_target_pairs={{1,2},{2,1},{5,6},{6,5},{9,10},{10,9},{13,14},{14,13},{17,18},{18,... | collective-permute-start | bytes 294920 | tf_op jit(solution)/shard_map/ppermute | solution.py:778
  34.8 1.9 %collective-permute-start.13 = (f32[25,8,128]{2,1,0:T(8,128)S(1)}, f32[25,8,128]{2,1,0:T(8,128)S(1)}, u32[]{:S(2)}, u32[]{:S(2)}) collective-permute-start(f32[25,8,128]{2,1,0:T(8,128)S(1)} %get-tuple-element.70), channel_id=1, source_target_pairs={{4,8},{8,4},{12,16},{16,12},{20,24},{24,20},{5,9},{9,5},{13,17},{1... | collective-permute-start | bytes 307208 | tf_op jit(solution)/shard_map/ppermute | solution.py:778
  36.7 0.1 collective-permute-start.14
  36.8 3.6 %collective-permute-start.15 = (f32[25,8,128]{2,1,0:T(8,128)S(1)}, f32[25,8,128]{2,1,0:T(8,128)S(1)}, u32[]{:S(2)}, u32[]{:S(2)}) collective-permute-start(f32[25,8,128]{2,1,0:T(8,128)S(1)} %get-tuple-element.72), channel_id=1, source_target_pairs={{1,2},{2,1},{5,6},{6,5},{9,10},{10,9},{13,14},{14,13},{17,18},{18,... | collective-permute-start | bytes 307208 | tf_op jit(solution)/shard_map/ppermute | solution.py:778
  40.5 0.0 collective-permute-done.9.r1
  40.5 1.7 %collective-permute-start.10 = (f32[16,8,128]{2,1,0:T(8,128)S(1)}, f32[16,8,128]{2,1,0:T(8,128)S(1)}, u32[]{:S(2)}, u32[]{:S(2)}) collective-permute-start(f32[16,8,128]{2,1,0:T(8,128)S(1)} %get-tuple-element.65), channel_id=1, source_target_pairs={{0,4},{4,0},{8,12},{12,8},{16,20},{20,16},{24,28},{28,24},{1,5},{5... | collective-permute-start | bytes 196616 | tf_op jit(solution)/shard_map/ppermute | solution.py:778
  42.2 0.0 collective-permute-done.12.rx0
  42.2 2.9 %collective-permute-start.11 = (f32[16,8,128]{2,1,0:T(8,128)S(1)}, f32[16,8,128]{2,1,0:T(8,128)S(1)}, u32[]{:S(2)}, u32[]{:S(2)}) collective-permute-start(f32[16,8,128]{2,1,0:T(8,128)S(1)} %get-tuple-element.66), channel_id=1, source_target_pairs={{4,8},{8,4},{12,16},{16,12},{20,24},{24,20},{5,9},{9,5},{13,17},{1... | collective-permute-start | bytes 196616 | tf_op jit(solution)/shard_map/ppermute | solution.py:778
  45.2 1.3 %shard_map.88.modal = f32[2,125,8,128]{3,2,1,0:T(8,128)S(1)} custom-call(f32[35,8,128]{2,1,0:T(8,128)S(1)} %get-tuple-element.43.basis, f32[2,125,8,128]{3,2,1,0:T(8,128)S(1)} %get-tuple-element.67.u1, f32[2,125,8,128]{3,2,1,0:T(8,128)S(1)} %get-tuple-element.68.rhs, f32[25,8,128]{2,1,0:T(8,128)S(1)} %collective-permute-done.12.rx0, ...), custom_call_target="tpu_custom_call" | custom-call | tf_op jit(solution)/shard_map/pallas_call | solution.py:854
  46.5 2.7 %collective-permute-done.11.r1 = f32[16,8,128]{2,1,0:T(8,128)S(1)} collective-permute-done((f32[16,8,128]{2,1,0:T(8,128)S(1)}, f32[16,8,128]{2,1,0:T(8,128)S(1)}, u32[]{:S(2)}, u32[]{:S(2)}) %collective-permute-start.11) | collective-permute-done | bytes 65568 | tf_op jit(solution)/shard_map/ppermute | solution.py:778
  49.3 2.6 %shard_map.89 = f32[4,125,4,128]{3,2,1,0:T(4,128)} custom-call(f32[35,8,128]{2,1,0:T(8,128)S(1)} %get-tuple-element.43.basis, f32[64,8,128]{2,1,0:T(8,128)S(1)} %get-tuple-element.64.s, f32[16,8,128]{2,1,0:T(8,128)S(1)} %collective-permute-done.10.r0, f32[16,8,128]{2,1,0:T(8,128)S(1)} %collective-permute-done.11.r1, ...), custom_call_target="tpu_custom_call" | custom-call | tf_op jit(solution)/shard_map/pallas_call | solution.py:856
  (16 shorter events, 0.1 us)
Async XLA Ops:
  0.0 9.2 %copy-start = (f32[4,5,5,5,2,2,128]{6,5,4,3,2,1,0:T(2,128)S(1)}, f32[4,5,5,5,2,2,128]{6,5,4,3,2,1,0:T(2,128)}, u32[]{:S(2)}) copy-start(f32[4,5,5,5,2,2,128]{6,5,4,3,2,1,0:T(2,128)} %param.8) | copy-start | bytes 3072004
  1.6 9.9 %collective-permute-start = (f32[25,8,128]{2,1,0:T(8,128)S(1)}, f32[25,8,128]{2,1,0:T(8,128)S(1)}, u32[]{:S(2)}, u32[]{:S(2)}) collective-permute-start(f32[25,8,128]{2,1,0:T(8,128)S(1)} %get-tuple-element.44), channel_id=1, source_target_pairs={{0,4},{4,0},{8,12},{12,8},{16,20},{20,16},{24,28},{28,24},{1,5},{5... | collective-permute-start | bytes 307208 | tf_op jit(solution)/shard_map/ppermute | solution.py:778
  2.2 9.3 %collective-permute-start.1 = (f32[25,8,128]{2,1,0:T(8,128)S(1)}, f32[25,8,128]{2,1,0:T(8,128)S(1)}, u32[]{:S(2)}, u32[]{:S(2)}) collective-permute-start(f32[25,8,128]{2,1,0:T(8,128)S(1)} %get-tuple-element.45), channel_id=1, source_target_pairs={{4,8},{8,4},{12,16},{16,12},{20,24},{24,20},{5,9},{9,5},{13,17},{1... | collective-permute-start | bytes 307208 | tf_op jit(solution)/shard_map/ppermute | solution.py:778
  6.6 4.9 %collective-permute-start.2 = (f32[25,8,128]{2,1,0:T(8,128)S(1)}, f32[25,8,128]{2,1,0:T(8,128)S(1)}, u32[]{:S(2)}, u32[]{:S(2)}) collective-permute-start(f32[25,8,128]{2,1,0:T(8,128)S(1)} %get-tuple-element.46), channel_id=1, source_target_pairs={{0,1},{1,0},{2,3},{3,2},{4,5},{5,4},{6,7},{7,6},{8,9},{9,8},{10,11... | collective-permute-start | bytes 307208 | tf_op jit(solution)/shard_map/ppermute | solution.py:778
  6.7 6.0 %collective-permute-start.3 = (f32[25,8,128]{2,1,0:T(8,128)S(1)}, f32[25,8,128]{2,1,0:T(8,128)S(1)}, u32[]{:S(2)}, u32[]{:S(2)}) collective-permute-start(f32[25,8,128]{2,1,0:T(8,128)S(1)} %get-tuple-element.47), channel_id=1, source_target_pairs={{1,2},{2,1},{5,6},{6,5},{9,10},{10,9},{13,14},{14,13},{17,18},{18,... | collective-permute-start | bytes 307208 | tf_op jit(solution)/shard_map/ppermute | solution.py:778
  12.6 15.0 %copy-start.3 = (s32[512,8]{0,1:T(8,128)S(1)}, s32[512,8]{0,1:T(8,128)}, u32[]{:S(2)}) copy-start(s32[512,8]{0,1:T(8,128)} %param.15) | copy-start | bytes 49156
  14.4 13.2 %copy-start.1 = (f32[256,256]{1,0:T(8,128)S(1)}, f32[256,256]{1,0:T(8,128)}, u32[]{:S(2)}) copy-start(f32[256,256]{1,0:T(8,128)} %inverse.1) | copy-start | bytes 786436
  14.4 4.4 %collective-permute-start.4 = (f32[16,8,128]{2,1,0:T(8,128)S(1)}, f32[16,8,128]{2,1,0:T(8,128)S(1)}, u32[]{:S(2)}, u32[]{:S(2)}) collective-permute-start(f32[16,8,128]{2,1,0:T(8,128)S(1)} %get-tuple-element.51), channel_id=1, source_target_pairs={{0,4},{4,0},{8,12},{12,8},{16,20},{20,16},{24,28},{28,24},{1,5},{5... | collective-permute-start | bytes 196616 | tf_op jit(solution)/shard_map/ppermute | solution.py:778
  14.5 7.1 %collective-permute-start.5 = (f32[16,8,128]{2,1,0:T(8,128)S(1)}, f32[16,8,128]{2,1,0:T(8,128)S(1)}, u32[]{:S(2)}, u32[]{:S(2)}) collective-permute-start(f32[16,8,128]{2,1,0:T(8,128)S(1)} %get-tuple-element.52), channel_id=1, source_target_pairs={{4,8},{8,4},{12,16},{16,12},{20,24},{24,20},{5,9},{9,5},{13,17},{1... | collective-permute-start | bytes 196616 | tf_op jit(solution)/shard_map/ppermute | solution.py:778
  21.6 6.1 %copy-start.2 = (s32[512,8]{0,1:T(8,128)S(1)}, s32[512,8]{0,1:T(8,128)}, u32[]{:S(2)}) copy-start(s32[512,8]{0,1:T(8,128)} %param.14) | copy-start | bytes 49156
  21.6 2.0 %collective-permute-start.6 = (f32[24,8,128]{2,1,0:T(8,128)S(1)}, f32[24,8,128]{2,1,0:T(8,128)S(1)}, u32[]{:S(2)}, u32[]{:S(2)}) collective-permute-start(f32[24,8,128]{2,1,0:T(8,128)S(1)} %get-tuple-element.56), channel_id=1, source_target_pairs={{0,1},{1,0},{2,3},{3,2},{4,5},{5,4},{6,7},{7,6},{8,9},{9,8},{10,11... | collective-permute-start | bytes 294920 | tf_op jit(solution)/shard_map/ppermute | solution.py:778
  21.7 5.9 %collective-permute-start.7 = (f32[24,8,128]{2,1,0:T(8,128)S(1)}, f32[24,8,128]{2,1,0:T(8,128)S(1)}, u32[]{:S(2)}, u32[]{:S(2)}) collective-permute-start(f32[24,8,128]{2,1,0:T(8,128)S(1)} %get-tuple-element.57), channel_id=1, source_target_pairs={{1,2},{2,1},{5,6},{6,5},{9,10},{10,9},{13,14},{14,13},{17,18},{18,... | collective-permute-start | bytes 294920 | tf_op jit(solution)/shard_map/ppermute | solution.py:778
  30.7 6.1 %collective-permute-start.8 = (f32[24,8,128]{2,1,0:T(8,128)S(1)}, f32[24,8,128]{2,1,0:T(8,128)S(1)}, u32[]{:S(2)}, u32[]{:S(2)}) collective-permute-start(f32[24,8,128]{2,1,0:T(8,128)S(1)} %get-tuple-element.62), channel_id=1, source_target_pairs={{0,1},{1,0},{2,3},{3,2},{4,5},{5,4},{6,7},{7,6},{8,9},{9,8},{10,11... | collective-permute-start | bytes 294920 | tf_op jit(solution)/shard_map/ppermute | solution.py:778
  30.8 11.4 %collective-permute-start.12 = (f32[25,8,128]{2,1,0:T(8,128)S(1)}, f32[25,8,128]{2,1,0:T(8,128)S(1)}, u32[]{:S(2)}, u32[]{:S(2)}) collective-permute-start(f32[25,8,128]{2,1,0:T(8,128)S(1)} %get-tuple-element.69), channel_id=1, source_target_pairs={{0,4},{4,0},{8,12},{12,8},{16,20},{20,16},{24,28},{28,24},{1,5},{5... | collective-permute-start | bytes 307208 | tf_op jit(solution)/shard_map/ppermute | solution.py:778
  32.9 7.6 %collective-permute-start.9 = (f32[24,8,128]{2,1,0:T(8,128)S(1)}, f32[24,8,128]{2,1,0:T(8,128)S(1)}, u32[]{:S(2)}, u32[]{:S(2)}) collective-permute-start(f32[24,8,128]{2,1,0:T(8,128)S(1)} %get-tuple-element.63), channel_id=1, source_target_pairs={{1,2},{2,1},{5,6},{6,5},{9,10},{10,9},{13,14},{14,13},{17,18},{18,... | collective-permute-start | bytes 294920 | tf_op jit(solution)/shard_map/ppermute | solution.py:778
  34.8 10.4 %collective-permute-start.13 = (f32[25,8,128]{2,1,0:T(8,128)S(1)}, f32[25,8,128]{2,1,0:T(8,128)S(1)}, u32[]{:S(2)}, u32[]{:S(2)}) collective-permute-start(f32[25,8,128]{2,1,0:T(8,128)S(1)} %get-tuple-element.70), channel_id=1, source_target_pairs={{4,8},{8,4},{12,16},{16,12},{20,24},{24,20},{5,9},{9,5},{13,17},{1... | collective-permute-start | bytes 307208 | tf_op jit(solution)/shard_map/ppermute | solution.py:778
  36.7 8.5 %collective-permute-start.14 = (f32[25,8,128]{2,1,0:T(8,128)S(1)}, f32[25,8,128]{2,1,0:T(8,128)S(1)}, u32[]{:S(2)}, u32[]{:S(2)}) collective-permute-start(f32[25,8,128]{2,1,0:T(8,128)S(1)} %get-tuple-element.71), channel_id=1, source_target_pairs={{0,1},{1,0},{2,3},{3,2},{4,5},{5,4},{6,7},{7,6},{8,9},{9,8},{10,11... | collective-permute-start | bytes 307208 | tf_op jit(solution)/shard_map/ppermute | solution.py:778
  36.8 8.4 %collective-permute-start.15 = (f32[25,8,128]{2,1,0:T(8,128)S(1)}, f32[25,8,128]{2,1,0:T(8,128)S(1)}, u32[]{:S(2)}, u32[]{:S(2)}) collective-permute-start(f32[25,8,128]{2,1,0:T(8,128)S(1)} %get-tuple-element.72), channel_id=1, source_target_pairs={{1,2},{2,1},{5,6},{6,5},{9,10},{10,9},{13,14},{14,13},{17,18},{18,... | collective-permute-start | bytes 307208 | tf_op jit(solution)/shard_map/ppermute | solution.py:778
  40.5 6.0 %collective-permute-start.10 = (f32[16,8,128]{2,1,0:T(8,128)S(1)}, f32[16,8,128]{2,1,0:T(8,128)S(1)}, u32[]{:S(2)}, u32[]{:S(2)}) collective-permute-start(f32[16,8,128]{2,1,0:T(8,128)S(1)} %get-tuple-element.65), channel_id=1, source_target_pairs={{0,4},{4,0},{8,12},{12,8},{16,20},{20,16},{24,28},{28,24},{1,5},{5... | collective-permute-start | bytes 196616 | tf_op jit(solution)/shard_map/ppermute | solution.py:778
  42.2 7.0 %collective-permute-start.11 = (f32[16,8,128]{2,1,0:T(8,128)S(1)}, f32[16,8,128]{2,1,0:T(8,128)S(1)}, u32[]{:S(2)}, u32[]{:S(2)}) collective-permute-start(f32[16,8,128]{2,1,0:T(8,128)S(1)} %get-tuple-element.66), channel_id=1, source_target_pairs={{4,8},{8,4},{12,16},{16,12},{20,24},{24,20},{5,9},{9,5},{13,17},{1... | collective-permute-start | bytes 196616 | tf_op jit(solution)/shard_map/ppermute | solution.py:778

commit v5 on v4

--- a/solution.py
+++ b/solution.py
@@ -234,8 +234,7 @@
             )
 
 
-def local_kernel(basis_in, lam_in, coef, u, rhs_hbm, rhs, w, crd, invd, basis, wide_ref, work, sems):
-    copies = take_in(rhs_hbm, rhs, sems)
+def local_kernel(basis_in, lam_in, coef, u, rhs_in, rhs, w, crd, invd, basis, wide_ref, work):
     scale = coef[...]
     for i in range(NODES):
         for a in range(NODES):
@@ -251,8 +250,6 @@
             modal.append(lam[m] * v)
         for i in range(NODES):
             wide_ref[c * NODES + i] = combine([1.0] * NODES, [basis[i * NODES + m] * modal[m] for m in range(NODES)])
-    for cp in copies:
-        cp.wait()
 
     def pair(g, carry):
         def val(n):
@@ -263,7 +260,9 @@
             for j in range(NODES):
                 for k in range(NODES):
                     extra = couple(val, i, j, k)
-                    v = rhs[g, node(i, j, k)]
+                    n = node(i, j, k)
+                    v = jnp.concatenate([rhs_in[2 * g, n], rhs_in[2 * g + 1, n]], axis=0)
+                    rhs[g, n] = v
                     vals.append(v if extra is None else v + FACE_PENALTY * extra)
             return vals
 
@@ -808,10 +807,10 @@
     fy = swaps("py", fy0, fy1)
     rhs, w, crd, invd, basis = call(
         local_kernel,
-        [VMEM, VMEM, VMEM, VMEM, HBM],
+        [VMEM] * 5,
         [regs(2, CUBE), regs(2, CUBE), regs(2, 8), regs(len(TRIPLES)), regs(FACE + 2 * NODES)],
         [VMEM] * 5,
-        [pltpu.VMEM((2 * NODES, SUB, LANES), F32), work, field_sems],
+        [pltpu.VMEM((2 * NODES, SUB, LANES), F32), work],
     )(*few, u, right_side.reshape(flat))
     u1, c0, xpk, yf, ux0, ux1, uy0, uy1, mx0, mx1 = call(
         first_kernel,

time: 52.9 us -> 52.9 us (level)
  transfers between devices with their start and end apart: 16 -> 16, of which waited for: 5 -> 5; matrix products, arithmetic and copies ran while one was open for 0% -> 0% of each run, Pallas kernels for 7% -> 6%
where the time goes in v5:
time: 52.9 us; the launch traced here: 51.9 us
  starting transfers between devices  26.3 us (50%)
  waiting for transfers between devices  13 us (25%)
  Pallas kernels  12.4 us (23%)
    ppermute x16, starting transfers between devices, swaps(): got[colour] = lax.ppermute((m0, m1)[colour], axis, pairs)  26.3 us
    ppermute x16, waiting for transfers between devices, swaps(): got[colour] = lax.ppermute((m0, m1)[colour], axis, pairs)  13 us
    pallas_call x1, Pallas kernels, per_device(): patches(*ry, c1, ring, ypk, patch_elements.T, patch_mask.T, patch_inverse)  3.07 us
    pallas_call x1, Pallas kernels, per_device(): call(last_kernel, [VMEM] * 7, jax.ShapeDtypeStruct(flat, F32), HBM, [pltp...  2.62 us
    pallas_call x1, Pallas kernels, per_device(): call(local_kernel, [VMEM] * 5, [regs(2, CUBE), regs(2, CUBE), regs(2, 8),...  1.93 us
    pallas_call x1, Pallas kernels, per_device(): call(first_kernel, [VMEM] * 9, [regs(2, CUBE), regs(2, 8), regs(2, 4), re...  1.78 us
    pallas_call x1, Pallas kernels, per_device(): call(faces_kernel, [HBM] * 4, [regs(2, CUBE), jax.ShapeDtypeStruct((NODES...  1.57 us
    pallas_call x1, Pallas kernels, per_device(): modal = early(basis, u1, rhs, *ux, *uy)  1.33 us
  transfers between devices with their start and end apart: 16, of which 5 were waited for; matrix products, arithmetic and copies ran while one was open for 0% of the time, Pallas kernels for 6%

profile of v5, /device:TPU:22, one launch (start us, length us, event | category | flops | bytes accessed | tf_op | source)
XLA Modules:
  0.0 51.9 jit_solution(5941377296079860365)
XLA Ops:
  0.0 1.6 %shard_map.82 = (f32[2,125,8,128]{3,2,1,0:T(8,128)S(1)}, f32[5,5]{1,0:T(8,128)S(1)}, f32[1,5]{1,0:T(1,128)S(1)}, f32[8,128]{1,0:T(8,128)S(1)}, f32[25,8,128]{2,1...) custom-call(f32[4,125,4,128]{3,2,1,0:T(4,128)} %bitcast.10, ...), custom_call_target="tpu_custom_call" | custom-call | tf_op jit(solution)/shard_map/pallas_call | solution.py:793
  1.6 0.6 %collective-permute-start = (f32[25,8,128]{2,1,0:T(8,128)S(1)}, f32[25,8,128]{2,1,0:T(8,128)S(1)}, u32[]{:S(2)}, u32[]{:S(2)}) collective-permute-start(f32[25,8,128]{2,1,0:T(8,128)S(1)} %get-tuple-element.44), channel_id=1, source_target_pairs={{0,4},{4,0},{8,12},{12,8},{16,20},{20,16},{24,28},{28,24},{1,5},{5... | collective-permute-start | bytes 307208 | tf_op jit(solution)/shard_map/ppermute | solution.py:777
  2.2 4.4 %collective-permute-start.1 = (f32[25,8,128]{2,1,0:T(8,128)S(1)}, f32[25,8,128]{2,1,0:T(8,128)S(1)}, u32[]{:S(2)}, u32[]{:S(2)}) collective-permute-start(f32[25,8,128]{2,1,0:T(8,128)S(1)} %get-tuple-element.45), channel_id=1, source_target_pairs={{4,8},{8,4},{12,16},{16,12},{20,24},{24,20},{5,9},{9,5},{13,17},{1... | collective-permute-start | bytes 307208 | tf_op jit(solution)/shard_map/ppermute | solution.py:777
  6.6 0.1 collective-permute-start.2
  6.7 2.5 %collective-permute-start.3 = (f32[25,8,128]{2,1,0:T(8,128)S(1)}, f32[25,8,128]{2,1,0:T(8,128)S(1)}, u32[]{:S(2)}, u32[]{:S(2)}) collective-permute-start(f32[25,8,128]{2,1,0:T(8,128)S(1)} %get-tuple-element.47), channel_id=1, source_target_pairs={{1,2},{2,1},{5,6},{6,5},{9,10},{10,9},{13,14},{14,13},{17,18},{18,... | collective-permute-start | bytes 307208 | tf_op jit(solution)/shard_map/ppermute | solution.py:777
  9.2 1.9 %shard_map.83 = (f32[2,125,8,128]{3,2,1,0:T(8,128)S(1)}, f32[2,125,8,128]{3,2,1,0:T(8,128)S(1)}, f32[2,8,8,128]{3,2,1,0:T(8,128)S(1)}, f32[35,8,128]{2,1,0:T(8,128)S(1)}, f32[35,8,128]{2,1,0:T(8,128)S(1)}) custom-call(f32[5,5]{1,0:T(8,128)S(1)} %get-tuple-element.39.basis_in, f32[1,5]{1,0:T(1,128)S(1)} %get-tuple-element.40.lam_in, ...), custom_call_target="tpu_custom_call" | custom-call | tf_op jit(solution)/shard_map/pallas_call | solution.py:808
  11.2 0.0 collective-permute-done.1.fx1
  11.2 1.5 %collective-permute-done.3.fy1 = f32[25,8,128]{2,1,0:T(8,128)S(1)} collective-permute-done((f32[25,8,128]{2,1,0:T(8,128)S(1)}, f32[25,8,128]{2,1,0:T(8,128)S(1)}, u32[]{:S(2)}, u32[]{:S(2)}) %collective-permute-start.3) | collective-permute-done | bytes 102432 | tf_op jit(solution)/shard_map/ppermute | solution.py:777
  12.7 1.8 %shard_map.84 = (f32[2,125,8,128]{3,2,1,0:T(8,128)S(1)}, f32[2,8,8,128]{3,2,1,0:T(8,128)S(1)}, f32[2,4,8,128]{3,2,1,0:T(8,128)S(1)}, f32[2,4,8,128]{3,2,1,0:T(8,...) custom-call(f32[35,8,128]{2,1,0:T(8,128)S(1)} %get-tuple-element.43., ...), custom_call_target="tpu_custom_call" | custom-call | tf_op jit(solution)/shard_map/pallas_call | solution.py:815
  14.4 0.0 copy-start.1
  14.4 0.1 collective-permute-start.4
  14.5 2.3 %collective-permute-start.5 = (f32[16,8,128]{2,1,0:T(8,128)S(1)}, f32[16,8,128]{2,1,0:T(8,128)S(1)}, u32[]{:S(2)}, u32[]{:S(2)}) collective-permute-start(f32[16,8,128]{2,1,0:T(8,128)S(1)} %get-tuple-element.52), channel_id=1, source_target_pairs={{4,8},{8,4},{12,16},{16,12},{20,24},{24,20},{5,9},{9,5},{13,17},{1... | collective-permute-start | bytes 196616 | tf_op jit(solution)/shard_map/ppermute | solution.py:777
  16.8 1.9 %collective-permute-done.4.rx0 = f32[16,8,128]{2,1,0:T(8,128)S(1)} collective-permute-done((f32[16,8,128]{2,1,0:T(8,128)S(1)}, f32[16,8,128]{2,1,0:T(8,128)S(1)}, u32[]{:S(2)}, u32[]{:S(2)}) %collective-permute-start.4) | collective-permute-done | bytes 65568 | tf_op jit(solution)/shard_map/ppermute | solution.py:777
  18.8 2.8 %collective-permute-done.5.rx1 = f32[16,8,128]{2,1,0:T(8,128)S(1)} collective-permute-done((f32[16,8,128]{2,1,0:T(8,128)S(1)}, f32[16,8,128]{2,1,0:T(8,128)S(1)}, u32[]{:S(2)}, u32[]{:S(2)}) %collective-permute-start.5) | collective-permute-done | bytes 65568 | tf_op jit(solution)/shard_map/ppermute | solution.py:777
  21.6 0.1 collective-permute-start.6
  21.7 1.9 %collective-permute-start.7 = (f32[24,8,128]{2,1,0:T(8,128)S(1)}, f32[24,8,128]{2,1,0:T(8,128)S(1)}, u32[]{:S(2)}, u32[]{:S(2)}) collective-permute-start(f32[24,8,128]{2,1,0:T(8,128)S(1)} %get-tuple-element.57), channel_id=1, source_target_pairs={{1,2},{2,1},{5,6},{6,5},{9,10},{10,9},{13,14},{14,13},{17,18},{18,... | collective-permute-start | bytes 294920 | tf_op jit(solution)/shard_map/ppermute | solution.py:777
  23.6 0.0 collective-permute-done.6.ry0
  23.7 4.0 %collective-permute-done.7.ry1 = f32[24,8,128]{2,1,0:T(8,128)S(1)} collective-permute-done((f32[24,8,128]{2,1,0:T(8,128)S(1)}, f32[24,8,128]{2,1,0:T(8,128)S(1)}, u32[]{:S(2)}, u32[]{:S(2)}) %collective-permute-start.7) | collective-permute-done | bytes 98336 | tf_op jit(solution)/shard_map/ppermute | solution.py:777
  27.7 3.1 %shard_map.86 = (f32[64,8,128]{2,1,0:T(8,128)S(1)}, f32[24,8,128]{2,1,0:T(8,128)S(1)}, f32[24,8,128]{2,1,0:T(8,128)S(1)}) custom-call(f32[24,8,128]{2,1,0:T(8,128)S(1)} %collective-permute-done.6.ry0, f32[24,8,128]{2,1,0:T(8,128)S(1)} %collective-permute-done.7.ry1, f32[2,8,8,128]{3,2,1,0:T(8,128)S(1)} %get-tuple-element.58.c1, ...), custom_call_target="tpu_custom_call" | custom-call | tf_op jit(solution)/shard_map/pallas_call | solution.py:848
  30.7 0.1 collective-permute-start.8
  30.8 2.1 %collective-permute-start.12 = (f32[25,8,128]{2,1,0:T(8,128)S(1)}, f32[25,8,128]{2,1,0:T(8,128)S(1)}, u32[]{:S(2)}, u32[]{:S(2)}) collective-permute-start(f32[25,8,128]{2,1,0:T(8,128)S(1)} %get-tuple-element.69), channel_id=1, source_target_pairs={{0,4},{4,0},{8,12},{12,8},{16,20},{20,16},{24,28},{28,24},{1,5},{5... | collective-permute-start | bytes 307208 | tf_op jit(solution)/shard_map/ppermute | solution.py:777
  32.9 1.9 %collective-permute-start.9 = (f32[24,8,128]{2,1,0:T(8,128)S(1)}, f32[24,8,128]{2,1,0:T(8,128)S(1)}, u32[]{:S(2)}, u32[]{:S(2)}) collective-permute-start(f32[24,8,128]{2,1,0:T(8,128)S(1)} %get-tuple-element.63), channel_id=1, source_target_pairs={{1,2},{2,1},{5,6},{6,5},{9,10},{10,9},{13,14},{14,13},{17,18},{18,... | collective-permute-start | bytes 294920 | tf_op jit(solution)/shard_map/ppermute | solution.py:777
  34.8 1.9 %collective-permute-start.13 = (f32[25,8,128]{2,1,0:T(8,128)S(1)}, f32[25,8,128]{2,1,0:T(8,128)S(1)}, u32[]{:S(2)}, u32[]{:S(2)}) collective-permute-start(f32[25,8,128]{2,1,0:T(8,128)S(1)} %get-tuple-element.70), channel_id=1, source_target_pairs={{4,8},{8,4},{12,16},{16,12},{20,24},{24,20},{5,9},{9,5},{13,17},{1... | collective-permute-start | bytes 307208 | tf_op jit(solution)/shard_map/ppermute | solution.py:777
  36.7 0.1 collective-permute-start.14
  36.8 3.6 %collective-permute-start.15 = (f32[25,8,128]{2,1,0:T(8,128)S(1)}, f32[25,8,128]{2,1,0:T(8,128)S(1)}, u32[]{:S(2)}, u32[]{:S(2)}) collective-permute-start(f32[25,8,128]{2,1,0:T(8,128)S(1)} %get-tuple-element.72), channel_id=1, source_target_pairs={{1,2},{2,1},{5,6},{6,5},{9,10},{10,9},{13,14},{14,13},{17,18},{18,... | collective-permute-start | bytes 307208 | tf_op jit(solution)/shard_map/ppermute | solution.py:777
  40.5 0.0 collective-permute-done.9.r1
  40.5 1.7 %collective-permute-start.10 = (f32[16,8,128]{2,1,0:T(8,128)S(1)}, f32[16,8,128]{2,1,0:T(8,128)S(1)}, u32[]{:S(2)}, u32[]{:S(2)}) collective-permute-start(f32[16,8,128]{2,1,0:T(8,128)S(1)} %get-tuple-element.65), channel_id=1, source_target_pairs={{0,4},{4,0},{8,12},{12,8},{16,20},{20,16},{24,28},{28,24},{1,5},{5... | collective-permute-start | bytes 196616 | tf_op jit(solution)/shard_map/ppermute | solution.py:777
  42.2 0.0 collective-permute-done.12.rx0
  42.2 2.9 %collective-permute-start.11 = (f32[16,8,128]{2,1,0:T(8,128)S(1)}, f32[16,8,128]{2,1,0:T(8,128)S(1)}, u32[]{:S(2)}, u32[]{:S(2)}) collective-permute-start(f32[16,8,128]{2,1,0:T(8,128)S(1)} %get-tuple-element.66), channel_id=1, source_target_pairs={{4,8},{8,4},{12,16},{16,12},{20,24},{24,20},{5,9},{9,5},{13,17},{1... | collective-permute-start | bytes 196616 | tf_op jit(solution)/shard_map/ppermute | solution.py:777
  45.2 1.3 %shard_map.88.modal = f32[2,125,8,128]{3,2,1,0:T(8,128)S(1)} custom-call(f32[35,8,128]{2,1,0:T(8,128)S(1)} %get-tuple-element.43.basis, f32[2,125,8,128]{3,2,1,0:T(8,128)S(1)} %get-tuple-element.67.u1, f32[2,125,8,128]{3,2,1,0:T(8,128)S(1)} %get-tuple-element.68.rhs, f32[25,8,128]{2,1,0:T(8,128)S(1)} %collective-permute-done.12.rx0, ...), custom_call_target="tpu_custom_call" | custom-call | tf_op jit(solution)/shard_map/pallas_call | solution.py:853
  46.5 2.7 %collective-permute-done.11.r1 = f32[16,8,128]{2,1,0:T(8,128)S(1)} collective-permute-done((f32[16,8,128]{2,1,0:T(8,128)S(1)}, f32[16,8,128]{2,1,0:T(8,128)S(1)}, u32[]{:S(2)}, u32[]{:S(2)}) %collective-permute-start.11) | collective-permute-done | bytes 65568 | tf_op jit(solution)/shard_map/ppermute | solution.py:777
  49.3 2.6 %shard_map.89 = f32[4,125,4,128]{3,2,1,0:T(4,128)} custom-call(f32[35,8,128]{2,1,0:T(8,128)S(1)} %get-tuple-element.43.basis, f32[64,8,128]{2,1,0:T(8,128)S(1)} %get-tuple-element.64.s, f32[16,8,128]{2,1,0:T(8,128)S(1)} %collective-permute-done.10.r0, f32[16,8,128]{2,1,0:T(8,128)S(1)} %collective-permute-done.11.r1, ...), custom_call_target="tpu_custom_call" | custom-call | tf_op jit(solution)/shard_map/pallas_call | solution.py:855
  (16 shorter events, 0.1 us)
Async XLA Ops:
  0.0 9.2 %copy-start = (f32[4,5,5,5,2,2,128]{6,5,4,3,2,1,0:T(2,128)S(1)}, f32[4,5,5,5,2,2,128]{6,5,4,3,2,1,0:T(2,128)}, u32[]{:S(2)}) copy-start(f32[4,5,5,5,2,2,128]{6,5,4,3,2,1,0:T(2,128)} %param.8) | copy-start | bytes 3072004
  1.6 9.6 %collective-permute-start = (f32[25,8,128]{2,1,0:T(8,128)S(1)}, f32[25,8,128]{2,1,0:T(8,128)S(1)}, u32[]{:S(2)}, u32[]{:S(2)}) collective-permute-start(f32[25,8,128]{2,1,0:T(8,128)S(1)} %get-tuple-element.44), channel_id=1, source_target_pairs={{0,4},{4,0},{8,12},{12,8},{16,20},{20,16},{24,28},{28,24},{1,5},{5... | collective-permute-start | bytes 307208 | tf_op jit(solution)/shard_map/ppermute | solution.py:777
  2.2 9.0 %collective-permute-start.1 = (f32[25,8,128]{2,1,0:T(8,128)S(1)}, f32[25,8,128]{2,1,0:T(8,128)S(1)}, u32[]{:S(2)}, u32[]{:S(2)}) collective-permute-start(f32[25,8,128]{2,1,0:T(8,128)S(1)} %get-tuple-element.45), channel_id=1, source_target_pairs={{4,8},{8,4},{12,16},{16,12},{20,24},{24,20},{5,9},{9,5},{13,17},{1... | collective-permute-start | bytes 307208 | tf_op jit(solution)/shard_map/ppermute | solution.py:777
  6.6 4.6 %collective-permute-start.2 = (f32[25,8,128]{2,1,0:T(8,128)S(1)}, f32[25,8,128]{2,1,0:T(8,128)S(1)}, u32[]{:S(2)}, u32[]{:S(2)}) collective-permute-start(f32[25,8,128]{2,1,0:T(8,128)S(1)} %get-tuple-element.46), channel_id=1, source_target_pairs={{0,1},{1,0},{2,3},{3,2},{4,5},{5,4},{6,7},{7,6},{8,9},{9,8},{10,11... | collective-permute-start | bytes 307208 | tf_op jit(solution)/shard_map/ppermute | solution.py:777
  6.7 6.0 %collective-permute-start.3 = (f32[25,8,128]{2,1,0:T(8,128)S(1)}, f32[25,8,128]{2,1,0:T(8,128)S(1)}, u32[]{:S(2)}, u32[]{:S(2)}) collective-permute-start(f32[25,8,128]{2,1,0:T(8,128)S(1)} %get-tuple-element.47), channel_id=1, source_target_pairs={{1,2},{2,1},{5,6},{6,5},{9,10},{10,9},{13,14},{14,13},{17,18},{18,... | collective-permute-start | bytes 307208 | tf_op jit(solution)/shard_map/ppermute | solution.py:777
  12.6 15.0 %copy-start.3 = (s32[512,8]{0,1:T(8,128)S(1)}, s32[512,8]{0,1:T(8,128)}, u32[]{:S(2)}) copy-start(s32[512,8]{0,1:T(8,128)} %param.15) | copy-start | bytes 49156
  14.4 13.2 %copy-start.1 = (f32[256,256]{1,0:T(8,128)S(1)}, f32[256,256]{1,0:T(8,128)}, u32[]{:S(2)}) copy-start(f32[256,256]{1,0:T(8,128)} %inverse.1) | copy-start | bytes 786436
  14.4 4.3 %collective-permute-start.4 = (f32[16,8,128]{2,1,0:T(8,128)S(1)}, f32[16,8,128]{2,1,0:T(8,128)S(1)}, u32[]{:S(2)}, u32[]{:S(2)}) collective-permute-start(f32[16,8,128]{2,1,0:T(8,128)S(1)} %get-tuple-element.51), channel_id=1, source_target_pairs={{0,4},{4,0},{8,12},{12,8},{16,20},{20,16},{24,28},{28,24},{1,5},{5... | collective-permute-start | bytes 196616 | tf_op jit(solution)/shard_map/ppermute | solution.py:777
  14.5 7.1 %collective-permute-start.5 = (f32[16,8,128]{2,1,0:T(8,128)S(1)}, f32[16,8,128]{2,1,0:T(8,128)S(1)}, u32[]{:S(2)}, u32[]{:S(2)}) collective-permute-start(f32[16,8,128]{2,1,0:T(8,128)S(1)} %get-tuple-element.52), channel_id=1, source_target_pairs={{4,8},{8,4},{12,16},{16,12},{20,24},{24,20},{5,9},{9,5},{13,17},{1... | collective-permute-start | bytes 196616 | tf_op jit(solution)/shard_map/ppermute | solution.py:777
  21.6 6.1 %copy-start.2 = (s32[512,8]{0,1:T(8,128)S(1)}, s32[512,8]{0,1:T(8,128)}, u32[]{:S(2)}) copy-start(s32[512,8]{0,1:T(8,128)} %param.14) | copy-start | bytes 49156
  21.6 2.0 %collective-permute-start.6 = (f32[24,8,128]{2,1,0:T(8,128)S(1)}, f32[24,8,128]{2,1,0:T(8,128)S(1)}, u32[]{:S(2)}, u32[]{:S(2)}) collective-permute-start(f32[24,8,128]{2,1,0:T(8,128)S(1)} %get-tuple-element.56), channel_id=1, source_target_pairs={{0,1},{1,0},{2,3},{3,2},{4,5},{5,4},{6,7},{7,6},{8,9},{9,8},{10,11... | collective-permute-start | bytes 294920 | tf_op jit(solution)/shard_map/ppermute | solution.py:777
  21.7 5.9 %collective-permute-start.7 = (f32[24,8,128]{2,1,0:T(8,128)S(1)}, f32[24,8,128]{2,1,0:T(8,128)S(1)}, u32[]{:S(2)}, u32[]{:S(2)}) collective-permute-start(f32[24,8,128]{2,1,0:T(8,128)S(1)} %get-tuple-element.57), channel_id=1, source_target_pairs={{1,2},{2,1},{5,6},{6,5},{9,10},{10,9},{13,14},{14,13},{17,18},{18,... | collective-permute-start | bytes 294920 | tf_op jit(solution)/shard_map/ppermute | solution.py:777
  30.7 6.1 %collective-permute-start.8 = (f32[24,8,128]{2,1,0:T(8,128)S(1)}, f32[24,8,128]{2,1,0:T(8,128)S(1)}, u32[]{:S(2)}, u32[]{:S(2)}) collective-permute-start(f32[24,8,128]{2,1,0:T(8,128)S(1)} %get-tuple-element.62), channel_id=1, source_target_pairs={{0,1},{1,0},{2,3},{3,2},{4,5},{5,4},{6,7},{7,6},{8,9},{9,8},{10,11... | collective-permute-start | bytes 294920 | tf_op jit(solution)/shard_map/ppermute | solution.py:777
  30.8 11.4 %collective-permute-start.12 = (f32[25,8,128]{2,1,0:T(8,128)S(1)}, f32[25,8,128]{2,1,0:T(8,128)S(1)}, u32[]{:S(2)}, u32[]{:S(2)}) collective-permute-start(f32[25,8,128]{2,1,0:T(8,128)S(1)} %get-tuple-element.69), channel_id=1, source_target_pairs={{0,4},{4,0},{8,12},{12,8},{16,20},{20,16},{24,28},{28,24},{1,5},{5... | collective-permute-start | bytes 307208 | tf_op jit(solution)/shard_map/ppermute | solution.py:777
  32.9 7.6 %collective-permute-start.9 = (f32[24,8,128]{2,1,0:T(8,128)S(1)}, f32[24,8,128]{2,1,0:T(8,128)S(1)}, u32[]{:S(2)}, u32[]{:S(2)}) collective-permute-start(f32[24,8,128]{2,1,0:T(8,128)S(1)} %get-tuple-element.63), channel_id=1, source_target_pairs={{1,2},{2,1},{5,6},{6,5},{9,10},{10,9},{13,14},{14,13},{17,18},{18,... | collective-permute-start | bytes 294920 | tf_op jit(solution)/shard_map/ppermute | solution.py:777
  34.8 10.4 %collective-permute-start.13 = (f32[25,8,128]{2,1,0:T(8,128)S(1)}, f32[25,8,128]{2,1,0:T(8,128)S(1)}, u32[]{:S(2)}, u32[]{:S(2)}) collective-permute-start(f32[25,8,128]{2,1,0:T(8,128)S(1)} %get-tuple-element.70), channel_id=1, source_target_pairs={{4,8},{8,4},{12,16},{16,12},{20,24},{24,20},{5,9},{9,5},{13,17},{1... | collective-permute-start | bytes 307208 | tf_op jit(solution)/shard_map/ppermute | solution.py:777
  36.7 8.5 %collective-permute-start.14 = (f32[25,8,128]{2,1,0:T(8,128)S(1)}, f32[25,8,128]{2,1,0:T(8,128)S(1)}, u32[]{:S(2)}, u32[]{:S(2)}) collective-permute-start(f32[25,8,128]{2,1,0:T(8,128)S(1)} %get-tuple-element.71), channel_id=1, source_target_pairs={{0,1},{1,0},{2,3},{3,2},{4,5},{5,4},{6,7},{7,6},{8,9},{9,8},{10,11... | collective-permute-start | bytes 307208 | tf_op jit(solution)/shard_map/ppermute | solution.py:777
  36.8 8.4 %collective-permute-start.15 = (f32[25,8,128]{2,1,0:T(8,128)S(1)}, f32[25,8,128]{2,1,0:T(8,128)S(1)}, u32[]{:S(2)}, u32[]{:S(2)}) collective-permute-start(f32[25,8,128]{2,1,0:T(8,128)S(1)} %get-tuple-element.72), channel_id=1, source_target_pairs={{1,2},{2,1},{5,6},{6,5},{9,10},{10,9},{13,14},{14,13},{17,18},{18,... | collective-permute-start | bytes 307208 | tf_op jit(solution)/shard_map/ppermute | solution.py:777
  40.5 6.0 %collective-permute-start.10 = (f32[16,8,128]{2,1,0:T(8,128)S(1)}, f32[16,8,128]{2,1,0:T(8,128)S(1)}, u32[]{:S(2)}, u32[]{:S(2)}) collective-permute-start(f32[16,8,128]{2,1,0:T(8,128)S(1)} %get-tuple-element.65), channel_id=1, source_target_pairs={{0,4},{4,0},{8,12},{12,8},{16,20},{20,16},{24,28},{28,24},{1,5},{5... | collective-permute-start | bytes 196616 | tf_op jit(solution)/shard_map/ppermute | solution.py:777
  42.2 7.0 %collective-permute-start.11 = (f32[16,8,128]{2,1,0:T(8,128)S(1)}, f32[16,8,128]{2,1,0:T(8,128)S(1)}, u32[]{:S(2)}, u32[]{:S(2)}) collective-permute-start(f32[16,8,128]{2,1,0:T(8,128)S(1)} %get-tuple-element.66), channel_id=1, source_target_pairs={{4,8},{8,4},{12,16},{16,12},{20,24},{24,20},{5,9},{9,5},{13,17},{1... | collective-permute-start | bytes 196616 | tf_op jit(solution)/shard_map/ppermute | solution.py:777
